TPU v7x, 32 devices: a whole 2x2x4 slice. The times are simulated.
32 devices in a mesh: dp: 8 (over y, x, core), tensor: 4 (over z).
Axes of the slice: x: 2, y: 2, z: 4, core: 2. Of those that a mesh axis runs over, the one named last changes fastest.
Arguments:
- inputs: bfloat16 [32768, 512], P(('dp', 'tensor')), may hold values from -6 to 6
- norm_gain: float32 [512], replicated, may hold values from 0.5 to 1.5
- in_weight: bfloat16 [512, 2, 1024], P(None, None, 'tensor'), may hold values from -0.25 to 0.25
- conv_kernel: float32 [4, 1024], P(None, 'tensor'), may hold values from -3 to 3
- gate_bias: float32 [1024], P('tensor'), may hold values from -9 to -2
- out_weight: bfloat16 [1024, 512], P('tensor'), may hold values from -0.25 to 0.25
- mlp_gain: float32 [512], replicated, may hold values from 0.5 to 1.5
- up_weight: bfloat16 [512, 2048], P(None, 'tensor'), may hold values from -0.25 to 0.25
- down_weight: bfloat16 [2048, 512], P('tensor'), may hold values from -0.1875 to 0.1875
- short_lengths: int32 [16], P('dp'), may hold values from 256 to 1024, as said below
- long_lengths: int32 [8], P('dp'), may hold values from 512 to 2048, as said below
- cotangent: bfloat16 [32768, 512], P(('dp', 'tensor')), may hold values from -6 to 6
Outputs:
- result: bfloat16 [32768, 512], P(('dp', 'tensor'))
- grad_inputs: float32 [32768, 512], P(('dp', 'tensor'))
- grad_norm_gain: float32 [512], replicated
- grad_in_weight: float32 [512, 2, 1024], P(None, None, 'tensor')
- grad_conv_kernel: float32 [4, 1024], P(None, 'tensor')
- grad_gate_bias: float32 [1024], P('tensor')
- grad_out_weight: float32 [1024, 512], P('tensor')
- grad_mlp_gain: float32 [512], replicated
- grad_up_weight: float32 [512, 2048], P(None, 'tensor')
- grad_down_weight: float32 [2048, 512], P('tensor')
Inputs may be any that keep to these rules, and one draw needn't show every extreme that they name: `short_lengths`: the first short sequence of group 0 is full. `long_lengths`: the first long sequence of group 0 is full.
All inputs are finite; a program needn't handle non-finite values.
Results may differ from a plain program's by a relative error of at most 0.0075.
Values may be sent and summed in bfloat16 or wider, within the bound.
A program may use at most 192 MiB of HBM per device.

v0:
```python
import jax
import jax.numpy as jnp
from jax import lax
from jax.sharding import PartitionSpec as P

LSHORT = 1024
LLONG = 2048
SHORTS = 2
LONGS = 1


epsilon = 1e-05
run_length = 16


def normalize(values, gain):
    scale = lax.rsqrt(jnp.mean(values * values, axis=-1, keepdims=True) + epsilon)
    return values * scale * gain


def gain_grad(values, grads):
    scale = lax.rsqrt(jnp.mean(values * values, axis=-1, keepdims=True) + epsilon)
    return jnp.sum(grads * values * scale, axis=0)


def norm_back(values, gain, grads):
    pulled = jax.vjp(normalize, values, gain)[1](grads)
    return pulled[0]


def gelu_exact(values):
    return jax.nn.gelu(values, approximate=False)


def causal_filter(values, kernel):
    width = kernel.shape[0]
    total = values * kernel[0]
    for lag in range(1, width):
        total = total.at[:, lag:].add(values[:, :-lag] * kernel[lag])
    return total


def combine(early, late):
    return (early[0] * late[0], late[0] * early[1] + late[1])


def recurrence(gate, candidate, kernel):
    filtered = causal_filter(candidate, kernel)
    update = jax.nn.sigmoid(gate)
    log_decay = -jax.nn.softplus(gate)
    drive = update * filtered
    sequences, length, channels = gate.shape
    runs = length // run_length
    log_runs = log_decay.reshape(sequences, runs, run_length, channels)
    drive_runs = drive.reshape(sequences, runs, run_length, channels)
    places = jnp.arange(run_length, dtype=jnp.int32)
    lower = (places[:, None] >= places[None, :]).astype(jnp.float32)
    summed_logs = jnp.einsum("ts,nmsc->nmtc", lower, log_runs, precision=lax.Precision.HIGHEST)
    spread = summed_logs[:, :, :, None, :] - summed_logs[:, :, None, :, :]
    factors = jnp.where(lower[:, :, None] > 0.0, jnp.exp(jnp.minimum(spread, 0.0)), 0.0)
    inside = jnp.sum(factors * drive_runs[:, :, None, :, :], axis=3)
    run_decay = jnp.exp(summed_logs[:, :, -1])
    run_ends = inside[:, :, -1]
    product, carried = lax.associative_scan(combine, (run_decay, run_ends), axis=1)
    carry_in = jnp.concatenate(
        [jnp.zeros((sequences, 1, channels), jnp.float32), carried[:, :-1]], axis=1
    )
    states = inside + jnp.exp(summed_logs) * carry_in[:, :, None, :]
    return states.reshape(sequences, length, channels)


def mixer(projected, kernel, bias):
    split = SHORTS * LSHORT
    channels = projected.shape[-1]
    shorter = projected[:split].reshape(SHORTS, LSHORT, 2, channels)
    longer = projected[split:].reshape(LONGS, LLONG, 2, channels)
    first_part = recurrence(shorter[:, :, 0] + bias, shorter[:, :, 1], kernel)
    second_part = recurrence(longer[:, :, 0] + bias, longer[:, :, 1], kernel)
    return jnp.concatenate(
        [first_part.reshape(split, channels), second_part.reshape(LONGS * LLONG, channels)], axis=0
    )


def row_keep(short_lengths, long_lengths):
    short_place = jnp.arange(LSHORT, dtype=jnp.int32)
    long_place = jnp.arange(LLONG, dtype=jnp.int32)
    short_keep = (short_place[None, :] < short_lengths[:, None]).reshape(-1)
    long_keep = (long_place[None, :] < long_lengths[:, None]).reshape(-1)
    return jnp.concatenate([short_keep, long_keep]).astype(jnp.float32)


def per_device(
    inputs,
    norm_gain,
    in_weight,
    conv_kernel,
    gate_bias,
    out_weight,
    mlp_gain,
    up_weight,
    down_weight,
    short_lengths,
    long_lengths,
    cotangent,
):
    own_rows = inputs.shape[0]
    row_start = lax.axis_index("tensor") * own_rows
    channels = in_weight.shape[2]
    inputs_wide = inputs.astype(jnp.float32)
    first_own = normalize(inputs_wide, norm_gain).astype(jnp.bfloat16)
    first_all = lax.all_gather(first_own, "tensor", axis=0, tiled=True)
    projected = jnp.einsum("rd,dch->rch", first_all, in_weight, preferred_element_type=jnp.float32)
    states, pull_mixer = jax.vjp(mixer, projected, conv_kernel, gate_bias)
    hidden = states.astype(jnp.bfloat16)
    mixed_own = lax.psum_scatter(
        jnp.dot(hidden, out_weight, preferred_element_type=jnp.float32),
        "tensor",
        scatter_dimension=0,
        tiled=True,
    )
    middle_own = inputs_wide + mixed_own
    second_all = lax.all_gather(
        normalize(middle_own, mlp_gain).astype(jnp.bfloat16), "tensor", axis=0, tiled=True
    )
    inner = jnp.dot(second_all, up_weight, preferred_element_type=jnp.float32)
    activ_wide, pull_gelu = jax.vjp(gelu_exact, inner)
    activ = activ_wide.astype(jnp.bfloat16)
    branch = lax.psum_scatter(
        jnp.dot(activ, down_weight, preferred_element_type=jnp.float32),
        "tensor",
        scatter_dimension=0,
        tiled=True,
    )
    result = (middle_own + branch).astype(jnp.bfloat16)
    cot_all = lax.all_gather(cotangent, "tensor", axis=0, tiled=True)
    keep = row_keep(short_lengths, long_lengths)
    dout = cot_all * keep[:, None].astype(jnp.bfloat16)
    grad_activ = jnp.dot(dout, down_weight.T, preferred_element_type=jnp.float32)
    grad_inner = pull_gelu(grad_activ)[0].astype(jnp.bfloat16)
    grad_down = jnp.dot(activ.T, dout, preferred_element_type=jnp.float32)
    grad_up = jnp.dot(second_all.T, grad_inner, preferred_element_type=jnp.float32)
    grad_second_own = lax.psum_scatter(
        jnp.dot(grad_inner, up_weight.T, preferred_element_type=jnp.float32),
        "tensor",
        scatter_dimension=0,
        tiled=True,
    )
    keep_own = lax.dynamic_slice_in_dim(keep, row_start, own_rows, 0)
    grad_middle_own = cotangent.astype(jnp.float32) * keep_own[:, None] + norm_back(
        middle_own, mlp_gain, grad_second_own
    )
    grad_mlp_gain = gain_grad(middle_own, grad_second_own)
    grad_mixed = lax.all_gather(grad_middle_own.astype(jnp.bfloat16), "tensor", axis=0, tiled=True)
    grad_out = jnp.dot(hidden.T, grad_mixed, preferred_element_type=jnp.float32)
    grad_states = jnp.dot(grad_mixed, out_weight.T, preferred_element_type=jnp.float32)
    grad_proj_wide, grad_kernel, grad_bias = pull_mixer(grad_states)
    grad_proj = grad_proj_wide.astype(jnp.bfloat16)
    grad_in = jnp.einsum("rd,rch->dch", first_all, grad_proj, preferred_element_type=jnp.float32)
    grad_first_own = lax.psum_scatter(
        jnp.einsum("rch,dch->rd", grad_proj, in_weight, preferred_element_type=jnp.float32),
        "tensor",
        scatter_dimension=0,
        tiled=True,
    )
    grad_inputs = grad_middle_own + norm_back(inputs_wide, norm_gain, grad_first_own)
    grad_norm_gain = gain_grad(inputs_wide, grad_first_own)
    grad_in, grad_out, grad_up, grad_down = lax.psum((grad_in, grad_out, grad_up, grad_down), "dp")
    channel_grads = jnp.concatenate([grad_kernel, grad_bias[None, :]], axis=0)
    kernel_full = jnp.zeros(
        (channel_grads.shape[0], channels * lax.axis_size("tensor")), jnp.float32
    )
    kernel_full = lax.dynamic_update_slice_in_dim(
        kernel_full, channel_grads, lax.axis_index("tensor") * channels, 1
    )
    kernel_sum, norm_sum, mlp_sum = lax.psum(
        (kernel_full, grad_norm_gain, grad_mlp_gain), ("dp", "tensor")
    )
    channel_own = lax.dynamic_slice_in_dim(
        kernel_sum, lax.axis_index("tensor") * channels, channels, 1
    )
    taps_own = channel_own[:-1]
    bias_own = channel_own[-1]
    return (
        result,
        grad_inputs,
        norm_sum,
        grad_in,
        taps_own,
        bias_own,
        grad_out,
        mlp_sum,
        grad_up,
        grad_down,
    )


def solution(mesh):
    placed = (
        P(("dp", "tensor"), None),
        P(),
        P(None, None, "tensor"),
        P(None, "tensor"),
        P("tensor"),
        P("tensor", None),
        P(),
        P(None, "tensor"),
        P("tensor", None),
        P("dp"),
        P("dp"),
        P(("dp", "tensor"), None),
    )
    return jax.shard_map(
        per_device,
        mesh=mesh,
        in_specs=placed,
        out_specs=(
            P(("dp", "tensor"), None),
            P(("dp", "tensor"), None),
            P(),
            P(None, None, "tensor"),
            P(None, "tensor"),
            P("tensor"),
            P("tensor", None),
            P(),
            P(None, "tensor"),
            P("tensor", None),
        ),
        check_vma=False,
    )
```

profile of v0, /device:TPU:0, one launch (start us, length us, event | category | flops | bytes accessed | tf_op | source)
XLA Modules:
  0.0 1414.4 jit_solution(5033182647707537558)
XLA Ops:
  13.3 82.9 %all-gather.5.cloned.1.call-done = bf16[4096,512]{1,0:T(8,128)(2,1)} async-done(((bf16[1024,512]{1,0:T(8,128)(2,1)}), bf16[4096,512]{1,0:T(8,128)(2,1)}) %all-gather.5.cloned.1.call-update) | async-done | bytes 4194320 | tf_op jit(solution)/shard_map/all_gather | solution.py:111
  110.7 7.3 scatter-add.20
  121.2 6.9 scatter-add.21
  128.1 6.4 scatter-add.24
  139.8 12.3 fusion.5
  169.3 6.2 scatter-add.25
  178.8 6.4 scatter-add.26
  185.2 6.0 scatter-add.29
  196.5 12.3 fusion.13
  238.4 5.2 add_convert_fusion.3
  245.0 4.7 fusion.93
  249.7 143.2 %reduce-scatter.5.cloned.1.call-done = f32[1024,512]{1,0:T(8,128)} async-done(((f32[4096,512]{1,0:T(8,128)}), f32[1024,512]{1,0:T(8,128)}) %reduce-scatter.5.cloned.1.call-update) | async-done | bytes 2097168 | tf_op jit(solution)/shard_map/reduce_scatter | solution.py:115
  403.4 76.3 %all-gather.7.cloned.1.call-done = bf16[4096,512]{1,0:T(8,128)(2,1)} async-done(((bf16[1024,512]{1,0:T(8,128)(2,1)}), bf16[4096,512]{1,0:T(8,128)(2,1)}) %all-gather.7.cloned.1.call-update) | async-done | bytes 4194320 | tf_op jit(solution)/shard_map/all_gather | solution.py:122
  479.7 23.0 %multiply_convert_fusion = (bf16[4096,512]{1,0:T(8,128)(2,1)}, f32[4096,512]{1,0:T(8,128)}, f32[4096,512]{1,0:T(8,128)}) fusion(bf16[4096,512]{1,0:T(8,128)(2,1)} %all-gather.7.cloned.1.call-done, bf16[512,512]{1,0:T(8,128)(2,1)S(1)} %copy-done), kind=kOutput, calls=%fused_computation.30 | convolution fusion | flops 2283798528 | bytes 25690112 | tf_op jit(solution)/shard_map/dot_general | solution.py:125
  502.7 57.7 %all-gather.9.cloned.1.call-done = bf16[4096,512]{1,0:T(8,128)(2,1)} async-done(((bf16[1024,512]{1,0:T(8,128)(2,1)}), bf16[4096,512]{1,0:T(8,128)(2,1)}) %all-gather.9.cloned.1.call-update) | async-done | bytes 4194320 | tf_op jit(solution)/shard_map/all_gather | solution.py:135
  560.4 9.8 add_convert_fusion.1
  572.3 5.9 fusion.188
  579.3 7.9 fusion.187
  588.0 133.5 %reduce-scatter.9.cloned.1.call-done = f32[1024,512]{1,0:T(8,128)} async-done(((f32[4096,512]{1,0:T(8,128)}), f32[1024,512]{1,0:T(8,128)}) %reduce-scatter.9.cloned.1.call-update) | async-done | bytes 2097168 | tf_op jit(solution)/shard_map/reduce_scatter | solution.py:142
  724.3 144.7 %reduce-scatter.7.cloned.1.call-done = f32[1024,512]{1,0:T(8,128)} async-done(((f32[4096,512]{1,0:T(8,128)}), f32[1024,512]{1,0:T(8,128)}) %reduce-scatter.7.cloned.1.call-update) | async-done | bytes 2097168 | tf_op jit(solution)/shard_map/reduce_scatter | solution.py:128
  873.4 6.9 fusion.190
  883.8 71.1 %all-gather.11.cloned.1.call-done = bf16[4096,512]{1,0:T(8,128)(2,1)} async-done(((bf16[1024,512]{1,0:T(8,128)(2,1)}), bf16[4096,512]{1,0:T(8,128)(2,1)}) %all-gather.11.cloned.1.call-update) | async-done | bytes 4194320 | tf_op jit(solution)/shard_map/all_gather | solution.py:153
  964.2 4.7 multiply_reduce_fusion.10
  976.8 10.7 pad.640
  997.6 36.0 %fusion.17 = (f32[128,16,256]{2,1,0:T(8,128)S(1)}, f32[128,16,256]{2,1,0:T(8,128)}, f32[128,16,256]{2,1,0:T(8,128)}) fusion(f32[128,16,256]{2,1,0:T(8,128)} %bitcast.209, f32[128,16,256]{2,1,0:T(8,128)S(1)} %bitcast.208, f32[128,16,256]{2,1,0:T(8,128)S(1)} %bitcast.194, pred[16,16]{1,0:T(8,128)(4,1)} %copy.50), kind=kLoop, calls=%fused_computation.23 | loop fusion | flops 124256256 | bytes 12583168 | tf_op jit(solution)/shard_map/transpose(jvp())/reduce_sum | solution.py:59
  1035.2 9.4 add_bitcast_fusion.2
  1068.6 36.1 %fusion.19 = (f32[2,64,16,256]{3,2,1,0:T(8,128)}, f32[2,64,16,256]{3,2,1,0:T(8,128)}, f32[2,64,16,256]{3,2,1,0:T(8,128)S(1)}) fusion(f32[2,64,16,256]{3,2,1,0:T(8,128)} %copy.62, f32[2,64,16,256]{3,2,1,0:T(8,128)} %bitcast.206, f32[2,64,16,256]{3,2,1,0:T(8,128)S(1)} %copy-done.22, pred[16,16]{1,0:T(8,128)(4,1)} %copy.50), kind=kLoop, calls=%fused_computation.25 | loop fusion | flops 124256256 | bytes 12583168 | tf_op jit(solution)/shard_map/transpose(jvp())/reduce_sum | solution.py:59
  1104.7 7.1 fusion.65
  1135.7 9.6 convolution_bitcast_fusion
  1145.4 63.1 %all-reduce.152.cloned.1.call-done = (f32[512,2,256]{2,0,1:T(8,128)}, f32[256,512]{1,0:T(8,128)}, f32[512,512]{1,0:T(8,128)}, f32[512,512]{1,0:T(8,128)}) async-done(((f32[512,2,256]{2,0,1:T(8,128)}, f32[256,512]{1,0:T(8,128)}, f32[512,512]{1,0:T(8,128)}, f32[512,512]{1,0:T(8,128)}), (f32[512,2,256]{2,0,1:T(8,128)}, f32[256,512]{1,0:T(8,128)}, f32[512,512]{1,0:T(8,128)}, ...) | async-done | bytes 3670032 | tf_op jit(solution)/shard_map/psum | solution.py:167
  1211.6 144.1 %reduce-scatter.11.cloned.1.call-done = f32[1024,512]{1,0:T(8,128)} async-done(((f32[4096,512]{1,0:T(8,128)}), f32[1024,512]{1,0:T(8,128)}) %reduce-scatter.11.cloned.1.call-update) | async-done | bytes 2097168 | tf_op jit(solution)/shard_map/reduce_scatter | solution.py:159
  1358.1 41.3 %all-reduce.148 = (f32[512]{0:T(512)}, f32[5,1024]{1,0:T(8,128)S(1)}, f32[512]{0:T(512)}) all-reduce(f32[512]{0:T(512)S(1)} %get-tuple-element.120, f32[5,1024]{1,0:T(8,128)S(1)} %maximum_dynamic-update-slice_fusion, f32[512]{0:T(512)S(1)} %copy-done.169), channel_id=1, replica_groups=mesh['dp'=8,'tensor'=4] {'dp','tensor'}, use_global_device_ids=true, to_apply=%region_19.20 | all-reduce | flops 6144 | bytes 49152 | tf_op jit(solution)/shard_map/psum | solution.py:175
  (721 shorter events, 197.8 us)
Async XLA Ops:
  7.2 472.6 %copy-start = (bf16[512,512]{1,0:T(8,128)(2,1)S(1)}, bf16[512,512]{1,0:T(8,128)(2,1)}, u32[]{:S(2)}) copy-start(bf16[512,512]{1,0:T(8,128)(2,1)} %param.31) | copy-start | bytes 1572868
  7.2 89.0 %copy-start.70 = (bf16[512,2,256]{2,1,0:T(2,128)(2,1)S(1)}, bf16[512,2,256]{2,1,0:T(2,128)(2,1)}, u32[]{:S(2)}) copy-start(bf16[512,2,256]{2,1,0:T(2,128)(2,1)} %param.26) | copy-start | bytes 1572868
  7.2 89.0 %all-gather.5.cloned.1.call-start = ((), (), s32[]{:S(2)}) async-start(), calls=%async_computation.4 | async-start | bytes 5242880 | tf_op jit(solution)/shard_map/all_gather | solution.py:111
  12.6 380.4 %reduce-scatter.5.cloned.1.call-start = ((), (), s32[]{:S(2)}) async-start(), calls=%async_computation.5 | async-start | bytes 10485760 | tf_op jit(solution)/shard_map/reduce_scatter | solution.py:115
  13.3 147.4 %copy-start.161 = (f32[1,256]{1,0:T(1,128)}, f32[1,256]{1,0:T(1,128)S(1)}, u32[]{:S(2)}) copy-start(f32[1,256]{1,0:T(1,128)S(1)} %get-tuple-element.286) | copy-start | bytes 3076
  13.3 152.2 %copy-start.155 = (f32[1,256]{1,0:T(1,128)}, f32[1,256]{1,0:T(1,128)S(1)}, u32[]{:S(2)}) copy-start(f32[1,256]{1,0:T(1,128)S(1)} %get-tuple-element.285) | copy-start | bytes 3076
  13.3 152.6 %copy-start.157 = (f32[1,256]{1,0:T(1,128)}, f32[1,256]{1,0:T(1,128)S(1)}, u32[]{:S(2)}) copy-start(f32[1,256]{1,0:T(1,128)S(1)} %get-tuple-element.287) | copy-start | bytes 3076
  13.3 162.2 %copy-start.159 = (f32[1,256]{1,0:T(1,128)}, f32[1,256]{1,0:T(1,128)S(1)}, u32[]{:S(2)}) copy-start(f32[1,256]{1,0:T(1,128)S(1)} %get-tuple-element.284) | copy-start | bytes 3076
  156.2 61.4 %copy-start.119 = (f32[2,3,256]{2,1,0:T(4,128)}, f32[2,3,256]{2,1,0:T(4,128)S(1)}, u32[]{:S(2)}) copy-start(f32[2,3,256]{2,1,0:T(4,128)S(1)} %slice.646) | copy-start | bytes 18436
  157.5 61.7 %copy-start.101 = (f32[2,7,256]{2,1,0:T(8,128)}, f32[2,7,256]{2,1,0:T(8,128)S(1)}, u32[]{:S(2)}) copy-start(f32[2,7,256]{2,1,0:T(8,128)S(1)} %slice.640) | copy-start | bytes 43012
  158.7 62.6 %copy-start.80 = (f32[2,15,256]{2,1,0:T(8,128)}, f32[2,15,256]{2,1,0:T(8,128)S(1)}, u32[]{:S(2)}) copy-start(f32[2,15,256]{2,1,0:T(8,128)S(1)} %slice.634) | copy-start | bytes 92164
  160.0 66.9 %copy-start.64 = (f32[2,31,256]{2,1,0:T(8,128)}, f32[2,31,256]{2,1,0:T(8,128)S(1)}, u32[]{:S(2)}) copy-start(f32[2,31,256]{2,1,0:T(8,128)S(1)} %slice.628) | copy-start | bytes 190468
  196.4 42.0 %copy-start.18 = (f32[128,256,16]{1,2,0:T(8,128)}, f32[128,256,16]{1,2,0:T(8,128)S(1)}, u32[]{:S(2)}) copy-start(f32[128,256,16]{1,2,0:T(8,128)S(1)} %fusion.52) | copy-start | bytes 6291460
  249.7 230.1 %all-gather.7.cloned.1.call-start = ((), (), s32[]{:S(2)}) async-start(), calls=%async_computation.6 | async-start | bytes 5242880 | tf_op jit(solution)/shard_map/all_gather | solution.py:122
  398.2 162.2 %all-gather.9.cloned.1.call-start = ((), (), s32[]{:S(2)}) async-start(), calls=%async_computation.8 | async-start | bytes 5242880 | tf_op jit(solution)/shard_map/all_gather | solution.py:135
  398.8 322.7 %reduce-scatter.9.cloned.1.call-start = ((), (), s32[]{:S(2)}) async-start(), calls=%async_computation.9 | async-start | bytes 10485760 | tf_op jit(solution)/shard_map/reduce_scatter | solution.py:142
  578.2 290.7 %reduce-scatter.7.cloned.1.call-start = ((), (), s32[]{:S(2)}) async-start(), calls=%async_computation.7 | async-start | bytes 10485760 | tf_op jit(solution)/shard_map/reduce_scatter | solution.py:128
  587.2 134.3 %copy-start.129 = (f32[1024]{0:T(1024)S(1)}, f32[1024]{0:T(1024)}, u32[]{:S(2)}) copy-start(f32[1024]{0:T(1024)} %copy-done.128) | copy-start | bytes 12292
  587.2 134.3 %copy-start.163 = (f32[512]{0:T(512)S(1)}, f32[512]{0:T(512)}, u32[]{:S(2)}) copy-start(f32[512]{0:T(512)} %param.30) | copy-start | bytes 6148
  587.2 367.6 %all-gather.11.cloned.1.call-start = ((), (), s32[]{:S(2)}) async-start(), calls=%async_computation.10 | async-start | bytes 5242880 | tf_op jit(solution)/shard_map/all_gather | solution.py:153
  588.0 136.3 %copy-start.148 = (f32[1024]{0:T(1024)S(1)}, f32[1024]{0:T(1024)}, u32[]{:S(2)}) copy-start(f32[1024]{0:T(1024)} %copy-done.147) | copy-start | bytes 12292
  873.4 335.2 %all-reduce.152.cloned.1.call-start = ((), (), s32[]{:S(2)}) async-start(), calls=%async_computation.12 | async-start | bytes 7340032 | tf_op jit(solution)/shard_map/psum | solution.py:167
  971.2 20.7 %copy-start.93 = (f32[1,63,256]{2,0,1:T(1,128)S(1)}, f32[1,63,256]{2,0,1:T(1,128)}, u32[]{:S(2)}) copy-start(f32[1,63,256]{2,0,1:T(1,128)} %get-tuple-element.201) | copy-start | bytes 193540
  1068.5 36.1 %copy-start.54 = (f32[2,64,1,256]{3,2,1,0:T(1,128)S(1)}, f32[2,64,1,256]{3,2,1,0:T(1,128)}, u32[]{:S(2)}) copy-start(f32[2,64,1,256]{3,2,1,0:T(1,128)} %copy-done.53) | copy-start | bytes 393220
  1068.5 36.1 %copy-start.16 = (f32[2048,256]{1,0:T(8,128)S(1)}, f32[2048,256]{1,0:T(8,128)}, u32[]{:S(2)}) copy-start(f32[2048,256]{1,0:T(8,128)} %get-tuple-element.174) | copy-start | bytes 6291460
  1068.5 36.1 %copy-start.50 = (f32[2,64,256]{2,1,0:T(8,128)S(1)}, f32[2,64,256]{2,1,0:T(8,128)}, u32[]{:S(2)}) copy-start(f32[2,64,256]{2,1,0:T(8,128)} %copy-done.49) | copy-start | bytes 393220
  1134.7 220.9 %reduce-scatter.11.cloned.1.call-start = ((), (), s32[]{:S(2)}) async-start(), calls=%async_computation.11 | async-start | bytes 10485760 | tf_op jit(solution)/shard_map/reduce_scatter | solution.py:159
  1145.3 210.3 %copy-start.17 = (bf16[1024,512]{1,0:T(8,128)(2,1)S(1)}, bf16[1024,512]{1,0:T(8,128)(2,1)}, u32[]{:S(2)}) copy-start(bf16[1024,512]{1,0:T(8,128)(2,1)} %param.24) | copy-start | bytes 3145732
  1145.3 210.3 %copy-start.127 = (f32[1024]{0:T(1024)S(1)}, f32[1024]{0:T(1024)}, u32[]{:S(2)}) copy-start(f32[1024]{0:T(1024)} %copy-done.126) | copy-start | bytes 12292
  1145.4 210.3 %copy-start.164 = (f32[512]{0:T(512)S(1)}, f32[512]{0:T(512)}, u32[]{:S(2)}) copy-start(f32[512]{0:T(512)} %param.25) | copy-start | bytes 6148
  1211.6 146.5 %copy-start.169 = (f32[512]{0:T(512)S(1)}, f32[512]{0:T(512)}, u32[]{:S(2)}) copy-start(f32[512]{0:T(512)} %get-tuple-element.118) | copy-start | bytes 6148
  1211.6 189.1 %copy-start.140 = (f32[1024]{0:T(1024)S(1)}, f32[1024]{0:T(1024)}, u32[]{:S(2)}) copy-start(f32[1024]{0:T(1024)} %copy-done.139) | copy-start | bytes 12292
  (158 other events, 585.7 us)
Sparse Core Ops, SparseCore 0:
  12.7 83.4 all-gather.4
  249.8 143.0 reduce-scatter.4
  398.4 81.3 all-gather.6
  481.2 79.2 all-gather.8
  578.4 143.0 reduce-scatter.8
  723.7 145.2 reduce-scatter.6
  873.5 81.3 all-gather.10
  1134.8 73.6 all-reduce.151
  1210.9 144.6 reduce-scatter.10
where the time goes:
time: 1420 us; the launch traced here: 1410 us
  waiting for transfers between devices  917 us (65%)
  other arithmetic  212 us (15%)
  local copies, waits for them, and re-layouts  133 us (9%)
  matrix products  92.8 us (7%)
  blocking collectives  41.3 us (3%)
  between operations  17.8 us (1%)
    reduce_scatter x1, waiting for transfers between devices, per_device(): lax.psum_scatter(jnp.dot(activ, down_weight, preferred_element_type=jnp.f...  145 us
    reduce_scatter x1, waiting for transfers between devices, per_device(): lax.psum_scatter(jnp.einsum('rch,dch->rd', grad_proj, in_weight, preferre...  144 us
    reduce_scatter x1, waiting for transfers between devices, per_device(): lax.psum_scatter(jnp.dot(hidden, out_weight, preferred_element_type=jnp.f...  143 us
    reduce_scatter x1, waiting for transfers between devices, per_device(): lax.psum_scatter(jnp.dot(grad_inner, up_weight.T, preferred_element_type=...  134 us
    all_gather x1, waiting for transfers between devices, per_device(): first_all = lax.all_gather(first_own, 'tensor', axis=0, tiled=True)  82.9 us
    all_gather x1, waiting for transfers between devices, per_device(): lax.all_gather(normalize(middle_own, mlp_gain).astype(jnp.bfloat16), 'ten...  76.3 us
    reduce_sum x2, other arithmetic, recurrence(): spread = summed_logs[:, :, :, None, :] - summed_logs[:, :, None, :, :]  72.1 us
    all_gather x1, waiting for transfers between devices, per_device(): lax.all_gather(grad_middle_own.astype(jnp.bfloat16), 'tensor', axis=0, ti...  71.1 us
  transfers between devices with their start and end apart: 9, of which 9 were waited for; matrix products, arithmetic and copies ran while one was open for 4% of the time, Pallas kernels for 0%

commit v1 on v0

v1 whole, which is shorter than its diff:
```python
import functools

import jax
import jax.numpy as jnp
import numpy as np
from jax import lax
from jax.experimental import pallas as pl
from jax.experimental.pallas import tpu as pltpu
from jax.sharding import PartitionSpec as P

LSHORT = 1024
LLONG = 2048
SEGS = 8
EPS = 1e-05
CHUNK = 256
F32 = jnp.float32
BF16 = jnp.bfloat16
MESH = pl.DeviceIdType.MESH


def dot(a, b):
    return jnp.dot(a, b, preferred_element_type=F32)


def dot_t(a, b):
    return lax.dot_general(a, b, (((1,), (1,)), ((), ())), preferred_element_type=F32)


def scale_of(v):
    return lax.rsqrt(jnp.mean(v * v, axis=-1, keepdims=True) + EPS)


def sigmoid(v):
    return 1.0 / (1.0 + jnp.exp(-v))


def block_kernel(
    dims,
    lim_ref,
    x_ref,
    halo_ref,
    cot_ref,
    g1_ref,
    g2_ref,
    w_ref,
    conv_ref,
    bias_ref,
    res_ref,
    gx_ref,
    grad_ref,
    gains_ref,
    chan_ref,
    cand,
    upd,
    filt,
    st,
    dst,
    lhs,
    first_t,
    second_t,
    dout,
    dout_t,
    dmix_t,
    bufa,
    mid,
    bufc,
    act,
    din,
    ends,
    bends,
    fsend,
    frecv,
    bsend,
    brecv,
    sems,
):
    rows, d, blocks, ch, ff = dims
    steps = rows // SEGS
    t = lax.axis_index("tensor")
    even = lax.rem(t, 2) == 0
    partner = t + 1 - 2 * lax.rem(t, 2)
    nchunk = rows // CHUNK
    o_in, o_out, o_up, o_down = 0, d, d + ch, d + ch + ff

    barrier = pltpu.get_barrier_semaphore()
    pl.semaphore_signal(barrier, inc=1, device_id={"tensor": partner}, device_id_type=MESH)
    pl.semaphore_wait(barrier, 1)

    def norm_rows(r, _):
        at = pl.multiple_of(r * CHUNK, CHUNK)
        xv = x_ref[pl.ds(at, CHUNK), :].astype(F32)
        fv = xv * scale_of(xv) * g1_ref[...]
        lhs[pl.ds(at, CHUNK), :] = fv.astype(BF16)
        first_t[:, pl.ds(at, CHUNK)] = fv.T.astype(BF16)
        place = at + lax.broadcasted_iota(jnp.int32, (CHUNK, d), 0)
        pos = lax.rem(place, SEGS) * steps + place // SEGS
        dv = jnp.where(pos < lim_ref[0], cot_ref[pl.ds(at, CHUNK), :].astype(F32), 0.0)
        dout[pl.ds(at, CHUNK), :] = dv.astype(BF16)
        dout_t[:, pl.ds(at, CHUNK)] = dv.T.astype(BF16)
        return 0

    lax.fori_loop(0, nchunk, norm_rows, 0)
    hv = halo_ref[...].astype(F32)
    lhs[pl.ds(rows, 16), :] = (hv * scale_of(hv) * g1_ref[...]).astype(BF16)

    seg_id = lax.broadcasted_iota(jnp.int32, (SEGS, ch), 0)
    has_prev = jnp.where(t == 3, 1.0, 0.0).astype(F32)
    has_next = jnp.where(t == 2, 1.0, 0.0).astype(F32)

    def forward_block(b, _):
        def project(r, _):
            at = pl.multiple_of(r * CHUNK, CHUNK)
            p = dot(lhs[pl.ds(at, CHUNK), :], w_ref[b, pl.ds(o_in, d), :])
            bufa[pl.ds(at, CHUNK), :ch] = p[:, :ch]
            cand[b, pl.ds(at + 3 * SEGS, CHUNK), :] = p[:, ch:]
            return 0

        lax.fori_loop(0, nchunk, project, 0)
        ph = dot(lhs[pl.ds(rows, 16), :], w_ref[b, pl.ds(o_in, d), ch:])
        for back in range(3):
            last = cand[b, pl.ds((steps + back) * SEGS, SEGS), :]
            rolled = pltpu.roll(last, 1, 0)
            edge = ph[13 + back : 14 + back, :] * has_prev
            cand[b, pl.ds(back * SEGS, SEGS), :] = jnp.where(seg_id == 0, edge, rolled)
        k = [jnp.broadcast_to(conv_ref[b, pl.ds(i, 1), :], (SEGS, ch)) for i in range(4)]
        bias = jnp.broadcast_to(bias_ref[b], (SEGS, ch))

        def step4(j, carry):
            s, p = carry
            for q in range(4):
                at = pl.multiple_of((j * 4 + q) * SEGS, SEGS)
                u = sigmoid(bufa[pl.ds(at, SEGS), :ch] + bias)
                f = k[0] * cand[b, pl.ds(at + 3 * SEGS, SEGS), :]
                for lag in range(1, 4):
                    f = f + k[lag] * cand[b, pl.ds(at + (3 - lag) * SEGS, SEGS), :]
                upd[b, pl.ds(at, SEGS), :] = u
                filt[b, pl.ds(at, SEGS), :] = f
                a = 1.0 - u
                s = a * s + u * f
                p = a * p
            return s, p

        s, p = lax.fori_loop(
            0, steps // 4, step4, (jnp.zeros((SEGS, ch), F32), jnp.ones((SEGS, ch), F32))
        )
        ends[0, b] = s
        ends[1, b] = p
        return 0

    lax.fori_loop(0, blocks, forward_block, 0)

    def forward_chain(start):
        run = start
        for seg in range(SEGS):
            st[:, pl.ds(seg, 1), :] = run
            run = ends[0, :, pl.ds(seg, 1), :] + ends[1, :, pl.ds(seg, 1), :] * run
        return run

    final = forward_chain(jnp.zeros((blocks, 1, ch), F32))
    fsend[...] = jnp.broadcast_to(final, (blocks, 8, ch))
    fcopy = pltpu.make_async_remote_copy(
        src_ref=fsend,
        dst_ref=frecv,
        send_sem=sems.at[0],
        recv_sem=sems.at[1],
        device_id={"tensor": partner},
        device_id_type=MESH,
    )

    fcopy.start()
    fcopy.wait()
    forward_chain(frecv[:, pl.ds(0, 1), :] * has_prev)

    def forward_fix(b, _):
        def step8(j, s):
            for q in range(8):
                at = pl.multiple_of((j * 8 + q) * SEGS, SEGS)
                u = upd[b, pl.ds(at, SEGS), :]
                s = (1.0 - u) * s + u * filt[b, pl.ds(at, SEGS), :]
                st[b, pl.ds(at + SEGS, SEGS), :] = s
            return s

        lax.fori_loop(0, steps // 8, step8, st[b, pl.ds(0, SEGS), :])
        return 0

    lax.fori_loop(0, blocks, forward_fix, 0)

    def second_rows(r, _):
        at = pl.multiple_of(r * CHUNK, CHUNK)
        m = x_ref[pl.ds(at, CHUNK), :].astype(F32)
        for b in range(blocks):
            m = m + dot(st[b, pl.ds(at + SEGS, CHUNK), :].astype(BF16), w_ref[b, pl.ds(o_out, ch), :])
        mid[pl.ds(at, CHUNK), :] = m
        sv = m * scale_of(m) * g2_ref[...]
        lhs[pl.ds(at, CHUNK), :] = sv.astype(BF16)
        second_t[:, pl.ds(at, CHUNK)] = sv.T.astype(BF16)
        bufa[pl.ds(at, CHUNK), :] = m
        bufc[pl.ds(at, CHUNK), :] = jnp.zeros((CHUNK, d), F32)
        return 0

    lax.fori_loop(0, nchunk, second_rows, 0)

    def ff_block(b, _):
        def ff_rows(r, _):
            at = pl.multiple_of(r * CHUNK, CHUNK)
            wu = w_ref[b, pl.ds(o_up, ff), :]
            wd = w_ref[b, pl.ds(o_down, ff), :]
            inner = dot(lhs[pl.ds(at, CHUNK), :], wu)
            da = dot_t(dout[pl.ds(at, CHUNK), :], wd)
            cdf = 0.5 + 0.5 * lax.erf(inner * np.float32(np.sqrt(0.5)))
            pdf = jnp.exp(inner * inner * -0.5) * np.float32(1.0 / np.sqrt(2.0 * np.pi))
            av = (inner * cdf).astype(BF16)
            dv = (da * (cdf + inner * pdf)).astype(BF16)
            act[pl.ds(at, CHUNK), :] = av
            din[pl.ds(at, CHUNK), :] = dv
            bufa[pl.ds(at, CHUNK), :] += dot(av, wd)
            bufc[pl.ds(at, CHUNK), :] += dot_t(dv, wu)
            return 0

        lax.fori_loop(0, nchunk, ff_rows, 0)

        def ff_grads(r, _):
            at = pl.multiple_of(r * CHUNK, CHUNK)
            grad_ref[b, pl.ds(o_up + at, CHUNK), :] = dot(second_t[pl.ds(at, CHUNK), :], din[...]).astype(BF16)
            grad_ref[b, pl.ds(o_down + at, CHUNK), :] = dot(dout_t[pl.ds(at, CHUNK), :], act[...]).astype(BF16)
            return 0

        lax.fori_loop(0, d // CHUNK, ff_grads, 0)
        return 0

    lax.fori_loop(0, blocks, ff_block, 0)

    def second_back(r, gain):
        at = pl.multiple_of(r * CHUNK, CHUNK)
        res_ref[pl.ds(at, CHUNK), :] = bufa[pl.ds(at, CHUNK), :].astype(BF16)
        m = mid[pl.ds(at, CHUNK), :]
        s = scale_of(m)
        dn = bufc[pl.ds(at, CHUNK), :]
        gain = gain + jnp.sum(dn * m * s, axis=0, keepdims=True)
        gd = dn * g2_ref[...]
        dm = dout[pl.ds(at, CHUNK), :].astype(F32) + s * gd - m * (s * s * s * jnp.mean(gd * m, axis=-1, keepdims=True))
        gx_ref[pl.ds(at, CHUNK), :] = dm
        lhs[pl.ds(at, CHUNK), :] = dm.astype(BF16)
        dmix_t[:, pl.ds(at, CHUNK)] = dm.T.astype(BF16)
        bufc[pl.ds(at, CHUNK), :] = jnp.zeros((CHUNK, d), F32)
        return gain

    gains_ref[pl.ds(1, 1), :] = lax.fori_loop(0, nchunk, second_back, jnp.zeros((1, d), F32))

    def backward_block(b, _):
        def project(r, _):
            at = pl.multiple_of(r * CHUNK, CHUNK)
            dst[b, pl.ds(at, CHUNK), :] = dot_t(lhs[pl.ds(at, CHUNK), :], w_ref[b, pl.ds(o_out, ch), :])
            return 0

        lax.fori_loop(0, nchunk, project, 0)
        for half in range(2):
            rr = d // 2
            grad_ref[b, pl.ds(o_out, ch), half * ch : (half + 1) * ch] = dot(
                dmix_t[half * rr : (half + 1) * rr, :], st[b, pl.ds(SEGS, rows), :].astype(BF16)
            ).astype(BF16)

        def one(step, w, p):
            at = pl.multiple_of(step * SEGS, SEGS)
            a = 1.0 - upd[b, pl.ds(at, SEGS), :]
            c = dst[b, pl.ds(at, SEGS), :] + w
            return c, a * c, p * a

        w, p = jnp.zeros((SEGS, ch), F32), jnp.ones((SEGS, ch), F32)
        for step in range(steps - 1, steps - 6, -1):
            _, w, p = one(step, w, p)

        def step8(j, carry):
            w, p = carry
            for q in range(8):
                _, w, p = one(steps - 6 - (j * 8 + q), w, p)
            return w, p

        left = (steps - 8) // 8
        w, p = lax.fori_loop(0, left, step8, (w, p))
        for step in range(2, -1, -1):
            bends[2 * step, b] = p
            c, w, p = one(step, w, p)
            bends[2 * step + 1, b] = c
        bends[6, b] = w
        bends[7, b] = p
        return 0

    lax.fori_loop(0, blocks, backward_block, 0)

    def backward_chain(start):
        run = start
        for seg in range(SEGS - 1, -1, -1):
            ends[0, :, pl.ds(seg, 1), :] = run
            run = bends[6, :, pl.ds(seg, 1), :] + bends[7, :, pl.ds(seg, 1), :] * run
        return run

    bsend[:, pl.ds(0, 1), :] = backward_chain(jnp.zeros((blocks, 1, ch), F32))
    for step in range(3):
        bsend[:, pl.ds(step + 1, 1), :] = upd[:, pl.ds(step * SEGS, 1), :] * (
            bends[2 * step + 1, :, pl.ds(0, 1), :]
            + bends[2 * step, :, pl.ds(0, 1), :] * ends[0, :, pl.ds(0, 1), :]
        )
    bcopy = pltpu.make_async_remote_copy(
        src_ref=bsend,
        dst_ref=brecv,
        send_sem=sems.at[2],
        recv_sem=sems.at[3],
        device_id={"tensor": partner},
        device_id_type=MESH,
    )
    bcopy.start()
    bcopy.wait()
    backward_chain(brecv[:, pl.ds(0, 1), :] * has_next)

    def backward_fix(b, _):
        w = ends[0, b]
        after = []
        for step in range(3):
            df = upd[b, pl.ds(step * SEGS, SEGS), :] * (bends[2 * step + 1, b] + bends[2 * step, b] * w)
            edge = brecv[b, pl.ds(step + 1, 1), :] * has_next
            after.append(jnp.where(seg_id == SEGS - 1, edge, pltpu.roll(df, SEGS - 1, 0)))
        k = [jnp.broadcast_to(conv_ref[b, pl.ds(i, 1), :], (SEGS, ch)) for i in range(4)]
        zero = jnp.zeros((SEGS, ch), F32)

        def pair(j, carry):
            w, d1, d2, d3, c0, c1, c2, k0, k1, k2, k3, gb = carry
            top = steps - 2 - 2 * j
            made = []
            for q in range(2):
                step = top + 1 - q
                at = pl.multiple_of(step * SEGS, SEGS)
                u = upd[b, pl.ds(at, SEGS), :]
                c = dst[b, pl.ds(at, SEGS), :] + w
                d0 = c * u
                a = 1.0 - u
                w = a * c
                dg = d0 * a * (filt[b, pl.ds(at, SEGS), :] - st[b, pl.ds(at, SEGS), :])
                dc = k[0] * d0 + k[1] * d1 + k[2] * d2 + k[3] * d3
                c3 = cand[b, pl.ds(at, SEGS), :]
                k0, k1, k2, k3 = k0 + d0 * c0, k1 + d0 * c1, k2 + d0 * c2, k3 + d0 * c3
                gb = gb + dg
                c0, c1, c2 = c1, c2, c3
                d1, d2, d3 = d0, d1, d2
                made.append((dg, dc))
            at = pl.multiple_of(top * SEGS, 2 * SEGS)
            act[pl.ds(at, 2 * SEGS), :ch] = jnp.concatenate([made[1][0], made[0][0]], axis=0).astype(BF16)
            act[pl.ds(at, 2 * SEGS), ch:] = jnp.concatenate([made[1][1], made[0][1]], axis=0).astype(BF16)
            return w, d1, d2, d3, c0, c1, c2, k0, k1, k2, k3, gb

        window = [cand[b, pl.ds((steps + 2 - i) * SEGS, SEGS), :] for i in range(3)]
        out = lax.fori_loop(0, steps // 2, pair, (w, *after, *window, zero, zero, zero, zero, zero))
        for i in range(5):
            chan_ref[b, pl.ds(i, 1), :] = jnp.sum(out[7 + i], axis=0, keepdims=True)

        def first_grad(r, _):
            at = pl.multiple_of(r * CHUNK, CHUNK)
            grad_ref[b, pl.ds(o_in + at, CHUNK), :] = dot(first_t[pl.ds(at, CHUNK), :], act[...]).astype(BF16)
            return 0

        lax.fori_loop(0, d // CHUNK, first_grad, 0)

        def first_back(r, _):
            at = pl.multiple_of(r * CHUNK, CHUNK)
            bufc[pl.ds(at, CHUNK), :] += dot_t(act[pl.ds(at, CHUNK), :], w_ref[b, pl.ds(o_in, d), :])
            return 0

        lax.fori_loop(0, nchunk, first_back, 0)
        return 0

    chan_ref[...] = jnp.zeros_like(chan_ref)
    lax.fori_loop(0, blocks, backward_fix, 0)

    def first_norm_back(r, gain):
        at = pl.multiple_of(r * CHUNK, CHUNK)
        m = x_ref[pl.ds(at, CHUNK), :].astype(F32)
        s = scale_of(m)
        dn = bufc[pl.ds(at, CHUNK), :]
        gain = gain + jnp.sum(dn * m * s, axis=0, keepdims=True)
        gd = dn * g1_ref[...]
        gx_ref[pl.ds(at, CHUNK), :] += s * gd - m * (s * s * s * jnp.mean(gd * m, axis=-1, keepdims=True))
        return gain

    gains_ref[pl.ds(0, 1), :] = lax.fori_loop(0, nchunk, first_norm_back, jnp.zeros((1, d), F32))


def permute(v):
    rows, d = v.shape
    return v.reshape(SEGS, rows // SEGS, d).transpose(1, 0, 2).reshape(rows, d)


def unpermute(v):
    rows, d = v.shape
    return v.reshape(rows // SEGS, SEGS, d).transpose(1, 0, 2).reshape(rows, d)


def per_device(
    inputs,
    norm_gain,
    in_weight,
    conv_kernel,
    gate_bias,
    out_weight,
    mlp_gain,
    up_weight,
    down_weight,
    short_lengths,
    long_lengths,
    cotangent,
):
    rows, d = inputs.shape
    ch = in_weight.shape[2]
    ff = up_weight.shape[1]
    blocks = lax.axis_size("tensor")
    dp = lax.axis_size("dp")
    assert blocks == 4 and rows == LSHORT and 2 * rows == LLONG
    assert short_lengths.shape == (2,) and long_lengths.shape == (1,)
    t = lax.axis_index("tensor")
    shard = jnp.concatenate([in_weight.reshape(d, 2 * ch), out_weight, up_weight, down_weight], axis=0)
    total = shard.shape[0]
    mine = lax.dynamic_slice_in_dim(shard, lax.axis_index("dp") * (total // dp), total // dp, 0)
    w_all = lax.all_gather(mine, ("tensor", "dp"), axis=0, tiled=True).reshape(blocks, total, d)
    small = jnp.concatenate([conv_kernel, gate_bias[None]], axis=0)
    small_all = lax.all_gather(small, "tensor", axis=0)
    conv_all = small_all[:, :4]
    bias_all = small_all[:, 4:5]
    halo = lax.ppermute(inputs[-16:], "tensor", [(i, i + 1) for i in range(blocks - 1)])
    lengths = jnp.concatenate([short_lengths, long_lengths, long_lengths - rows])
    limit = lax.dynamic_slice_in_dim(lengths, t, 1, 0)
    vm = pl.BlockSpec(memory_space=pltpu.VMEM)
    dims = (rows, d, blocks, ch, ff)
    res, gx, grads, gains, chan = pl.pallas_call(
        functools.partial(block_kernel, dims),
        out_shape=(
            jax.ShapeDtypeStruct((rows, d), BF16),
            jax.ShapeDtypeStruct((rows, d), F32),
            jax.ShapeDtypeStruct((blocks, total, d), BF16),
            jax.ShapeDtypeStruct((2, d), F32),
            jax.ShapeDtypeStruct((blocks, 8, ch), F32),
        ),
        in_specs=[pl.BlockSpec(memory_space=pltpu.SMEM)] + [vm] * 8,
        out_specs=(vm,) * 5,
        scratch_shapes=[
            pltpu.VMEM((blocks, rows + 3 * SEGS, ch), F32),
            pltpu.VMEM((blocks, rows, ch), F32),
            pltpu.VMEM((blocks, rows, ch), F32),
            pltpu.VMEM((blocks, rows + SEGS, ch), F32),
            pltpu.VMEM((blocks, rows, ch), F32),
            pltpu.VMEM((rows + 16, d), BF16),
            pltpu.VMEM((d, rows), BF16),
            pltpu.VMEM((d, rows), BF16),
            pltpu.VMEM((rows, d), BF16),
            pltpu.VMEM((d, rows), BF16),
            pltpu.VMEM((d, rows), BF16),
            pltpu.VMEM((rows, d), F32),
            pltpu.VMEM((rows, d), F32),
            pltpu.VMEM((rows, d), F32),
            pltpu.VMEM((rows, ff), BF16),
            pltpu.VMEM((rows, ff), BF16),
            pltpu.VMEM((2, blocks, SEGS, ch), F32),
            pltpu.VMEM((8, blocks, SEGS, ch), F32),
            pltpu.VMEM((blocks, 8, ch), F32),
            pltpu.VMEM((blocks, 8, ch), F32),
            pltpu.VMEM((blocks, 8, ch), F32),
            pltpu.VMEM((blocks, 8, ch), F32),
            pltpu.SemaphoreType.DMA((4,)),
        ],
        compiler_params=pltpu.CompilerParams(
            collective_id=0, has_side_effects=True, vmem_limit_bytes=67043328
        ),
        name="block",
    )(limit, permute(inputs), halo, permute(cotangent), norm_gain[None], mlp_gain[None], w_all, conv_all, bias_all)
    result = unpermute(res)
    grad_inputs = unpermute(gx)
    part = lax.psum_scatter(grads, "dp", scatter_dimension=1, tiled=True)
    part = lax.psum_scatter(part, "tensor", scatter_dimension=0, tiled=True)
    own = lax.all_gather(part[0], "dp", axis=0, tiled=True).astype(F32)
    grad_in = own[:d].reshape(d, 2, ch)
    packed = own[d : d + ch]
    grad_out = jnp.concatenate([packed[:, :ch], packed[:, ch:]], axis=0).T
    grad_up = own[d + ch : d + ch + ff]
    grad_down = own[d + ch + ff :].T
    gains, chan = lax.psum((gains, chan), ("dp", "tensor"))
    chan = lax.dynamic_slice_in_dim(chan, t, 1, 0)[0]
    return (
        result,
        grad_inputs,
        gains[0],
        grad_in,
        chan[:4],
        chan[4],
        grad_out,
        gains[1],
        grad_up,
        grad_down,
    )


def solution(mesh):
    placed = (
        P(("dp", "tensor"), None),
        P(),
        P(None, None, "tensor"),
        P(None, "tensor"),
        P("tensor"),
        P("tensor", None),
        P(),
        P(None, "tensor"),
        P("tensor", None),
        P("dp"),
        P("dp"),
        P(("dp", "tensor"), None),
    )
    return jax.shard_map(
        per_device,
        mesh=mesh,
        in_specs=placed,
        out_specs=(
            P(("dp", "tensor"), None),
            P(("dp", "tensor"), None),
            P(),
            P(None, None, "tensor"),
            P(None, "tensor"),
            P("tensor"),
            P("tensor", None),
            P(),
            P(None, "tensor"),
            P("tensor", None),
        ),
        check_vma=False,
    )
```

time: 1420 us -> 321 us (0.23)
  waiting for transfers between devices: 917 us -> 147 us
  other arithmetic: 212 us -> 5.42 us
  local copies, waits for them, and re-layouts: 133 us -> 18.5 us
  matrix products: 92.8 us -> 0 us
  Pallas kernels: 0 us -> 77 us
    reduce_scatter x4 -> x2, waiting for transfers between devices: 565 us -> 93.1 us  [the longest x1 65.6 us: per_device(): part = lax.psum_scatter(grads, 'dp', scatter_dimension=1, tiled=True)]
    all_gather x4 -> x2, waiting for transfers between devices: 288 us -> 53.8 us  [the longest x1 53.8 us: per_device(): lax.all_gather(mine, ('tensor', 'dp'), axis=0, tiled=True)]
    reduce_sum x18 -> x0, other arithmetic: 127 us -> none  [the longest x2 72.1 us: recurrence(): spread = summed_logs[:, :, :, None, :] - summed_logs[:, :, None, :, :]]
    dot_general x16 -> x0, matrix products: 92.8 us -> none  [the longest x1 23 us: per_device(): inner = jnp.dot(second_all, up_weight, preferred_element_type=jnp.float32)]
    pallas_call x0 -> x1, Pallas kernels: none -> 77 us  [per_device(): pl.pallas_call(functools.partial(block_kernel, dims), out_shape=(jax.Shap...]
    psum x1 -> x0, waiting for transfers between devices: 63.1 us -> none  [per_device(): lax.psum((grad_in, grad_out, grad_up, grad_down), 'dp')]
    scatter-add x6 -> x0, local copies, waits for them, and re-layouts: 39.3 us -> none  [causal_filter(): total = total.at[:, lag:].add(values[:, :-lag] * kernel[lag])]
    unnamed x371 -> x23, local copies, waits for them, and re-layouts: 39.1 us -> 4.17 us
  transfers between devices with their start and end apart: 9 -> 5, of which waited for: 9 -> 3; matrix products, arithmetic and copies ran while one was open for 4% -> 3% of each run, Pallas kernels for 0% -> 0%
where the time goes in v1:
time: 321 us; the launch traced here: 320 us
  waiting for transfers between devices  147 us (46%)
  Pallas kernels  77 us (24%)
  blocking collectives  52 us (16%)
  local copies, waits for them, and re-layouts  18.5 us (6%)
  between operations  14.6 us (5%)
  starting transfers between devices  5.71 us (2%)
  other arithmetic  5.42 us (2%)
    pallas_call x1, Pallas kernels, per_device(): pl.pallas_call(functools.partial(block_kernel, dims), out_shape=(jax.Shap...  77 us
    reduce_scatter x1, waiting for transfers between devices, per_device(): part = lax.psum_scatter(grads, 'dp', scatter_dimension=1, tiled=True)  65.6 us
    all_gather x1, waiting for transfers between devices, per_device(): lax.all_gather(mine, ('tensor', 'dp'), axis=0, tiled=True)  53.8 us
    psum x1, blocking collectives, per_device(): gains, chan = lax.psum((gains, chan), ('dp', 'tensor'))  38.9 us
    reduce_scatter x1, waiting for transfers between devices, per_device(): part = lax.psum_scatter(part, 'tensor', scatter_dimension=0, tiled=True)  27.5 us
    all_gather x1, blocking collectives, per_device(): small_all = lax.all_gather(small, 'tensor', axis=0)  13.1 us
  transfers between devices with their start and end apart: 5, of which 3 were waited for; matrix products, arithmetic and copies ran while one was open for 3% of the time, Pallas kernels for 0%

profile of v1, /device:TPU:0, one launch (start us, length us, event | category | flops | bytes accessed | tf_op | source)
XLA Modules:
  0.0 320.2 jit_solution(9046578466565432916)
XLA Ops:
  7.2 0.0 all-gather.6.cloned.1.call-start
  7.3 1.3 copy.34
  8.5 1.1 fusion.2
  9.6 0.0 all-gather.6.cloned.1.call-update
  9.6 0.0 reduce-scatter.3.cloned.1.call-start
  9.7 5.6 %collective-permute-start = (bf16[16,512]{1,0:T(8,128)(2,1)S(1)}, bf16[16,512]{1,0:T(8,128)(2,1)}, u32[]{:S(2)}, u32[]{:S(2)}) collective-permute-start(bf16[16,512]{1,0:T(8,128)(2,1)S(1)} %slice.43), channel_id=1, source_target_pairs={{0,1},{1,2},{2,3},{4,5},{5,6},{6,7},{8,9},{9,10},{10,11},{12,13},{... | collective-permute-start | bytes 49160 | tf_op jit(solution)/shard_map/ppermute | solution.py:427
  15.9 2.5 copy_bitcast_fusion
  18.4 0.1 pad_add_fusion
  18.5 13.1 %all-gather.2 = f32[4,5,256]{2,1,0:T(8,128)S(1)} all-gather(f32[1,5,256]{2,1,0:T(8,128)S(1)} %maximum_bitcast_fusion.1), channel_id=2, replica_groups=mesh['dp'=8,'tensor'=4] {'tensor'}, dimensions={0}, use_global_device_ids=true | all-gather | bytes 25600 | tf_op jit(solution)/shard_map/all_gather | solution.py:424
  31.6 0.6 slice.59.conv_ref
  32.2 0.6 slice.60.bias_ref
  32.8 0.6 dynamic_slice.9.lim_ref
  33.4 53.8 %all-gather.6.cloned.1.call-done = bf16[7168,512]{1,0:T(8,128)(2,1)} async-done(((bf16[224,512]{1,0:T(8,128)(2,1)}), bf16[7168,512]{1,0:T(8,128)(2,1)}) %all-gather.6.cloned.1.call-update) | async-done | bytes 7340048 | tf_op jit(solution)/shard_map/all_gather | solution.py:422
  87.3 77.0 %block.1 = (bf16[1024,512]{1,0:T(8,128)(2,1)}, f32[1024,512]{1,0:T(8,128)}, bf16[4,1792,512]{2,1,0:T(8,128)(2,1)}, f32[2,512]{1,0:T(2,128)}, f32[4,8,256]{2,1,0:T(8,128)}) custom-call(s32[1]{0:T(128)} %dynamic_slice.9.lim_ref, bf16[1024,512]{1,0:T(8,128)(2,1)} %get-tuple-element.51.x_ref, bf16[16,512]{1,0:T(8,128)(2,1)} %collective-permute-done.halo_ref, ...), custom_call_target="tpu_custom_call" | custom-call | tf_op jit(solution)/shard_map/block/pallas_call | solution.py:432
  164.3 0.0 reduce-scatter.3.cloned.1.call-update
  164.3 0.0 reduce-scatter.5.cloned.1.call-start
  164.4 65.6 %reduce-scatter.3.cloned.1.call-done = bf16[4,224,512]{2,1,0:T(8,128)(2,1)} async-done(((bf16[4,1792,512]{2,1,0:T(8,128)(2,1)}), bf16[4,224,512]{2,1,0:T(8,128)(2,1)}) %reduce-scatter.3.cloned.1.call-update) | async-done | bytes 917520 | tf_op jit(solution)/shard_map/reduce_scatter | solution.py:475
  229.9 0.0 all-gather.8.cloned.1.call-start
  230.0 27.5 %reduce-scatter.5.cloned.1.call-done = bf16[1,224,512]{2,1,0:T(8,128)(2,1)} async-done(((bf16[4,224,512]{2,1,0:T(8,128)(2,1)}), bf16[1,224,512]{2,1,0:T(8,128)(2,1)}) %reduce-scatter.5.cloned.1.call-update) | async-done | bytes 229392 | tf_op jit(solution)/shard_map/reduce_scatter | solution.py:476
  257.5 2.5 copy.31
  260.1 1.3 copy.30
  261.4 38.9 %all-reduce = (f32[2,512]{1,0:T(2,128)S(1)}, f32[4,8,256]{2,1,0:T(8,128)S(1)}) all-reduce(f32[2,512]{1,0:T(2,128)S(1)} %copy-done.6, f32[4,8,256]{2,1,0:T(8,128)S(1)} %copy-done.5), channel_id=1, replica_groups=mesh['dp'=8,'tensor'=4] {'dp','tensor'}, use_global_device_ids=true, to_apply=%region_0.0 | all-reduce | flops 9216 | bytes 73728 | tf_op jit(solution)/shard_map/psum | solution.py:483
  300.3 0.6 constant_dynamic-slice_fusion
  300.9 0.6 dynamic-slice_bitcast_fusion
  301.5 0.6 fusion.5
  302.1 4.2 %fusion.4 = (f32[1,1792,512]{2,1,0:T(8,128)}, f32[1792,512]{1,0:T(8,128)S(1)}) fusion(bf16[1,1792,512]{2,1,0:T(8,128)(2,1)} %all-gather.8.cloned.1.call-done), kind=kLoop, calls=%fused_computation.18 | loop fusion | flops 917504 | bytes 9175040 | tf_op jit(solution)/shard_map/convert_element_type | solution.py:477
  306.4 1.0 copy.32
  307.4 2.7 slice_bitcast_fusion
  310.1 1.3 copy.33
  311.4 0.6 copy-done
  311.9 0.1 slice.62
  312.1 1.6 reshape.66
  (27 shorter events, 0.2 us)
Async XLA Ops:
  7.2 2.5 copy-start.2
  7.2 8.7 %copy-start.8 = (f32[256]{0:T(256)S(1)}, f32[256]{0:T(256)}, u32[]{:S(2)}) copy-start(f32[256]{0:T(256)} %param.16) | copy-start | bytes 3076
  7.2 8.7 %copy-start.7 = (f32[4,256]{1,0:T(4,128)S(1)}, f32[4,256]{1,0:T(4,128)}, u32[]{:S(2)}) copy-start(f32[4,256]{1,0:T(4,128)} %param.15) | copy-start | bytes 12292
  7.2 8.7 %copy-start.4 = (bf16[1024,512]{1,0:T(8,128)(2,1)S(1)}, bf16[1024,512]{1,0:T(8,128)(2,1)}, u32[]{:S(2)}) copy-start(bf16[1024,512]{1,0:T(8,128)(2,1)} %param.23) | copy-start | bytes 3145732
  7.2 80.0 %all-gather.6.cloned.1.call-start = ((), (), s32[]{:S(2)}) async-start(), calls=%async_computation.2 | async-start | bytes 7569408 | tf_op jit(solution)/shard_map/all_gather | solution.py:422
  9.6 220.3 %reduce-scatter.3.cloned.1.call-start = ((), (), s32[]{:S(2)}) async-start(), calls=%async_computation.3 | async-start | bytes 8257536 | tf_op jit(solution)/shard_map/reduce_scatter | solution.py:475
  9.7 23.7 %collective-permute-start = (bf16[16,512]{1,0:T(8,128)(2,1)S(1)}, bf16[16,512]{1,0:T(8,128)(2,1)}, u32[]{:S(2)}, u32[]{:S(2)}) collective-permute-start(bf16[16,512]{1,0:T(8,128)(2,1)S(1)} %slice.43), channel_id=1, source_target_pairs={{0,1},{1,2},{2,3},{4,5},{5,6},{6,7},{8,9},{9,10},{10,11},{12,13},{... | collective-permute-start | bytes 49160 | tf_op jit(solution)/shard_map/ppermute | solution.py:427
  15.9 2.5 copy-start.9
  164.3 93.3 %copy-start.1 = (f32[1024,512]{1,0:T(8,128)S(1)}, f32[1024,512]{1,0:T(8,128)}, u32[]{:S(2)}) copy-start(f32[1024,512]{1,0:T(8,128)} %get-tuple-element.16) | copy-start | bytes 6291460
  164.3 93.2 %reduce-scatter.5.cloned.1.call-start = ((), (), s32[]{:S(2)}) async-start(), calls=%async_computation.4 | async-start | bytes 1146880 | tf_op jit(solution)/shard_map/reduce_scatter | solution.py:476
  229.9 72.1 %all-gather.8.cloned.1.call-start = ((), (), s32[]{:S(2)}) async-start(), calls=%async_computation.5 | async-start | bytes 2064384 | tf_op jit(solution)/shard_map/all_gather | solution.py:477
  257.5 2.6 copy-start.3
  260.1 1.3 copy-start.5
  260.1 1.3 copy-start.6
  310.1 1.9 copy-start
Sparse Core Ops, SparseCore 0:
  11.4 75.7 all-gather.5
  164.4 65.4 reduce-scatter.2
  232.2 25.2 reduce-scatter.4
  259.2 25.6 all-gather.7

commit v2 on v1

v2 whole, which is shorter than its diff:
```python
import functools

import jax
import jax.numpy as jnp
import numpy as np
from jax import lax
from jax.experimental import pallas as pl
from jax.experimental.pallas import tpu as pltpu
from jax.sharding import PartitionSpec as P

LSHORT = 1024
LLONG = 2048
SEGS = 8
EPS = 1e-05
CHUNK = 256
TILE = 16
LANES = 128
F32 = jnp.float32
BF16 = jnp.bfloat16
MESH = pl.DeviceIdType.MESH
IN, OUT, FF = 0, 1, 2


def dot(a, b):
    return jnp.dot(a, b, preferred_element_type=F32)


def dot_t(a, b):
    return lax.dot_general(a, b, (((1,), (1,)), ((), ())), preferred_element_type=F32)


def scale_of(v):
    return lax.rsqrt(jnp.mean(v * v, axis=-1, keepdims=True) + EPS)


def sigmoid(v):
    return 1.0 / (1.0 + jnp.exp(-v))


def bit_of(v, bit):
    return lax.rem(lax.div(v, 1 << bit), 2)


def flip(v, bit):
    return v + (1 << bit) * (1 - 2 * bit_of(v, bit))


def log2(n):
    return int(n).bit_length() - 1


def block_kernel(
    dims,
    short_ref,
    long_ref,
    x_hbm,
    cot_hbm,
    g1_ref,
    g2_ref,
    conv_ref,
    bias_ref,
    win_hbm,
    wout_hbm,
    wup_hbm,
    wdown_hbm,
    res_hbm,
    gx_hbm,
    gin_ref,
    gout_ref,
    gup_ref,
    gdown_ref,
    gains_ref,
    chan_ref,
    w_all,
    grad,
    fin,
    xp,
    cand,
    upd,
    st,
    dst,
    lhs,
    first_t,
    second_t,
    dout,
    dout_t,
    bufa,
    mid,
    bufc,
    dproj,
    perm,
    halo,
    cb,
    ends,
    bends,
    fsend,
    frecv,
    bsend,
    brecv,
    zbuf,
    gsum,
    grecv,
    csum,
    crecv,
    lsem,
    csem,
    zsem,
    w_s,
    w_r,
    r_s,
    r_r,
    a_s,
    a_r,
    s_s,
    s_r,
    *stage_bufs,
):
    rows, d, blocks, ch, ff, nb = dims
    steps = rows // SEGS
    t = lax.axis_index("tensor")
    p = lax.axis_index("dp")
    partner = flip(t, 0)
    nchunk = rows // CHUNK
    offs = (0, d, d + ch)
    sizes = (d, ch, 2 * ff)
    o_in, o_out, o_up, o_down = 0, d, d + ch, d + ch + ff
    halves = tuple(min(nb, log2(r // TILE)) for r in sizes)
    half_d = d // 2
    lanes = (pl.ds(0, half_d), pl.ds(half_d, half_d))
    orders = ((0,) + tuple(range(nb - 1, 0, -1)), tuple(range(nb)))
    nstage = len(stage_bufs)

    def zflip(j):
        b0, b1 = lax.rem(j, 2), lax.div(j, 2)
        return t + b0 * (1 - 2 * bit_of(t, 0)) + b1 * (2 - 4 * bit_of(t, 1))

    def low_of(kind, c, k):
        low = 0
        for i in range(min(k, halves[kind])):
            low = low + bit_of(p, orders[c][i]) * (sizes[kind] >> (i + 1))
        return low

    def span(kind, k):
        return sizes[kind] >> min(k, halves[kind])

    def at_rows(kind, start, n):
        return pl.ds(pl.multiple_of(offs[kind] + start, TILE), n)

    def stage_rows(kind, k):
        base = sum(span(i, k + 1) for i in range(kind))
        return pl.ds(base, span(kind, k + 1))

    def remote(src, dst_, ss, rs, **dev):
        return pltpu.make_async_remote_copy(
            src_ref=src, dst_ref=dst_, send_sem=ss, recv_sem=rs, device_id=dev, device_id_type=MESH
        )

    def w_z(kind, j, c, shard, target):
        at = at_rows(kind, low_of(kind, c, nb), span(kind, nb))
        ref = w_all.at[shard, at, lanes[c]]
        return remote(ref, ref, w_s.at[kind, j, nb, c], w_r.at[kind, j, nb, c], tensor=target)

    def w_step(kind, j, k):
        s = zflip(j)
        if k == 0:
            at = at_rows(kind, low_of(kind, 0, 1), span(kind, 1))
            ref = w_all.at[s, at, :]
            return [remote(ref, ref, w_s.at[kind, j, 0, 0], w_r.at[kind, j, 0, 0], dp=flip(p, 0))]
        made = []
        for c in range(2):
            at = at_rows(kind, low_of(kind, c, k + 1), span(kind, k + 1))
            ref = w_all.at[s, at, lanes[c]]
            made.append(remote(ref, ref, w_s.at[kind, j, k, c], w_r.at[kind, j, k, c], dp=flip(p, orders[c][k])))
        return made

    def w_sources(kind, j):
        return [w_z(kind, j, c, t, zflip(j)) for c in range(2)]

    def w_wait(kind, j, k):
        if k == halves[kind]:
            copies = [w_z(kind, j, c, zflip(j), zflip(j)) for c in range(2)]
        else:
            copies = w_step(kind, j, k)
        for copy in copies:
            copy.wait_recv()

    def w_forward(kind, j, k):
        w_wait(kind, j, k + 1)
        for copy in w_step(kind, j, k):
            copy.start()

    def w_all_j(kind, k):
        def go(j, _):
            w_forward(kind, j, k)
            return 0

        lax.fori_loop(1, blocks, go, 0)

    def r_step(kind, j, k):
        s = zflip(j)
        buf = stage_bufs[k]
        base = sum(span(i, k + 1) for i in range(kind))
        made = []
        for c in range(2):
            if k < halves[kind]:
                low = low_of(kind, c, k) + (1 - bit_of(p, orders[c][k])) * span(kind, k + 1)
            else:
                low = low_of(kind, c, k)
            which = slice(None) if k == 0 else lanes[c]
            made.append(
                remote(
                    grad.at[s, at_rows(kind, low, span(kind, k + 1)), which],
                    buf.at[j, pl.ds(base, span(kind, k + 1)), which],
                    r_s.at[kind, j, k, c],
                    r_r.at[kind, j, k, c],
                    dp=flip(p, orders[c][k]),
                )
            )
            if k == 0:
                break
        return made

    def r_start(kind, j, k):
        for copy in r_step(kind, j, k):
            copy.start()

    def r_finish(kind, j, k):
        s = zflip(j)
        buf = stage_bufs[k]
        base = sum(span(i, k + 1) for i in range(kind))
        n = span(kind, k + 1)
        for copy in r_step(kind, j, k):
            if k >= halves[kind]:
                copy.wait_send()
            copy.wait_recv()
        piece = min(n, 128)
        for c in range(2):
            low = low_of(kind, c, k + 1)

            def add(i, _):
                at = at_rows(kind, low + i * piece, piece)
                here = pl.ds(pl.multiple_of(base + i * piece, TILE), piece)
                grad[s, at, lanes[c]] = (
                    grad[s, at, lanes[c]].astype(F32) + buf[j, here, lanes[c]].astype(F32)
                ).astype(BF16)
                return 0

            lax.fori_loop(0, n // piece, add, 0)

    def r_z(kind, j):
        s = zflip(j)
        base = sum(span(i, nb) for i in range(kind))
        made = []
        for c in range(2):
            at = at_rows(kind, low_of(kind, c, nb), span(kind, nb))
            made.append(
                remote(
                    grad.at[s, at, lanes[c]],
                    zbuf.at[j, pl.ds(base, span(kind, nb)), lanes[c]],
                    r_s.at[kind, j, nb, c],
                    r_r.at[kind, j, nb, c],
                    tensor=s,
                )
            )
        return made

    def r_out(kind, j):
        for copy in r_z(kind, j):
            copy.start()

    def r_total(kind):
        base = sum(span(i, nb) for i in range(kind))
        n = span(kind, nb)
        for j in range(1, blocks):
            for copy in r_z(kind, j):
                copy.wait_recv()
        for c in range(2):
            at = at_rows(kind, low_of(kind, c, nb), n)
            total = grad[t, at, lanes[c]].astype(F32)
            for j in range(1, blocks):
                total = total + zbuf[j, pl.ds(base, n), lanes[c]].astype(F32)
            fin[at, lanes[c]] = total.astype(BF16)

    def a_step(kind, k):
        if k == 0:
            ref = fin.at[at_rows(kind, low_of(kind, 0, 1), span(kind, 1)), :]
            return [remote(ref, ref, a_s.at[kind, 0, 0], a_r.at[kind, 0, 0], dp=flip(p, 0))]
        made = []
        for c in range(2):
            ref = fin.at[at_rows(kind, low_of(kind, c, k + 1), span(kind, k + 1)), lanes[c]]
            made.append(remote(ref, ref, a_s.at[kind, k, c], a_r.at[kind, k, c], dp=flip(p, orders[c][k])))
        return made

    def a_start(kind, k):
        for copy in a_step(kind, k):
            copy.start()

    def a_wait(kind, k):
        for copy in a_step(kind, k):
            copy.wait_recv()

    def r_middle(kind, j):
        for k in range(1, nb - 1):
            r_finish(kind, j, k)
            r_start(kind, j, k + 1)

    def r_first(kind, j):
        r_finish(kind, j, 0)
        r_start(kind, j, 1)

    def r_last(kind, j, shard_known=None):
        r_finish(kind, j, nb - 1)
        if shard_known is None:
            @pl.when(j > 0)
            def _():
                r_out(kind, j)
        elif shard_known > 0:
            r_out(kind, j)

    def s_step(which, k):
        total, got = ((gsum, grecv), (csum, crecv))[which]
        dev = {"dp": flip(p, k)} if k < nb else {"tensor": flip(t, k - nb)}
        return remote(total.at[k], got.at[k], s_s.at[which, k], s_r.at[which, k], **dev)

    def s_next(which, k):
        total, got = ((gsum, grecv), (csum, crecv))[which]
        s_step(which, k).wait_recv()
        total[k + 1] = total[k] + got[k]
        if k + 1 < nb + 2:
            s_step(which, k + 1).start()

    def local(src, dst_, i):
        return pltpu.make_async_copy(src, dst_, lsem.at[i])

    loads = [
        local(win_hbm, w_all.at[t, pl.ds(o_in, d), :], 0),
        local(wout_hbm, w_all.at[t, pl.ds(o_out, ch), :], 1),
        local(wup_hbm, w_all.at[t, pl.ds(o_up, ff), :], 2),
        local(wdown_hbm, w_all.at[t, pl.ds(o_down, ff), :], 3),
        local(x_hbm, dproj.at[0], 4),
        local(cot_hbm, dproj.at[1], 5),
    ]
    for copy in loads:
        copy.start()
    cb[0, pl.ds(0, 4), :] = conv_ref[...]
    cb[0, pl.ds(4, 1), :] = bias_ref[...]
    barrier = pltpu.get_barrier_semaphore()
    for b in range(nb):
        pl.semaphore_signal(barrier, inc=1, device_id={"dp": flip(p, b)}, device_id_type=MESH)
    for j in range(1, blocks):
        pl.semaphore_signal(barrier, inc=1, device_id={"tensor": zflip(j)}, device_id_type=MESH)
    pl.semaphore_wait(barrier, nb + blocks - 1)

    def c_copy(j):
        return remote(cb.at[0], cb.at[j], csem.at[0, j], csem.at[1, j], tensor=zflip(j))

    hcopy = remote(dproj.at[0, pl.ds(rows - 16, 16), :], halo, zsem.at[0], zsem.at[1], tensor=partner)
    loads[0].wait()
    for j in range(1, blocks):
        for copy in w_sources(IN, j):
            copy.start()
    for j in range(1, blocks):
        c_copy(j).start()
    loads[4].wait()
    hcopy.start()
    loads[1].wait()
    for j in range(1, blocks):
        for copy in w_sources(OUT, j):
            copy.start()
    loads[2].wait()
    loads[3].wait()
    for j in range(1, blocks):
        for copy in w_sources(FF, j):
            copy.start()

    nlane = d // LANES

    def spread(ref):
        for seg in range(SEGS):
            v = ref[pl.ds(seg * steps, steps), :].astype(F32)
            for i in range(nlane):
                perm[i, pl.ds(seg, steps, stride=SEGS), :] = v[:, i * LANES : (i + 1) * LANES]

    def gather(ref):
        for seg in range(SEGS):
            for i in range(nlane):
                v = perm[i, pl.ds(seg, steps, stride=SEGS), :]
                ref[pl.ds(seg * steps, steps), i * LANES : (i + 1) * LANES] = v.astype(ref.dtype)

    def perm_rows(at):
        return jnp.concatenate([perm[i, pl.ds(at, CHUNK), :] for i in range(nlane)], axis=1)

    def put_perm(at, v):
        for i in range(nlane):
            perm[i, pl.ds(at, CHUNK), :] = v[:, i * LANES : (i + 1) * LANES]

    spread(dproj.at[0])
    limit = jnp.where(
        t == 0,
        short_ref[0],
        jnp.where(t == 1, short_ref[1], jnp.where(t == 2, long_ref[0], long_ref[0] - rows)),
    )

    def norm_rows(r, _):
        at = pl.multiple_of(r * CHUNK, CHUNK)
        xv = perm_rows(at)
        xp[pl.ds(at, CHUNK), :] = xv.astype(BF16)
        fv = xv * scale_of(xv) * g1_ref[...]
        lhs[pl.ds(at, CHUNK), :] = fv.astype(BF16)
        first_t[:, pl.ds(at, CHUNK)] = fv.T.astype(BF16)
        return 0

    lax.fori_loop(0, nchunk, norm_rows, 0)
    loads[5].wait()
    spread(dproj.at[1])
    w_all_j(IN, halves[IN] - 1)

    def dout_rows(r, _):
        at = pl.multiple_of(r * CHUNK, CHUNK)
        place = at + lax.broadcasted_iota(jnp.int32, (CHUNK, d), 0)
        pos = lax.rem(place, SEGS) * steps + place // SEGS
        dv = jnp.where(pos < limit, perm_rows(at), 0.0)
        dout[pl.ds(at, CHUNK), :] = dv.astype(BF16)
        dout_t[:, pl.ds(at, CHUNK)] = dv.T.astype(BF16)
        return 0

    lax.fori_loop(0, nchunk, dout_rows, 0)
    hcopy.wait()
    hv = halo[...].astype(F32)
    lhs[pl.ds(rows, 16), :] = (hv * scale_of(hv) * g1_ref[...]).astype(BF16)
    for j in range(1, blocks):
        c_copy(j).wait()

    seg_id = lax.broadcasted_iota(jnp.int32, (SEGS, ch), 0)
    has_prev = jnp.where(t == 3, 1.0, 0.0).astype(F32)
    has_next = jnp.where(t == 2, 1.0, 0.0).astype(F32)

    def forward_block(j, _):
        s_ = zflip(j)

        @pl.when(j > 0)
        def _():
            w_wait(IN, j, 0)

        def project(r, _):
            at = pl.multiple_of(r * CHUNK, CHUNK)
            v = dot(lhs[pl.ds(at, CHUNK), :], w_all[s_, pl.ds(o_in, d), :])
            bufa[pl.ds(at, CHUNK), :ch] = v[:, :ch]
            cand[j, pl.ds(at + 3 * SEGS, CHUNK), :] = v[:, ch:]
            return 0

        lax.fori_loop(0, nchunk, project, 0)

        @pl.when(j == 0)
        def _():
            for k in range(halves[IN] - 2, 0, -1):
                w_all_j(IN, k)

        @pl.when(j == 1)
        def _():
            for kind in (OUT, FF):
                for k in range(halves[kind] - 2, 0, -1):
                    w_all_j(kind, k)

        ph = dot(lhs[pl.ds(rows, 16), :], w_all[s_, pl.ds(o_in, d), ch:])
        for back in range(3):
            last = cand[j, pl.ds((steps + back) * SEGS, SEGS), :]
            rolled = pltpu.roll(last, 1, 0)
            edge = ph[13 + back : 14 + back, :] * has_prev
            cand[j, pl.ds(back * SEGS, SEGS), :] = jnp.where(seg_id == 0, edge, rolled)
        k_ = [jnp.broadcast_to(cb[j, pl.ds(i, 1), :], (SEGS, ch)) for i in range(4)]
        bias = jnp.broadcast_to(cb[j, pl.ds(4, 1), :], (SEGS, ch))

        def step4(i, carry):
            s, q_ = carry
            for q in range(4):
                at = pl.multiple_of((i * 4 + q) * SEGS, SEGS)
                u = sigmoid(bufa[pl.ds(at, SEGS), :ch] + bias)
                f = k_[0] * cand[j, pl.ds(at + 3 * SEGS, SEGS), :]
                for lag in range(1, 4):
                    f = f + k_[lag] * cand[j, pl.ds(at + (3 - lag) * SEGS, SEGS), :]
                upd[j, pl.ds(at, SEGS), :] = u
                dst[j, pl.ds(at, SEGS), :] = f
                a = 1.0 - u
                s = a * s + u * f
                q_ = a * q_
            return s, q_

        s, q_ = lax.fori_loop(
            0, steps // 4, step4, (jnp.zeros((SEGS, ch), F32), jnp.ones((SEGS, ch), F32))
        )
        ends[0, j] = s
        ends[1, j] = q_

        @pl.when(j == 0)
        def _():
            w_all_j(IN, 0)
            w_all_j(OUT, halves[OUT] - 1)
            w_all_j(FF, halves[FF] - 1)

        @pl.when(j == 1)
        def _():
            w_all_j(OUT, 0)
            w_all_j(FF, 0)

        return 0

    lax.fori_loop(0, blocks, forward_block, 0)

    def forward_chain(start):
        run = start
        for seg in range(SEGS):
            st[:, pl.ds(seg, 1), :] = run
            run = ends[0, :, pl.ds(seg, 1), :] + ends[1, :, pl.ds(seg, 1), :] * run
        return run

    fsend[...] = jnp.broadcast_to(forward_chain(jnp.zeros((blocks, 1, ch), F32)), (blocks, 8, ch))
    fcopies = [
        remote(fsend.at[j], frecv.at[j ^ 1], zsem.at[2 + 2 * j], zsem.at[3 + 2 * j], tensor=partner)
        for j in range(blocks)
    ]
    waits = [
        remote(fsend.at[j ^ 1], frecv.at[j], zsem.at[2 + 2 * (j ^ 1)], zsem.at[3 + 2 * (j ^ 1)], tensor=partner)
        for j in range(blocks)
    ]
    for copy in fcopies:
        copy.start()
    for j in range(blocks):
        waits[j].wait_recv()
    forward_chain(frecv[:, pl.ds(0, 1), :] * has_prev)

    def forward_fix(b, _):
        def step8(i, s):
            for q in range(8):
                at = pl.multiple_of((i * 8 + q) * SEGS, SEGS)
                u = upd[b, pl.ds(at, SEGS), :]
                s = (1.0 - u) * s + u * dst[b, pl.ds(at, SEGS), :]
                st[b, pl.ds(at + SEGS, SEGS), :] = s
            return s

        lax.fori_loop(0, steps // 8, step8, st[b, pl.ds(0, SEGS), :])
        return 0

    lax.fori_loop(0, blocks, forward_fix, 0)
    for j in range(1, blocks):
        w_wait(OUT, j, 0)
    shards = [zflip(j) for j in range(blocks)]

    def second_rows(r, _):
        at = pl.multiple_of(r * CHUNK, CHUNK)
        m = xp[pl.ds(at, CHUNK), :].astype(F32)
        for j in range(blocks):
            m = m + dot(
                st[j, pl.ds(at + SEGS, CHUNK), :].astype(BF16), w_all[shards[j], pl.ds(o_out, ch), :]
            )
        mid[pl.ds(at, CHUNK), :] = m
        sv = m * scale_of(m) * g2_ref[...]
        lhs[pl.ds(at, CHUNK), :] = sv.astype(BF16)
        second_t[:, pl.ds(at, CHUNK)] = sv.T.astype(BF16)
        bufa[pl.ds(at, CHUNK), :] = m
        bufc[pl.ds(at, CHUNK), :] = jnp.zeros((CHUNK, d), F32)
        return 0

    lax.fori_loop(0, nchunk, second_rows, 0)

    act, din = dproj.at[1], dproj.at[2]

    def ff_block(j, _):
        s_ = zflip(j)

        @pl.when(j > 0)
        def _():
            w_wait(FF, j, 0)

        def ff_rows(r, _):
            at = pl.multiple_of(r * CHUNK, CHUNK)
            wu = w_all[s_, pl.ds(o_up, ff), :]
            wd = w_all[s_, pl.ds(o_down, ff), :]
            inner = dot(lhs[pl.ds(at, CHUNK), :], wu)
            da = dot_t(dout[pl.ds(at, CHUNK), :], wd)
            cdf = 0.5 + 0.5 * lax.erf(inner * np.float32(np.sqrt(0.5)))
            pdf = jnp.exp(inner * inner * -0.5) * np.float32(1.0 / np.sqrt(2.0 * np.pi))
            av = (inner * cdf).astype(BF16)
            dv = (da * (cdf + inner * pdf)).astype(BF16)
            act[pl.ds(at, CHUNK), :] = av
            din[pl.ds(at, CHUNK), :] = dv
            bufa[pl.ds(at, CHUNK), :] += dot(av, wd)
            bufc[pl.ds(at, CHUNK), :] += dot_t(dv, wu)

            @pl.when((r == 0) & (j > 0))
            def _():
                r_first(FF, j - 1)

            @pl.when((r == 1) & (j > 1))
            def _():
                r_last(FF, j - 2)

            @pl.when((r == 2) & (j > 0))
            def _():
                r_middle(FF, j - 1)

            return 0

        lax.fori_loop(0, nchunk, ff_rows, 0)

        def ff_grads(r, _):
            at = pl.multiple_of(r * CHUNK, CHUNK)
            grad[s_, pl.ds(o_up + at, CHUNK), :] = dot(second_t[pl.ds(at, CHUNK), :], din[...]).astype(BF16)
            grad[s_, pl.ds(o_down + at, CHUNK), :] = dot(dout_t[pl.ds(at, CHUNK), :], act[...]).astype(BF16)
            return 0

        lax.fori_loop(0, d // CHUNK, ff_grads, 0)
        r_start(FF, j, 0)
        return 0

    lax.fori_loop(0, blocks, ff_block, 0)

    def second_back(r, gain):
        at = pl.multiple_of(r * CHUNK, CHUNK)
        put_perm(at, bufa[pl.ds(at, CHUNK), :])
        m = mid[pl.ds(at, CHUNK), :]
        s = scale_of(m)
        dn = bufc[pl.ds(at, CHUNK), :]
        gain = gain + jnp.sum(dn * m * s, axis=0, keepdims=True)
        gd = dn * g2_ref[...]
        dm = dout[pl.ds(at, CHUNK), :].astype(F32) + s * gd - m * (s * s * s * jnp.mean(gd * m, axis=-1, keepdims=True))
        mid[pl.ds(at, CHUNK), :] = dm
        lhs[pl.ds(at, CHUNK), :] = dm.astype(BF16)
        second_t[:, pl.ds(at, CHUNK)] = dm.T.astype(BF16)
        bufc[pl.ds(at, CHUNK), :] = jnp.zeros((CHUNK, d), F32)
        return gain

    gain2 = lax.fori_loop(0, nchunk, second_back, jnp.zeros((1, d), F32))
    gsum[0] = jnp.zeros((8, d), F32)
    gsum[0, pl.ds(1, 1), :] = gain2
    gather(dproj.at[0])
    res_copy = pltpu.make_async_copy(dproj.at[0], res_hbm, lsem.at[6])
    res_copy.start()
    r_first(FF, blocks - 1)
    r_last(FF, blocks - 2, blocks - 2)

    def backward_block(i, _):
        j = blocks - 1 - i
        s_ = zflip(j)

        def project(r, _):
            at = pl.multiple_of(r * CHUNK, CHUNK)
            dst[j, pl.ds(at, CHUNK), :] = dot_t(lhs[pl.ds(at, CHUNK), :], w_all[s_, pl.ds(o_out, ch), :])
            return 0

        lax.fori_loop(0, nchunk, project, 0)
        for half in range(2):
            rr = d // 2
            grad[s_, pl.ds(o_out, ch), half * ch : (half + 1) * ch] = dot(
                second_t[half * rr : (half + 1) * rr, :], st[j, pl.ds(SEGS, rows), :].astype(BF16)
            ).astype(BF16)
        r_start(OUT, j, 0)

        @pl.when(i == 0)
        def _():
            r_middle(FF, blocks - 1)

        def one(step, w, q_):
            at = pl.multiple_of(step * SEGS, SEGS)
            a = 1.0 - upd[j, pl.ds(at, SEGS), :]
            c = dst[j, pl.ds(at, SEGS), :] + w
            return c, a * c, q_ * a

        w, q_ = jnp.zeros((SEGS, ch), F32), jnp.ones((SEGS, ch), F32)
        for step in range(steps - 1, steps - 6, -1):
            _, w, q_ = one(step, w, q_)

        def step8(n, carry):
            w, q_ = carry
            for q in range(8):
                _, w, q_ = one(steps - 6 - (n * 8 + q), w, q_)
            return w, q_

        w, q_ = lax.fori_loop(0, (steps - 8) // 8, step8, (w, q_))
        for step in range(2, -1, -1):
            bends[2 * step, j] = q_
            c, w, q_ = one(step, w, q_)
            bends[2 * step + 1, j] = c
        bends[6, j] = w
        bends[7, j] = q_

        @pl.when(i == 1)
        def _():
            r_last(FF, blocks - 1, blocks - 1)

        @pl.when(i > 0)
        def _():
            r_first(OUT, j + 1)

        @pl.when(i > 1)
        def _():
            r_middle(OUT, j + 2)

        @pl.when(i > 2)
        def _():
            r_last(OUT, j + 3)

        return 0

    lax.fori_loop(0, blocks, backward_block, 0)

    def backward_chain(start):
        run = start
        for seg in range(SEGS - 1, -1, -1):
            ends[0, :, pl.ds(seg, 1), :] = run
            run = bends[6, :, pl.ds(seg, 1), :] + bends[7, :, pl.ds(seg, 1), :] * run
        return run

    bsend[:, pl.ds(0, 1), :] = backward_chain(jnp.zeros((blocks, 1, ch), F32))
    for step in range(3):
        bsend[:, pl.ds(step + 1, 1), :] = upd[:, pl.ds(step * SEGS, 1), :] * (
            bends[2 * step + 1, :, pl.ds(0, 1), :]
            + bends[2 * step, :, pl.ds(0, 1), :] * ends[0, :, pl.ds(0, 1), :]
        )
    bcopies = [
        remote(bsend.at[j], brecv.at[j ^ 1], zsem.at[10 + 2 * j], zsem.at[11 + 2 * j], tensor=partner)
        for j in range(blocks)
    ]
    bwaits = [
        remote(bsend.at[j ^ 1], brecv.at[j], zsem.at[10 + 2 * (j ^ 1)], zsem.at[11 + 2 * (j ^ 1)], tensor=partner)
        for j in range(blocks)
    ]
    for copy in bcopies:
        copy.start()
    r_first(OUT, 0)
    r_middle(OUT, 1)
    r_last(OUT, 2, 2)
    for j in range(blocks):
        bwaits[j].wait_recv()
    backward_chain(brecv[:, pl.ds(0, 1), :] * has_next)
    csum[0] = jnp.zeros((blocks, 8, ch), F32)
    res_copy.wait()

    def backward_fix(i, _):
        j = blocks - 1 - i
        s_ = zflip(j)
        w = ends[0, j]
        after = []
        for step in range(3):
            df = upd[j, pl.ds(step * SEGS, SEGS), :] * (bends[2 * step + 1, j] + bends[2 * step, j] * w)
            edge = brecv[j, pl.ds(step + 1, 1), :] * has_next
            after.append(jnp.where(seg_id == SEGS - 1, edge, pltpu.roll(df, SEGS - 1, 0)))
        k_ = [jnp.broadcast_to(cb[j, pl.ds(n, 1), :], (SEGS, ch)) for n in range(4)]
        zero = jnp.zeros((SEGS, ch), F32)

        def pair(n, carry):
            w, d1, d2, d3, c0, c1, c2, k0, k1, k2, k3, gb = carry
            top = steps - 2 - 2 * n
            made = []
            for q in range(2):
                at = pl.multiple_of((top + 1 - q) * SEGS, SEGS)
                u = upd[j, pl.ds(at, SEGS), :]
                c = dst[j, pl.ds(at, SEGS), :] + w
                d0 = c * u
                a = 1.0 - u
                w = a * c
                c3 = cand[j, pl.ds(at, SEGS), :]
                f = k_[0] * c0 + k_[1] * c1 + k_[2] * c2 + k_[3] * c3
                dg = d0 * a * (f - st[j, pl.ds(at, SEGS), :])
                dc = k_[0] * d0 + k_[1] * d1 + k_[2] * d2 + k_[3] * d3
                k0, k1, k2, k3 = k0 + d0 * c0, k1 + d0 * c1, k2 + d0 * c2, k3 + d0 * c3
                gb = gb + dg
                c0, c1, c2 = c1, c2, c3
                d1, d2, d3 = d0, d1, d2
                made.append((dg, dc))
            at = pl.multiple_of(top * SEGS, 2 * SEGS)
            dproj[j, pl.ds(at, 2 * SEGS), :ch] = jnp.concatenate([made[1][0], made[0][0]], axis=0).astype(BF16)
            dproj[j, pl.ds(at, 2 * SEGS), ch:] = jnp.concatenate([made[1][1], made[0][1]], axis=0).astype(BF16)
            return w, d1, d2, d3, c0, c1, c2, k0, k1, k2, k3, gb

        window = [cand[j, pl.ds((steps + 2 - n) * SEGS, SEGS), :] for n in range(3)]
        out = lax.fori_loop(0, steps // 2, pair, (w, *after, *window, zero, zero, zero, zero, zero))
        for n in range(5):
            csum[0, s_, pl.ds(n, 1), :] = jnp.sum(out[7 + n], axis=0, keepdims=True)

        @pl.when(i == 0)
        def _():
            r_middle(OUT, 0)
            r_last(OUT, 1, 1)
            r_total(FF)
            a_start(FF, halves[FF] - 1)

        @pl.when(i == 1)
        def _():
            r_last(OUT, 0, 0)
            for k in range(halves[FF] - 2, 0, -1):
                a_wait(FF, k + 1)
                a_start(FF, k)

        @pl.when(i == 2)
        def _():
            a_wait(FF, 1)
            a_start(FF, 0)
            r_total(OUT)
            a_start(OUT, halves[OUT] - 1)

        @pl.when(i == 3)
        def _():
            for k in range(halves[OUT] - 2, 0, -1):
                a_wait(OUT, k + 1)
                a_start(OUT, k)

        @pl.when(i > 0)
        def _():
            r_first(IN, j + 1)

        @pl.when(i > 1)
        def _():
            r_last(IN, j + 2)

        def first_grad(r, _):
            at = pl.multiple_of(r * CHUNK, CHUNK)
            grad[s_, pl.ds(o_in + at, CHUNK), :] = dot(first_t[pl.ds(at, CHUNK), :], dproj[j]).astype(BF16)
            return 0

        lax.fori_loop(0, d // CHUNK, first_grad, 0)
        r_start(IN, j, 0)

        @pl.when(i > 0)
        def _():
            r_middle(IN, j + 1)

        return 0

    lax.fori_loop(0, blocks, backward_fix, 0)
    s_step(1, 0).start()

    def first_back(r):
        at = r * CHUNK
        v = dot_t(dproj[0, pl.ds(at, CHUNK), :], w_all[shards[0], pl.ds(o_in, d), :])
        for j in range(1, blocks):
            v = v + dot_t(dproj[j, pl.ds(at, CHUNK), :], w_all[shards[j], pl.ds(o_in, d), :])
        bufc[pl.ds(at, CHUNK), :] = v

    first_back(0)
    r_first(IN, 0)
    r_last(IN, 1, 1)
    s_next(1, 0)
    first_back(1)
    a_wait(OUT, 1)
    a_start(OUT, 0)
    s_next(1, 1)
    first_back(2)
    r_middle(IN, 0)
    s_next(1, 2)
    for r in range(3, nchunk):
        first_back(r)

    def first_norm_back(r, gain):
        at = pl.multiple_of(r * CHUNK, CHUNK)
        m = xp[pl.ds(at, CHUNK), :].astype(F32)
        s = scale_of(m)
        dn = bufc[pl.ds(at, CHUNK), :]
        gain = gain + jnp.sum(dn * m * s, axis=0, keepdims=True)
        gd = dn * g1_ref[...]
        dv = s * gd - m * (s * s * s * jnp.mean(gd * m, axis=-1, keepdims=True))
        put_perm(at, mid[pl.ds(at, CHUNK), :] + dv)
        return gain

    gsum[0, pl.ds(0, 1), :] = lax.fori_loop(0, nchunk, first_norm_back, jnp.zeros((1, d), F32))
    s_step(0, 0).start()
    r_last(IN, 0, 0)
    r_total(IN)
    a_start(IN, halves[IN] - 1)
    for k in range(3, nb + 2):
        s_next(1, k)
    gather(mid)
    gx_copy = pltpu.make_async_copy(mid, gx_hbm, lsem.at[7])
    gx_copy.start()
    chan_ref[...] = csum[nb + 2, t]
    s_next(0, 0)
    for k in range(halves[IN] - 2, 0, -1):
        a_wait(IN, k + 1)
        a_start(IN, k)
    a_wait(FF, 0)
    gup_ref[...] = fin[pl.ds(o_up, d), :].astype(F32)
    gdown_ref[...] = fin[pl.ds(o_down, d), :].astype(F32).T
    s_next(0, 1)
    a_wait(OUT, 0)
    gout_ref[:, :half_d] = fin[pl.ds(o_out, ch), :ch].astype(F32).T
    gout_ref[:, half_d:] = fin[pl.ds(o_out, ch), ch:].astype(F32).T
    a_wait(IN, 1)
    a_start(IN, 0)
    for k in range(2, nb + 2):
        s_next(0, k)
    gains_ref[...] = gsum[nb + 2]
    a_wait(IN, 0)
    gin_ref[...] = fin[pl.ds(o_in, d), :].astype(F32)

    gx_copy.wait()
    for copy in fcopies + bcopies:
        copy.wait_send()
    for kind in (IN, OUT, FF):
        def drain(j, _):
            for copy in w_sources(kind, j):
                copy.wait_send()
            for k in range(halves[kind]):
                for copy in w_step(kind, j, k):
                    copy.wait_send()
            for copy in r_z(kind, j):
                copy.wait_send()
            return 0

        lax.fori_loop(1, blocks, drain, 0)

        def drain_halving(j, _):
            for k in range(halves[kind]):
                for copy in r_step(kind, j, k):
                    copy.wait_send()
            return 0

        lax.fori_loop(0, blocks, drain_halving, 0)
        for k in range(halves[kind]):
            for copy in a_step(kind, k):
                copy.wait_send()
    for k in range(nb + 2):
        s_step(0, k).wait_send()
        s_step(1, k).wait_send()


def per_device(
    inputs,
    norm_gain,
    in_weight,
    conv_kernel,
    gate_bias,
    out_weight,
    mlp_gain,
    up_weight,
    down_weight,
    short_lengths,
    long_lengths,
    cotangent,
):
    rows, d = inputs.shape
    ch = in_weight.shape[2]
    ff = up_weight.shape[1]
    blocks = lax.axis_size("tensor")
    dp = lax.axis_size("dp")
    nb = log2(dp)
    assert dp == 1 << nb and blocks == 4 and rows == LSHORT and 2 * rows == LLONG
    assert short_lengths.shape == (2,) and long_lengths.shape == (1,)
    sizes = (d, ch, 2 * ff)
    total = sum(sizes)
    halves = tuple(min(nb, log2(r // TILE)) for r in sizes)

    def span_all(k):
        return sum(r >> min(k, h) for r, h in zip(sizes, halves))

    vm = pl.BlockSpec(memory_space=pltpu.VMEM)
    sm = pl.BlockSpec(memory_space=pltpu.SMEM)
    hb = pl.BlockSpec(memory_space=pl.ANY)
    dma = pltpu.SemaphoreType.DMA
    result, grad_inputs, gin, gout, gup, gdown, gains, chan = pl.pallas_call(
        functools.partial(block_kernel, (rows, d, blocks, ch, ff, nb)),
        out_shape=(
            jax.ShapeDtypeStruct((rows, d), BF16),
            jax.ShapeDtypeStruct((rows, d), F32),
            jax.ShapeDtypeStruct((d, 2 * ch), F32),
            jax.ShapeDtypeStruct((ch, d), F32),
            jax.ShapeDtypeStruct((d, ff), F32),
            jax.ShapeDtypeStruct((ff, d), F32),
            jax.ShapeDtypeStruct((8, d), F32),
            jax.ShapeDtypeStruct((8, ch), F32),
        ),
        in_specs=[sm, sm, hb, hb, vm, vm, vm, vm, hb, hb, hb, hb],
        out_specs=(hb, hb) + (vm,) * 6,
        scratch_shapes=[
            pltpu.VMEM((blocks, total, d), BF16),
            pltpu.VMEM((blocks, total, d), BF16),
            pltpu.VMEM((total, d), BF16),
            pltpu.VMEM((rows, d), BF16),
            pltpu.VMEM((blocks, rows + 3 * SEGS, ch), F32),
            pltpu.VMEM((blocks, rows, ch), F32),
            pltpu.VMEM((blocks, rows + SEGS, ch), F32),
            pltpu.VMEM((blocks, rows, ch), F32),
            pltpu.VMEM((rows + 16, d), BF16),
            pltpu.VMEM((d, rows), BF16),
            pltpu.VMEM((d, rows), BF16),
            pltpu.VMEM((rows, d), BF16),
            pltpu.VMEM((d, rows), BF16),
            pltpu.VMEM((rows, d), F32),
            pltpu.VMEM((rows, d), F32),
            pltpu.VMEM((rows, d), F32),
            pltpu.VMEM((blocks, rows, d), BF16),
            pltpu.VMEM((d // LANES, rows, LANES), F32),
            pltpu.VMEM((16, d), BF16),
            pltpu.VMEM((blocks, 8, ch), F32),
            pltpu.VMEM((2, blocks, SEGS, ch), F32),
            pltpu.VMEM((8, blocks, SEGS, ch), F32),
            pltpu.VMEM((blocks, 8, ch), F32),
            pltpu.VMEM((blocks, 8, ch), F32),
            pltpu.VMEM((blocks, 8, ch), F32),
            pltpu.VMEM((blocks, 8, ch), F32),
            pltpu.VMEM((blocks, span_all(nb), d), BF16),
            pltpu.VMEM((nb + 3, 8, d), F32),
            pltpu.VMEM((nb + 2, 8, d), F32),
            pltpu.VMEM((nb + 3, blocks, 8, ch), F32),
            pltpu.VMEM((nb + 2, blocks, 8, ch), F32),
            dma((8,)),
            dma((2, blocks)),
            dma((18,)),
            dma((3, blocks, nb + 1, 2)),
            dma((3, blocks, nb + 1, 2)),
            dma((3, blocks, nb + 1, 2)),
            dma((3, blocks, nb + 1, 2)),
            dma((3, nb, 2)),
            dma((3, nb, 2)),
            dma((2, nb + 2)),
            dma((2, nb + 2)),
        ]
        + [pltpu.VMEM((blocks, span_all(k + 1), d), BF16) for k in range(nb)],
        compiler_params=pltpu.CompilerParams(
            collective_id=0, has_side_effects=True, vmem_limit_bytes=67043328
        ),
        name="block",
    )(
        short_lengths,
        long_lengths,
        inputs,
        cotangent,
        norm_gain[None],
        mlp_gain[None],
        conv_kernel,
        gate_bias[None],
        in_weight.reshape(d, 2 * ch),
        out_weight,
        up_weight,
        down_weight,
    )
    return (
        result,
        grad_inputs,
        gains[0],
        gin.reshape(d, 2, ch),
        chan[:4],
        chan[4],
        gout,
        gains[1],
        gup,
        gdown,
    )


def solution(mesh):
    placed = (
        P(("dp", "tensor"), None),
        P(),
        P(None, None, "tensor"),
        P(None, "tensor"),
        P("tensor"),
        P("tensor", None),
        P(),
        P(None, "tensor"),
        P("tensor", None),
        P("dp"),
        P("dp"),
        P(("dp", "tensor"), None),
    )
    return jax.shard_map(
        per_device,
        mesh=mesh,
        in_specs=placed,
        out_specs=(
            P(("dp", "tensor"), None),
            P(("dp", "tensor"), None),
            P(),
            P(None, None, "tensor"),
            P(None, "tensor"),
            P("tensor"),
            P("tensor", None),
            P(),
            P(None, "tensor"),
            P("tensor", None),
        ),
        check_vma=False,
    )
```

time: 321 us -> 177 us (0.55)
  waiting for transfers between devices: 147 us -> 0 us
  Pallas kernels: 77 us -> 161 us
  blocking collectives: 52 us -> 0 us
  between operations: 14.6 us -> 1.31 us
  starting transfers between devices: 5.71 us -> 0 us
  other arithmetic: 5.42 us -> 0 us
  local copies, waits for them, and re-layouts: 18.5 us -> 14 us
    reduce_scatter x2 -> x0, waiting for transfers between devices: 93.1 us -> none  [the longest x1 65.6 us: per_device(): part = lax.psum_scatter(grads, 'dp', scatter_dimension=1, tiled=True)]
    pallas_call x1, Pallas kernels: 77 us -> 161 us  [per_device(): pl.pallas_call(functools.partial(block_kernel, (rows, d, blocks, ch, ff,...]
    all_gather x2 -> x0, waiting for transfers between devices: 53.8 us -> none  [the longest x1 53.8 us: per_device(): lax.all_gather(mine, ('tensor', 'dp'), axis=0, tiled=True)]
    psum x1 -> x0, blocking collectives: 38.9 us -> none  [per_device(): gains, chan = lax.psum((gains, chan), ('dp', 'tensor'))]
    all_gather x1 -> x0, blocking collectives: 13.1 us -> none  [per_device(): small_all = lax.all_gather(small, 'tensor', axis=0)]
    transpose x3 -> x0, local copies, waits for them, and re-layouts: 6.5 us -> none  [the longest x2 3.82 us: unpermute(): return v.reshape(rows // SEGS, SEGS, d).transpose(1, 0, 2).reshape(rows, d)]
    ppermute x1 -> x0, starting transfers between devices: 5.55 us -> none  [per_device(): lax.ppermute(inputs[-16:], 'tensor', [(i, i + 1) for i in range(blocks -...]
    convert_element_type x1 -> x0, other arithmetic: 4.24 us -> none  [per_device(): own = lax.all_gather(part[0], 'dp', axis=0, tiled=True).astype(F32)]
  transfers between devices with their start and end apart: 5 -> 0, of which waited for: 3 -> 0; matrix products, arithmetic and copies ran while one was open for 3% -> 0% of each run, Pallas kernels for 0% -> 0%
where the time goes in v2:
time: 177 us
  Pallas kernels  161 us (91%)
  local copies, waits for them, and re-layouts  14 us (8%)
    pallas_call x1, Pallas kernels, per_device(): pl.pallas_call(functools.partial(block_kernel, (rows, d, blocks, ch, ff,...  161 us
    unnamed x16, local copies, waits for them, and re-layouts  7.01 us

profile of v2, /device:TPU:0, one launch (start us, length us, event | category | flops | bytes accessed | tf_op | source)
XLA Modules:
  0.0 176.6 jit_solution(16308401086353034913)
XLA Ops:
  1.3 1.9 %copy.22 = bf16[64,8,2,256]{3,1,2,0:T(8,128)(2,1)} copy(bf16[64,8,2,256]{3,2,1,0:T(2,128)(2,1)} %bitcast.9) | data formatting | bytes 1048576
  3.2 161.3 %block.1 = (bf16[1024,512]{1,0:T(8,128)(2,1)}, f32[1024,512]{1,0:T(8,128)}, f32[512,512]{1,0:T(8,128)}, f32[256,512]{1,0:T(8,128)}, f32[512,512]{1,0:T(8,128)}, ...) custom-call(s32[2]{0:T(128)} %short_ref.1, s32[1]{0:T(128)S(6)} %copy.28.long_ref, ...), custom_call_target="tpu_custom_call" | custom-call | tf_op jit(solution)/shard_map/block/pallas_call | solution.py:959
  164.5 0.0 copy-start.3
  164.5 1.3 slice.14
  165.9 1.3 slice.13
  167.1 1.4 fusion
  168.5 0.0 copy-start
  168.5 3.0 %reshape.27 = f32[512,2,256]{2,1,0:T(2,128)} reshape(f32[512,512]{1,0:T(8,128)} %get-tuple-element.21) | data formatting | bytes 2097152 | tf_op jit(solution)/shard_map/reshape | solution.py:1040
  171.5 0.0 copy-done.3
  171.5 1.0 copy.29
  172.5 0.0 copy-done
  172.5 0.0 copy-start.4
  172.5 0.0 copy-start.2
  172.5 1.3 copy.30
  173.8 0.1 copy-done.4
  173.9 0.0 copy-start.1
  173.9 0.8 copy.31
  174.7 0.0 copy-done.2
  174.7 1.0 copy.32
  175.6 0.0 copy-done.1
  175.6 1.0 copy.33
Async XLA Ops:
  164.5 7.0 %copy-start.3 = (bf16[1024,512]{1,0:T(8,128)(2,1)S(1)}, bf16[1024,512]{1,0:T(8,128)(2,1)}, u32[]{:S(2)}) copy-start(bf16[1024,512]{1,0:T(8,128)(2,1)} %get-tuple-element.38) | copy-start | bytes 3145732
  168.5 4.0 %copy-start = (f32[1024,512]{1,0:T(8,128)S(1)}, f32[1024,512]{1,0:T(8,128)}, u32[]{:S(2)}) copy-start(f32[1024,512]{1,0:T(8,128)} %get-tuple-element.39) | copy-start | bytes 6291460
  172.5 1.4 copy-start.4
  172.5 2.2 %copy-start.2 = (f32[512,512]{1,0:T(8,128)S(1)}, f32[512,512]{1,0:T(8,128)}, u32[]{:S(2)}) copy-start(f32[512,512]{1,0:T(8,128)} %get-tuple-element.46) | copy-start | bytes 3145732
  173.9 1.8 %copy-start.1 = (f32[512,512]{1,0:T(8,128)S(1)}, f32[512,512]{1,0:T(8,128)}, u32[]{:S(2)}) copy-start(f32[512,512]{1,0:T(8,128)} %get-tuple-element.47) | copy-start | bytes 3145732

commit v3 on v2

--- a/solution.py
+++ b/solution.py
@@ -47,6 +47,11 @@
 
 def log2(n):
     return int(n).bit_length() - 1
+
+
+def bit_groups(nb):
+    groups = [(0,)] + [tuple(range(b, min(b + 2, nb))) for b in range(1, nb, 2)]
+    return groups + [(nb, nb + 1)]
 
 
 def block_kernel(
@@ -65,15 +70,11 @@
     wdown_hbm,
     res_hbm,
     gx_hbm,
-    gin_ref,
-    gout_ref,
-    gup_ref,
-    gdown_ref,
+    fin,
     gains_ref,
     chan_ref,
     w_all,
     grad,
-    fin,
     xp,
     cand,
     upd,
@@ -98,17 +99,22 @@
     bsend,
     brecv,
     zbuf,
-    gsum,
-    grecv,
-    csum,
-    crecv,
+    ssum,
+    sgot,
     lsem,
-    csem,
-    zsem,
+    c_s,
+    c_r,
+    f_s,
+    f_r,
+    b_s,
+    b_r,
+    h_s,
+    h_r,
     w_s,
     w_r,
     r_s,
     r_r,
+    x_s,
     a_s,
     a_r,
     s_s,
@@ -155,69 +161,64 @@
             src_ref=src, dst_ref=dst_, send_sem=ss, recv_sem=rs, device_id=dev, device_id_type=MESH
         )
 
-    def w_z(kind, j, c, shard, target):
-        at = at_rows(kind, low_of(kind, c, nb), span(kind, nb))
-        ref = w_all.at[shard, at, lanes[c]]
-        return remote(ref, ref, w_s.at[kind, j, nb, c], w_r.at[kind, j, nb, c], tensor=target)
+    def wait_for(ref, sem):
+        pltpu.make_async_copy(ref, ref, sem).wait()
 
     def w_step(kind, j, k):
-        s = zflip(j)
-        if k == 0:
-            at = at_rows(kind, low_of(kind, 0, 1), span(kind, 1))
-            ref = w_all.at[s, at, :]
-            return [remote(ref, ref, w_s.at[kind, j, 0, 0], w_r.at[kind, j, 0, 0], dp=flip(p, 0))]
+        made = []
+        for c in range(1 if k == 0 else 2):
+            at = at_rows(kind, low_of(kind, c, k + 1), span(kind, k + 1))
+            ref = w_all.at[zflip(j), at, slice(None) if k == 0 else lanes[c]]
+            made.append(remote(ref, ref, w_s.at[kind, k], w_r.at[kind, j, k], dp=flip(p, orders[c][k])))
+        return made
+
+    def w_sources(kind, j):
         made = []
         for c in range(2):
-            at = at_rows(kind, low_of(kind, c, k + 1), span(kind, k + 1))
-            ref = w_all.at[s, at, lanes[c]]
-            made.append(remote(ref, ref, w_s.at[kind, j, k, c], w_r.at[kind, j, k, c], dp=flip(p, orders[c][k])))
+            ref = w_all.at[t, at_rows(kind, low_of(kind, c, nb), span(kind, nb)), lanes[c]]
+            made.append(remote(ref, ref, w_s.at[kind, nb], w_r.at[kind, j, nb], tensor=zflip(j)))
         return made
 
-    def w_sources(kind, j):
-        return [w_z(kind, j, c, t, zflip(j)) for c in range(2)]
-
     def w_wait(kind, j, k):
-        if k == halves[kind]:
-            copies = [w_z(kind, j, c, zflip(j), zflip(j)) for c in range(2)]
-        else:
-            copies = w_step(kind, j, k)
-        for copy in copies:
-            copy.wait_recv()
+        k_ = nb if k == halves[kind] else k
+        wait_for(w_all.at[0, pl.ds(0, span(kind, k + 1))], w_r.at[kind, j, k_])
 
     def w_forward(kind, j, k):
         w_wait(kind, j, k + 1)
         for copy in w_step(kind, j, k):
             copy.start()
 
-    def w_all_j(kind, k):
-        def go(j, _):
-            w_forward(kind, j, k)
-            return 0
-
-        lax.fori_loop(1, blocks, go, 0)
+    def w_top(kind, *js):
+        for j in js:
+            w_forward(kind, j, halves[kind] - 1)
+
+    def w_mid(kind, *js):
+        for k in range(halves[kind] - 2, 0, -1):
+            for j in js:
+                w_forward(kind, j, k)
+
+    def w_end(kind, *js):
+        for j in js:
+            w_forward(kind, j, 0)
 
     def r_step(kind, j, k):
         s = zflip(j)
-        buf = stage_bufs[k]
         base = sum(span(i, k + 1) for i in range(kind))
         made = []
-        for c in range(2):
+        for c in range(1 if k == 0 else 2):
+            low = low_of(kind, c, k)
             if k < halves[kind]:
-                low = low_of(kind, c, k) + (1 - bit_of(p, orders[c][k])) * span(kind, k + 1)
-            else:
-                low = low_of(kind, c, k)
+                low = low + (1 - bit_of(p, orders[c][k])) * span(kind, k + 1)
             which = slice(None) if k == 0 else lanes[c]
             made.append(
                 remote(
                     grad.at[s, at_rows(kind, low, span(kind, k + 1)), which],
-                    buf.at[j, pl.ds(base, span(kind, k + 1)), which],
-                    r_s.at[kind, j, k, c],
-                    r_r.at[kind, j, k, c],
+                    stage_bufs[k].at[j, pl.ds(base, span(kind, k + 1)), which],
+                    r_s.at[kind, k] if k < halves[kind] else x_s.at[kind, j, k],
+                    r_r.at[kind, j, k],
                     dp=flip(p, orders[c][k]),
                 )
             )
-            if k == 0:
-                break
         return made
 
     def r_start(kind, j, k):
@@ -229,10 +230,10 @@
         buf = stage_bufs[k]
         base = sum(span(i, k + 1) for i in range(kind))
         n = span(kind, k + 1)
-        for copy in r_step(kind, j, k):
-            if k >= halves[kind]:
-                copy.wait_send()
-            copy.wait_recv()
+        here = stage_bufs[k].at[j, pl.ds(base, n), :]
+        if k >= halves[kind]:
+            wait_for(here, x_s.at[kind, j, k])
+        wait_for(here, r_r.at[kind, j, k])
         piece = min(n, 128)
         for c in range(2):
             low = low_of(kind, c, k + 1)
@@ -257,8 +258,8 @@
                 remote(
                     grad.at[s, at, lanes[c]],
                     zbuf.at[j, pl.ds(base, span(kind, nb)), lanes[c]],
-                    r_s.at[kind, j, nb, c],
-                    r_r.at[kind, j, nb, c],
+                    r_s.at[kind, nb],
+                    r_r.at[kind, j, nb],
                     tensor=s,
                 )
             )
@@ -272,8 +273,7 @@
         base = sum(span(i, nb) for i in range(kind))
         n = span(kind, nb)
         for j in range(1, blocks):
-            for copy in r_z(kind, j):
-                copy.wait_recv()
+            wait_for(zbuf.at[j, pl.ds(base, n), :], r_r.at[kind, j, nb])
         for c in range(2):
             at = at_rows(kind, low_of(kind, c, nb), n)
             total = grad[t, at, lanes[c]].astype(F32)
@@ -282,13 +282,11 @@
             fin[at, lanes[c]] = total.astype(BF16)
 
     def a_step(kind, k):
-        if k == 0:
-            ref = fin.at[at_rows(kind, low_of(kind, 0, 1), span(kind, 1)), :]
-            return [remote(ref, ref, a_s.at[kind, 0, 0], a_r.at[kind, 0, 0], dp=flip(p, 0))]
         made = []
-        for c in range(2):
-            ref = fin.at[at_rows(kind, low_of(kind, c, k + 1), span(kind, k + 1)), lanes[c]]
-            made.append(remote(ref, ref, a_s.at[kind, k, c], a_r.at[kind, k, c], dp=flip(p, orders[c][k])))
+        for c in range(1 if k == 0 else 2):
+            at = at_rows(kind, low_of(kind, c, k + 1), span(kind, k + 1))
+            ref = fin.at[at, slice(None) if k == 0 else lanes[c]]
+            made.append(remote(ref, ref, a_s.at[kind, k], a_r.at[kind, k], dp=flip(p, orders[c][k])))
         return made
 
     def a_start(kind, k):
@@ -296,8 +294,7 @@
             copy.start()
 
     def a_wait(kind, k):
-        for copy in a_step(kind, k):
-            copy.wait_recv()
+        wait_for(fin.at[pl.ds(0, span(kind, k + 1)), :], a_r.at[kind, k])
 
     def r_middle(kind, j):
         for k in range(1, nb - 1):
@@ -308,26 +305,49 @@
         r_finish(kind, j, 0)
         r_start(kind, j, 1)
 
-    def r_last(kind, j, shard_known=None):
+    def r_last(kind, j):
         r_finish(kind, j, nb - 1)
-        if shard_known is None:
-            @pl.when(j > 0)
-            def _():
+        if isinstance(j, int):
+            if j > 0:
                 r_out(kind, j)
-        elif shard_known > 0:
-            r_out(kind, j)
-
-    def s_step(which, k):
-        total, got = ((gsum, grecv), (csum, crecv))[which]
-        dev = {"dp": flip(p, k)} if k < nb else {"tensor": flip(t, k - nb)}
-        return remote(total.at[k], got.at[k], s_s.at[which, k], s_r.at[which, k], **dev)
-
-    def s_next(which, k):
-        total, got = ((gsum, grecv), (csum, crecv))[which]
-        s_step(which, k).wait_recv()
-        total[k + 1] = total[k] + got[k]
-        if k + 1 < nb + 2:
-            s_step(which, k + 1).start()
+        else:
+            pl.when(j > 0)(lambda: r_out(kind, j))
+
+    def a_first(kind):
+        r_total(kind)
+        a_start(kind, halves[kind] - 1)
+
+    def a_mid(kind):
+        for k in range(halves[kind] - 2, 0, -1):
+            a_wait(kind, k + 1)
+            a_start(kind, k)
+
+    def a_end(kind):
+        a_wait(kind, 1)
+        a_start(kind, 0)
+
+    groups = bit_groups(nb)
+
+    def s_start(g):
+        bits = groups[g]
+        for r in range(1, 1 << len(bits)):
+            dp_, tensor_ = p, t
+            for i, b in enumerate(bits):
+                if r >> i & 1:
+                    dp_, tensor_ = (flip(dp_, b), tensor_) if b < nb else (dp_, flip(tensor_, b - nb))
+            dev = {"dp": dp_} if bits[0] < nb else {"tensor": tensor_}
+            remote(ssum.at[g], sgot.at[g, r - 1], s_s.at[g], s_r.at[g, r - 1], **dev).start()
+
+    def s_next(g):
+        n = (1 << len(groups[g])) - 1
+        for r in range(n):
+            wait_for(sgot.at[g, r], s_r.at[g, r])
+        v = ssum[g] + sgot[g, 0]
+        if n == 3:
+            v = v + (sgot[g, 1] + sgot[g, 2])
+        ssum[g + 1] = v
+        if g + 1 < len(groups):
+            s_start(g + 1)
 
     def local(src, dst_, i):
         return pltpu.make_async_copy(src, dst_, lsem.at[i])
@@ -342,6 +362,9 @@
     ]
     for copy in loads:
         copy.start()
+    frecv[...] = jnp.zeros_like(frecv)
+    brecv[...] = jnp.zeros_like(brecv)
+    halo[...] = jnp.zeros_like(halo)
     cb[0, pl.ds(0, 4), :] = conv_ref[...]
     cb[0, pl.ds(4, 1), :] = bias_ref[...]
     barrier = pltpu.get_barrier_semaphore()
@@ -352,17 +375,17 @@
     pl.semaphore_wait(barrier, nb + blocks - 1)
 
     def c_copy(j):
-        return remote(cb.at[0], cb.at[j], csem.at[0, j], csem.at[1, j], tensor=zflip(j))
-
-    hcopy = remote(dproj.at[0, pl.ds(rows - 16, 16), :], halo, zsem.at[0], zsem.at[1], tensor=partner)
+        return remote(cb.at[0], cb.at[j], c_s.at[0], c_r.at[j], tensor=zflip(j))
+
+    hcopy = remote(dproj.at[0, pl.ds(rows - 16, 16), :], halo, h_s.at[0], h_r.at[0], tensor=partner)
+    for j in range(1, blocks):
+        c_copy(j).start()
     loads[0].wait()
     for j in range(1, blocks):
         for copy in w_sources(IN, j):
             copy.start()
-    for j in range(1, blocks):
-        c_copy(j).start()
     loads[4].wait()
-    hcopy.start()
+    pl.when(t == 2)(hcopy.start)
     loads[1].wait()
     for j in range(1, blocks):
         for copy in w_sources(OUT, j):
@@ -413,7 +436,6 @@
     lax.fori_loop(0, nchunk, norm_rows, 0)
     loads[5].wait()
     spread(dproj.at[1])
-    w_all_j(IN, halves[IN] - 1)
 
     def dout_rows(r, _):
         at = pl.multiple_of(r * CHUNK, CHUNK)
@@ -425,11 +447,11 @@
         return 0
 
     lax.fori_loop(0, nchunk, dout_rows, 0)
-    hcopy.wait()
+    w_top(IN, 1)
+    pl.when(t == 3)(hcopy.wait_recv)
+    pl.when(t == 2)(hcopy.wait_send)
     hv = halo[...].astype(F32)
     lhs[pl.ds(rows, 16), :] = (hv * scale_of(hv) * g1_ref[...]).astype(BF16)
-    for j in range(1, blocks):
-        c_copy(j).wait()
 
     seg_id = lax.broadcasted_iota(jnp.int32, (SEGS, ch), 0)
     has_prev = jnp.where(t == 3, 1.0, 0.0).astype(F32)
@@ -440,6 +462,7 @@
 
         @pl.when(j > 0)
         def _():
+            c_copy(j).wait_recv()
             w_wait(IN, j, 0)
 
         def project(r, _):
@@ -453,14 +476,23 @@
 
         @pl.when(j == 0)
         def _():
-            for k in range(halves[IN] - 2, 0, -1):
-                w_all_j(IN, k)
+            w_top(IN, 2)
+            w_mid(IN, 1)
 
         @pl.when(j == 1)
         def _():
-            for kind in (OUT, FF):
-                for k in range(halves[kind] - 2, 0, -1):
-                    w_all_j(kind, k)
+            w_end(IN, 2)
+            w_mid(IN, 3)
+
+        @pl.when(j == 2)
+        def _():
+            w_end(IN, 3)
+            w_top(OUT, 1, 2, 3)
+
+        @pl.when(j == 3)
+        def _():
+            w_mid(OUT, 1, 2, 3)
+            w_mid(FF, 1)
 
         ph = dot(lhs[pl.ds(rows, 16), :], w_all[s_, pl.ds(o_in, d), ch:])
         for back in range(3):
@@ -491,45 +523,51 @@
         )
         ends[0, j] = s
         ends[1, j] = q_
+        fsend[j] = jnp.broadcast_to(forward_chain(j, jnp.zeros((1, ch), F32)), (8, ch))
+        pl.when(t == 2)(f_copy(j).start)
 
         @pl.when(j == 0)
         def _():
-            w_all_j(IN, 0)
-            w_all_j(OUT, halves[OUT] - 1)
-            w_all_j(FF, halves[FF] - 1)
-
-        @pl.when(j == 1)
-        def _():
-            w_all_j(OUT, 0)
-            w_all_j(FF, 0)
+            w_mid(IN, 2)
+            w_top(IN, 3)
+            w_end(IN, 1)
+
+        @pl.when(j == 2)
+        def _():
+            w_top(FF, 1)
+
+        @pl.when(j == 3)
+        def _():
+            w_end(OUT, 1, 2, 3)
+            w_top(FF, 2)
 
         return 0
 
-    lax.fori_loop(0, blocks, forward_block, 0)
-
-    def forward_chain(start):
+    def forward_chain(j, start):
         run = start
         for seg in range(SEGS):
-            st[:, pl.ds(seg, 1), :] = run
-            run = ends[0, :, pl.ds(seg, 1), :] + ends[1, :, pl.ds(seg, 1), :] * run
+            st[j, pl.ds(seg, 1), :] = run
+            run = ends[0, j, pl.ds(seg, 1), :] + ends[1, j, pl.ds(seg, 1), :] * run
         return run
 
-    fsend[...] = jnp.broadcast_to(forward_chain(jnp.zeros((blocks, 1, ch), F32)), (blocks, 8, ch))
-    fcopies = [
-        remote(fsend.at[j], frecv.at[j ^ 1], zsem.at[2 + 2 * j], zsem.at[3 + 2 * j], tensor=partner)
-        for j in range(blocks)
-    ]
-    waits = [
-        remote(fsend.at[j ^ 1], frecv.at[j], zsem.at[2 + 2 * (j ^ 1)], zsem.at[3 + 2 * (j ^ 1)], tensor=partner)
-        for j in range(blocks)
-    ]
-    for copy in fcopies:
-        copy.start()
-    for j in range(blocks):
-        waits[j].wait_recv()
-    forward_chain(frecv[:, pl.ds(0, 1), :] * has_prev)
-
-    def forward_fix(b, _):
+    def f_copy(j):
+        there = flip(j, 0)
+        return remote(fsend.at[j], frecv.at[there], f_s.at[0], f_r.at[there], tensor=partner)
+
+    lax.fori_loop(0, blocks, forward_block, 0)
+    w_mid(FF, 2)
+    w_top(FF, 3)
+    w_end(FF, 1)
+
+    def forward_fix(i, _):
+        b = flip(i, 0)
+
+        @pl.when(t == 3)
+        def _():
+            wait_for(frecv.at[b], f_r.at[b])
+
+        forward_chain(b, frecv[b, pl.ds(0, 1), :] * has_prev)
+
         def step8(i, s):
             for q in range(8):
                 at = pl.multiple_of((i * 8 + q) * SEGS, SEGS)
@@ -587,17 +625,26 @@
             bufa[pl.ds(at, CHUNK), :] += dot(av, wd)
             bufc[pl.ds(at, CHUNK), :] += dot_t(dv, wu)
 
-            @pl.when((r == 0) & (j > 0))
+            @pl.when((r == 0) & (j == 0))
+            def _():
+                w_end(FF, 2)
+                w_mid(FF, 3)
+
+            @pl.when((r == 0) & (j == 1))
+            def _():
+                w_end(FF, 3)
+
+            @pl.when((r == 2) & (j > 0))
             def _():
                 r_first(FF, j - 1)
 
-            @pl.when((r == 1) & (j > 1))
+            @pl.when((r == 3) & (j > 1))
             def _():
-                r_last(FF, j - 2)
-
-            @pl.when((r == 2) & (j > 0))
+                r_middle(FF, j - 2)
+
+            @pl.when((r == 3) & (j > 2))
             def _():
-                r_middle(FF, j - 1)
+                r_last(FF, j - 3)
 
             return 0
 
@@ -631,13 +678,14 @@
         return gain
 
     gain2 = lax.fori_loop(0, nchunk, second_back, jnp.zeros((1, d), F32))
-    gsum[0] = jnp.zeros((8, d), F32)
-    gsum[0, pl.ds(1, 1), :] = gain2
+    ssum[0] = jnp.zeros((16, d), F32)
+    ssum[0, pl.ds(1, 1), :] = gain2
     gather(dproj.at[0])
     res_copy = pltpu.make_async_copy(dproj.at[0], res_hbm, lsem.at[6])
     res_copy.start()
-    r_first(FF, blocks - 1)
-    r_last(FF, blocks - 2, blocks - 2)
+    r_middle(FF, 2)
+    r_first(FF, 3)
+    r_last(FF, 1)
 
     def backward_block(i, _):
         j = blocks - 1 - i
@@ -656,10 +704,6 @@
             ).astype(BF16)
         r_start(OUT, j, 0)
 
-        @pl.when(i == 0)
-        def _():
-            r_middle(FF, blocks - 1)
-
         def one(step, w, q_):
             at = pl.multiple_of(step * SEGS, SEGS)
             a = 1.0 - upd[j, pl.ds(at, SEGS), :]
@@ -683,10 +727,21 @@
             bends[2 * step + 1, j] = c
         bends[6, j] = w
         bends[7, j] = q_
+        bsend[j, pl.ds(0, 1), :] = backward_chain(j, jnp.zeros((1, ch), F32))
+        for step in range(3):
+            bsend[j, pl.ds(step + 1, 1), :] = upd[j, pl.ds(step * SEGS, 1), :] * (
+                bends[2 * step + 1, j, pl.ds(0, 1), :]
+                + bends[2 * step, j, pl.ds(0, 1), :] * ends[0, j, pl.ds(0, 1), :]
+            )
+        pl.when(t == 3)(b_copy(j).start)
 
         @pl.when(i == 1)
         def _():
-            r_last(FF, blocks - 1, blocks - 1)
+            r_last(FF, 2)
+
+        @pl.when(i == 2)
+        def _():
+            r_middle(FF, 3)
 
         @pl.when(i > 0)
         def _():
@@ -702,43 +757,31 @@
 
         return 0
 
-    lax.fori_loop(0, blocks, backward_block, 0)
-
-    def backward_chain(start):
+    def backward_chain(j, start):
         run = start
         for seg in range(SEGS - 1, -1, -1):
-            ends[0, :, pl.ds(seg, 1), :] = run
-            run = bends[6, :, pl.ds(seg, 1), :] + bends[7, :, pl.ds(seg, 1), :] * run
+            ends[0, j, pl.ds(seg, 1), :] = run
+            run = bends[6, j, pl.ds(seg, 1), :] + bends[7, j, pl.ds(seg, 1), :] * run
         return run
 
-    bsend[:, pl.ds(0, 1), :] = backward_chain(jnp.zeros((blocks, 1, ch), F32))
-    for step in range(3):
-        bsend[:, pl.ds(step + 1, 1), :] = upd[:, pl.ds(step * SEGS, 1), :] * (
-            bends[2 * step + 1, :, pl.ds(0, 1), :]
-            + bends[2 * step, :, pl.ds(0, 1), :] * ends[0, :, pl.ds(0, 1), :]
-        )
-    bcopies = [
-        remote(bsend.at[j], brecv.at[j ^ 1], zsem.at[10 + 2 * j], zsem.at[11 + 2 * j], tensor=partner)
-        for j in range(blocks)
-    ]
-    bwaits = [
-        remote(bsend.at[j ^ 1], brecv.at[j], zsem.at[10 + 2 * (j ^ 1)], zsem.at[11 + 2 * (j ^ 1)], tensor=partner)
-        for j in range(blocks)
-    ]
-    for copy in bcopies:
-        copy.start()
-    r_first(OUT, 0)
-    r_middle(OUT, 1)
-    r_last(OUT, 2, 2)
-    for j in range(blocks):
-        bwaits[j].wait_recv()
-    backward_chain(brecv[:, pl.ds(0, 1), :] * has_next)
-    csum[0] = jnp.zeros((blocks, 8, ch), F32)
+    def b_copy(j):
+        there = flip(j, 0)
+        return remote(bsend.at[j], brecv.at[there], b_s.at[0], b_r.at[there], tensor=partner)
+
+    lax.fori_loop(0, blocks, backward_block, 0)
+
+    r_last(FF, 3)
     res_copy.wait()
 
     def backward_fix(i, _):
         j = blocks - 1 - i
         s_ = zflip(j)
+
+        @pl.when(t == 2)
+        def _():
+            wait_for(brecv.at[j], b_r.at[j])
+
+        backward_chain(j, brecv[j, pl.ds(0, 1), :] * has_next)
         w = ends[0, j]
         after = []
         for step in range(3):
@@ -776,42 +819,25 @@
         window = [cand[j, pl.ds((steps + 2 - n) * SEGS, SEGS), :] for n in range(3)]
         out = lax.fori_loop(0, steps // 2, pair, (w, *after, *window, zero, zero, zero, zero, zero))
         for n in range(5):
-            csum[0, s_, pl.ds(n, 1), :] = jnp.sum(out[7 + n], axis=0, keepdims=True)
+            at = 2 + 2 * n + bit_of(s_, 1)
+            ssum[0, pl.ds(at, 1), pl.ds(pl.multiple_of(bit_of(s_, 0) * ch, LANES), ch)] = jnp.sum(
+                out[7 + n], axis=0, keepdims=True
+            )
 
         @pl.when(i == 0)
         def _():
+            r_first(OUT, 0)
+            r_middle(OUT, 1)
+            r_last(OUT, 2)
+
+        @pl.when(i == 1)
+        def _():
             r_middle(OUT, 0)
-            r_last(OUT, 1, 1)
-            r_total(FF)
-            a_start(FF, halves[FF] - 1)
-
-        @pl.when(i == 1)
-        def _():
-            r_last(OUT, 0, 0)
-            for k in range(halves[FF] - 2, 0, -1):
-                a_wait(FF, k + 1)
-                a_start(FF, k)
+            r_last(OUT, 1)
 
         @pl.when(i == 2)
         def _():
-            a_wait(FF, 1)
-            a_start(FF, 0)
-            r_total(OUT)
-            a_start(OUT, halves[OUT] - 1)
-
-        @pl.when(i == 3)
-        def _():
-            for k in range(halves[OUT] - 2, 0, -1):
-                a_wait(OUT, k + 1)
-                a_start(OUT, k)
-
-        @pl.when(i > 0)
-        def _():
-            r_first(IN, j + 1)
-
-        @pl.when(i > 1)
-        def _():
-            r_last(IN, j + 2)
+            r_last(OUT, 0)
 
         def first_grad(r, _):
             at = pl.multiple_of(r * CHUNK, CHUNK)
@@ -821,14 +847,31 @@
         lax.fori_loop(0, d // CHUNK, first_grad, 0)
         r_start(IN, j, 0)
 
+
         @pl.when(i > 0)
         def _():
-            r_middle(IN, j + 1)
+            r_first(IN, j + 1)
+
+        @pl.when(i > 1)
+        def _():
+            r_middle(IN, j + 2)
+
+        @pl.when(i > 2)
+        def _():
+            r_last(IN, j + 3)
+
+        @pl.when(i == 2)
+        def _():
+            a_first(FF)
+
+        @pl.when(i == 3)
+        def _():
+            a_mid(FF)
+            a_first(OUT)
 
         return 0
 
     lax.fori_loop(0, blocks, backward_fix, 0)
-    s_step(1, 0).start()
 
     def first_back(r):
         at = r * CHUNK
@@ -838,17 +881,15 @@
         bufc[pl.ds(at, CHUNK), :] = v
 
     first_back(0)
+    r_last(IN, 2)
+    first_back(1)
     r_first(IN, 0)
-    r_last(IN, 1, 1)
-    s_next(1, 0)
-    first_back(1)
-    a_wait(OUT, 1)
-    a_start(OUT, 0)
-    s_next(1, 1)
+    r_middle(IN, 1)
+    a_end(FF)
     first_back(2)
-    r_middle(IN, 0)
-    s_next(1, 2)
-    for r in range(3, nchunk):
+    a_mid(OUT)
+    first_back(3)
+    for r in range(4, nchunk):
         first_back(r)
 
     def first_norm_back(r, gain):
@@ -862,65 +903,88 @@
         put_perm(at, mid[pl.ds(at, CHUNK), :] + dv)
         return gain
 
-    gsum[0, pl.ds(0, 1), :] = lax.fori_loop(0, nchunk, first_norm_back, jnp.zeros((1, d), F32))
-    s_step(0, 0).start()
-    r_last(IN, 0, 0)
-    r_total(IN)
-    a_start(IN, halves[IN] - 1)
-    for k in range(3, nb + 2):
-        s_next(1, k)
+    ssum[0, pl.ds(0, 1), :] = lax.fori_loop(0, nchunk, first_norm_back, jnp.zeros((1, d), F32))
+    s_start(0)
+    r_middle(IN, 0)
+    r_last(IN, 1)
     gather(mid)
     gx_copy = pltpu.make_async_copy(mid, gx_hbm, lsem.at[7])
     gx_copy.start()
-    chan_ref[...] = csum[nb + 2, t]
-    s_next(0, 0)
-    for k in range(halves[IN] - 2, 0, -1):
-        a_wait(IN, k + 1)
-        a_start(IN, k)
+    a_end(OUT)
+    s_next(0)
+    r_last(IN, 0)
+    a_first(IN)
+    for g in range(1, len(groups) - 1):
+        s_next(g)
+    a_mid(IN)
+    a_end(IN)
+    s_next(len(groups) - 1)
+    gains_ref[...] = ssum[len(groups), pl.ds(0, 8), :]
+    for n in range(5):
+        at = 2 + 2 * n + bit_of(t, 1)
+        chan_ref[pl.ds(n, 1), :] = ssum[
+            len(groups), pl.ds(at, 1), pl.ds(pl.multiple_of(bit_of(t, 0) * ch, LANES), ch)
+        ]
     a_wait(FF, 0)
-    gup_ref[...] = fin[pl.ds(o_up, d), :].astype(F32)
-    gdown_ref[...] = fin[pl.ds(o_down, d), :].astype(F32).T
-    s_next(0, 1)
     a_wait(OUT, 0)
-    gout_ref[:, :half_d] = fin[pl.ds(o_out, ch), :ch].astype(F32).T
-    gout_ref[:, half_d:] = fin[pl.ds(o_out, ch), ch:].astype(F32).T
-    a_wait(IN, 1)
-    a_start(IN, 0)
-    for k in range(2, nb + 2):
-        s_next(0, k)
-    gains_ref[...] = gsum[nb + 2]
     a_wait(IN, 0)
-    gin_ref[...] = fin[pl.ds(o_in, d), :].astype(F32)
 
     gx_copy.wait()
-    for copy in fcopies + bcopies:
-        copy.wait_send()
+    wait_for(cb.at[pl.ds(0, blocks - 1)], c_s.at[0])
+    pl.when(t == 2)(lambda: wait_for(fsend, f_s.at[0]))
+    pl.when(t == 3)(lambda: wait_for(bsend, b_s.at[0]))
     for kind in (IN, OUT, FF):
-        def drain(j, _):
-            for copy in w_sources(kind, j):
-                copy.wait_send()
-            for k in range(halves[kind]):
-                for copy in w_step(kind, j, k):
-                    copy.wait_send()
-            for copy in r_z(kind, j):
-                copy.wait_send()
-            return 0
-
-        lax.fori_loop(1, blocks, drain, 0)
-
-        def drain_halving(j, _):
-            for k in range(halves[kind]):
-                for copy in r_step(kind, j, k):
-                    copy.wait_send()
-            return 0
-
-        lax.fori_loop(0, blocks, drain_halving, 0)
         for k in range(halves[kind]):
-            for copy in a_step(kind, k):
-                copy.wait_send()
-    for k in range(nb + 2):
-        s_step(0, k).wait_send()
-        s_step(1, k).wait_send()
+            n = span(kind, k + 1)
+            wait_for(w_all.at[0, pl.ds(0, (blocks - 1) * n), :], w_s.at[kind, k])
+            wait_for(grad.at[pl.ds(0, 2), pl.ds(0, blocks // 2 * n), :], r_s.at[kind, k])
+            wait_for(fin.at[pl.ds(0, n), :], a_s.at[kind, k])
+        n = span(kind, nb)
+        wait_for(w_all.at[0, pl.ds(0, (blocks - 1) * n), :], w_s.at[kind, nb])
+        wait_for(w_all.at[0, pl.ds(0, (blocks - 1) * n), :], r_s.at[kind, nb])
+    for g in range(len(groups)):
+        wait_for(sgot.at[g, pl.ds(0, (1 << len(groups[g])) - 1)], s_s.at[g])
+
+
+def finish_kernel(dims, gains, chan, res, gx, fin, res_out, gx_out, gin_o, gout_o, gup_o, gdown_o, gnorm, gmlp, taps, gbias,
+                  rbuf, gbuf, fbuf, gin, gout, gup, gdown, sem):
+    rows, d, ch, ff = dims
+    cuts = ((d + ch, ff), (d + ch + ff, ff), (d, ch), (0, d))
+    parts = [pltpu.make_async_copy(fin.at[pl.ds(a, n)], fbuf.at[pl.ds(a, n)], sem.at[i]) for i, (a, n) in enumerate(cuts)]
+    ins = [pltpu.make_async_copy(gx, gbuf, sem.at[4]), pltpu.make_async_copy(res, rbuf, sem.at[5])]
+    for copy in parts + ins:
+        copy.start()
+    outs = []
+
+    def put(src, dst):
+        copy = pltpu.make_async_copy(src, dst, sem.at[6 + len(outs)])
+        copy.start()
+        outs.append(copy)
+
+    gnorm[...] = gains[pl.ds(0, 1), :]
+    gmlp[...] = gains[pl.ds(1, 1), :]
+    taps[...] = chan[pl.ds(0, 4), :]
+    gbias[...] = chan[pl.ds(4, 1), :]
+    parts[0].wait()
+    gup[...] = fbuf[pl.ds(d + ch, d), :].astype(F32)
+    put(gup, gup_o)
+    parts[1].wait()
+    gdown[...] = fbuf[pl.ds(d + ch + ff, d), :].astype(F32).T
+    put(gdown, gdown_o)
+    ins[0].wait()
+    put(gbuf, gx_out)
+    ins[1].wait()
+    put(rbuf, res_out)
+    parts[2].wait()
+    gout[:, : d // 2] = fbuf[pl.ds(d, ch), :ch].astype(F32).T
+    gout[:, d // 2 :] = fbuf[pl.ds(d, ch), ch:].astype(F32).T
+    put(gout, gout_o)
+    parts[3].wait()
+    gin[:, 0, :] = fbuf[pl.ds(0, d), :ch].astype(F32)
+    gin[:, 1, :] = fbuf[pl.ds(0, d), ch:].astype(F32)
+    put(gin, gin_o)
+    for copy in outs:
+        copy.wait()
 
 
 def per_device(
@@ -952,28 +1016,25 @@
     def span_all(k):
         return sum(r >> min(k, h) for r, h in zip(sizes, halves))
 
+    ngroups = len(bit_groups(nb))
     vm = pl.BlockSpec(memory_space=pltpu.VMEM)
     sm = pl.BlockSpec(memory_space=pltpu.SMEM)
     hb = pl.BlockSpec(memory_space=pl.ANY)
     dma = pltpu.SemaphoreType.DMA
-    result, grad_inputs, gin, gout, gup, gdown, gains, chan = pl.pallas_call(
+    res, gx, fin, gains, chan = pl.pallas_call(
         functools.partial(block_kernel, (rows, d, blocks, ch, ff, nb)),
         out_shape=(
             jax.ShapeDtypeStruct((rows, d), BF16),
             jax.ShapeDtypeStruct((rows, d), F32),
-            jax.ShapeDtypeStruct((d, 2 * ch), F32),
-            jax.ShapeDtypeStruct((ch, d), F32),
-            jax.ShapeDtypeStruct((d, ff), F32),
-            jax.ShapeDtypeStruct((ff, d), F32),
+            jax.ShapeDtypeStruct((total, d), BF16),
             jax.ShapeDtypeStruct((8, d), F32),
             jax.ShapeDtypeStruct((8, ch), F32),
         ),
         in_specs=[sm, sm, hb, hb, vm, vm, vm, vm, hb, hb, hb, hb],
-        out_specs=(hb, hb) + (vm,) * 6,
+        out_specs=(hb, hb) + (vm,) * 3,
         scratch_shapes=[
             pltpu.VMEM((blocks, total, d), BF16),
             pltpu.VMEM((blocks, total, d), BF16),
-            pltpu.VMEM((total, d), BF16),
             pltpu.VMEM((rows, d), BF16),
             pltpu.VMEM((blocks, rows + 3 * SEGS, ch), F32),
             pltpu.VMEM((blocks, rows, ch), F32),
@@ -998,21 +1059,26 @@
             pltpu.VMEM((blocks, 8, ch), F32),
             pltpu.VMEM((blocks, 8, ch), F32),
             pltpu.VMEM((blocks, span_all(nb), d), BF16),
-            pltpu.VMEM((nb + 3, 8, d), F32),
-            pltpu.VMEM((nb + 2, 8, d), F32),
-            pltpu.VMEM((nb + 3, blocks, 8, ch), F32),
-            pltpu.VMEM((nb + 2, blocks, 8, ch), F32),
+            pltpu.VMEM((ngroups + 1, 16, d), F32),
+            pltpu.VMEM((ngroups, 3, 16, d), F32),
             dma((8,)),
-            dma((2, blocks)),
-            dma((18,)),
-            dma((3, blocks, nb + 1, 2)),
-            dma((3, blocks, nb + 1, 2)),
-            dma((3, blocks, nb + 1, 2)),
-            dma((3, blocks, nb + 1, 2)),
-            dma((3, nb, 2)),
-            dma((3, nb, 2)),
-            dma((2, nb + 2)),
-            dma((2, nb + 2)),
+            dma((1,)),
+            dma((blocks,)),
+            dma((1,)),
+            dma((blocks,)),
+            dma((1,)),
+            dma((blocks,)),
+            dma((1,)),
+            dma((1,)),
+            dma((3, nb + 1)),
+            dma((3, blocks, nb + 1)),
+            dma((3, nb + 1)),
+            dma((3, blocks, nb + 1)),
+            dma((3, blocks, nb)),
+            dma((3, nb)),
+            dma((3, nb)),
+            dma((ngroups,)),
+            dma((ngroups, 3)),
         ]
         + [pltpu.VMEM((blocks, span_all(k + 1), d), BF16) for k in range(nb)],
         compiler_params=pltpu.CompilerParams(
@@ -1033,18 +1099,36 @@
         up_weight,
         down_weight,
     )
-    return (
-        result,
-        grad_inputs,
-        gains[0],
-        gin.reshape(d, 2, ch),
-        chan[:4],
-        chan[4],
-        gout,
-        gains[1],
-        gup,
-        gdown,
-    )
+    result, grad_inputs, gin, gout, gup, gdown, gnorm, gmlp, taps, gbias = pl.pallas_call(
+        functools.partial(finish_kernel, (rows, d, ch, ff)),
+        out_shape=(
+            jax.ShapeDtypeStruct((rows, d), BF16),
+            jax.ShapeDtypeStruct((rows, d), F32),
+            jax.ShapeDtypeStruct((d, 2, ch), F32),
+            jax.ShapeDtypeStruct((ch, d), F32),
+            jax.ShapeDtypeStruct((d, ff), F32),
+            jax.ShapeDtypeStruct((ff, d), F32),
+            jax.ShapeDtypeStruct((1, d), F32),
+            jax.ShapeDtypeStruct((1, d), F32),
+            jax.ShapeDtypeStruct((4, ch), F32),
+            jax.ShapeDtypeStruct((1, ch), F32),
+        ),
+        in_specs=[vm, vm, hb, hb, hb],
+        out_specs=(hb,) * 6 + (vm,) * 4,
+        scratch_shapes=[
+            pltpu.VMEM((rows, d), BF16),
+            pltpu.VMEM((rows, d), F32),
+            pltpu.VMEM((total, d), BF16),
+            pltpu.VMEM((d, 2, ch), F32),
+            pltpu.VMEM((ch, d), F32),
+            pltpu.VMEM((d, ff), F32),
+            pltpu.VMEM((ff, d), F32),
+            dma((12,)),
+        ],
+        compiler_params=pltpu.CompilerParams(vmem_limit_bytes=67043328),
+        name="finish",
+    )(gains, chan, res, gx, fin)
+    return (result, grad_inputs, gnorm[0], gin, taps, gbias[0], gout, gmlp[0], gup, gdown)
 
 
 def solution(mesh):

time: 177 us -> 120 us (0.68)
  Pallas kernels: 161 us -> 116 us
  local copies, waits for them, and re-layouts: 14 us -> 1.92 us
    pallas_call x1, Pallas kernels: 161 us -> 110 us  [per_device(): pl.pallas_call(functools.partial(block_kernel, (rows, d, blocks, ch, ff,...]
    pallas_call x0 -> x1, Pallas kernels: none -> 6.04 us  [per_device(): pl.pallas_call(functools.partial(finish_kernel, (rows, d, ch, ff)), out_s...]
    unnamed x16 -> x1, local copies, waits for them, and re-layouts: 7.01 us -> 1.92 us
    slice x3 -> x0, local copies, waits for them, and re-layouts: 4.02 us -> none  [the longest x1 1.38 us: per_device(): gains[1]]
    reshape x1 -> x0, local copies, waits for them, and re-layouts: 3 us -> none  [per_device(): gin.reshape(d, 2, ch)]
where the time goes in v3:
time: 120 us; the launch traced here: 119 us
  Pallas kernels  116 us (97%)
  local copies, waits for them, and re-layouts  1.92 us (2%)
  between operations  1.3 us (1%)
    pallas_call x1, Pallas kernels, per_device(): pl.pallas_call(functools.partial(block_kernel, (rows, d, blocks, ch, ff,...  110 us
    pallas_call x1, Pallas kernels, per_device(): pl.pallas_call(functools.partial(finish_kernel, (rows, d, ch, ff)), out_s...  6.04 us

profile of v3, /device:TPU:0, one launch (start us, length us, event | category | flops | bytes accessed | tf_op | source)
XLA Modules:
  0.0 119.2 jit_solution(15621270448257662038)
XLA Ops:
  1.3 1.9 %copy.22 = bf16[64,8,2,256]{3,1,2,0:T(8,128)(2,1)} copy(bf16[64,8,2,256]{3,2,1,0:T(2,128)(2,1)} %bitcast.9) | data formatting | bytes 1048576
  3.2 109.9 %block.1 = (bf16[1024,512]{1,0:T(8,128)(2,1)}, f32[1024,512]{1,0:T(8,128)}, bf16[1792,512]{1,0:T(8,128)(2,1)}, f32[8,512]{1,0:T(8,128)}, f32[8,256]{1,0:T(8,128)}) custom-call(s32[2]{0:T(128)} %short_ref.1, s32[1]{0:T(128)S(6)} %copy.23.long_ref, bf16[1024,512]{1,0:T(8,128)(2,1)} %x_hbm.1, bf16[1024,512]{1,0:T(8,128)(2,1)} %cot_hbm.1, f32[1,512]{1,0:T(1,128)} %bitcast.10, ...), custom_call_target="tpu_custom_call" | custom-call | tf_op jit(solution)/shard_map/block/pallas_call | solution.py:1024
  113.2 6.0 %finish.1 = (bf16[1024,512]{1,0:T(8,128)(2,1)}, f32[1024,512]{1,0:T(8,128)}, f32[512,2,256]{2,1,0:T(2,128)}, f32[256,512]{1,0:T(8,128)}, f32[512,512]{1,0:T(8,12...) custom-call(f32[8,512]{1,0:T(8,128)} %get-tuple-element.25.gains, ...), custom_call_target="tpu_custom_call" | custom-call | tf_op jit(solution)/shard_map/finish/pallas_call | solution.py:1102

commit v4 on v3

--- a/solution.py
+++ b/solution.py
@@ -354,11 +354,11 @@
 
     loads = [
         local(win_hbm, w_all.at[t, pl.ds(o_in, d), :], 0),
-        local(wout_hbm, w_all.at[t, pl.ds(o_out, ch), :], 1),
-        local(wup_hbm, w_all.at[t, pl.ds(o_up, ff), :], 2),
-        local(wdown_hbm, w_all.at[t, pl.ds(o_down, ff), :], 3),
-        local(x_hbm, dproj.at[0], 4),
-        local(cot_hbm, dproj.at[1], 5),
+        local(x_hbm, dproj.at[0], 1),
+        local(cot_hbm, dproj.at[1], 2),
+        local(wout_hbm, w_all.at[t, pl.ds(o_out, ch), :], 3),
+        local(wup_hbm, w_all.at[t, pl.ds(o_up, ff), :], 4),
+        local(wdown_hbm, w_all.at[t, pl.ds(o_down, ff), :], 5),
     ]
     for copy in loads:
         copy.start()
@@ -377,24 +377,15 @@
     def c_copy(j):
         return remote(cb.at[0], cb.at[j], c_s.at[0], c_r.at[j], tensor=zflip(j))
 
-    hcopy = remote(dproj.at[0, pl.ds(rows - 16, 16), :], halo, h_s.at[0], h_r.at[0], tensor=partner)
+    hcopy = remote(x_hbm.at[pl.ds(rows - 16, 16), :], halo, h_s.at[0], h_r.at[0], tensor=partner)
+    pl.when(t == 2)(hcopy.start)
     for j in range(1, blocks):
         c_copy(j).start()
     loads[0].wait()
     for j in range(1, blocks):
         for copy in w_sources(IN, j):
             copy.start()
-    loads[4].wait()
-    pl.when(t == 2)(hcopy.start)
     loads[1].wait()
-    for j in range(1, blocks):
-        for copy in w_sources(OUT, j):
-            copy.start()
-    loads[2].wait()
-    loads[3].wait()
-    for j in range(1, blocks):
-        for copy in w_sources(FF, j):
-            copy.start()
 
     nlane = d // LANES
 
@@ -434,7 +425,7 @@
         return 0
 
     lax.fori_loop(0, nchunk, norm_rows, 0)
-    loads[5].wait()
+    loads[2].wait()
     spread(dproj.at[1])
 
     def dout_rows(r, _):
@@ -447,18 +438,19 @@
         return 0
 
     lax.fori_loop(0, nchunk, dout_rows, 0)
-    w_top(IN, 1)
-    pl.when(t == 3)(hcopy.wait_recv)
-    pl.when(t == 2)(hcopy.wait_send)
-    hv = halo[...].astype(F32)
-    lhs[pl.ds(rows, 16), :] = (hv * scale_of(hv) * g1_ref[...]).astype(BF16)
-
     seg_id = lax.broadcasted_iota(jnp.int32, (SEGS, ch), 0)
     has_prev = jnp.where(t == 3, 1.0, 0.0).astype(F32)
     has_next = jnp.where(t == 2, 1.0, 0.0).astype(F32)
 
     def forward_block(j, _):
         s_ = zflip(j)
+
+        @pl.when(j == 1)
+        def _():
+            w_top(IN, 3)
+            w_mid(IN, 2)
+            w_end(IN, 1)
+            w_mid(IN, 3)
 
         @pl.when(j > 0)
         def _():
@@ -470,29 +462,32 @@
             v = dot(lhs[pl.ds(at, CHUNK), :], w_all[s_, pl.ds(o_in, d), :])
             bufa[pl.ds(at, CHUNK), :ch] = v[:, :ch]
             cand[j, pl.ds(at + 3 * SEGS, CHUNK), :] = v[:, ch:]
+
+            @pl.when((j == 0) & (r == 1))
+            def _():
+                w_top(IN, 1)
+
             return 0
 
         lax.fori_loop(0, nchunk, project, 0)
 
         @pl.when(j == 0)
         def _():
-            w_top(IN, 2)
-            w_mid(IN, 1)
+            pl.when(t == 3)(hcopy.wait_recv)
+            hv = halo[...].astype(F32)
+            lhs[pl.ds(rows, 16), :] = (hv * scale_of(hv) * g1_ref[...]).astype(BF16)
 
         @pl.when(j == 1)
         def _():
             w_end(IN, 2)
-            w_mid(IN, 3)
 
         @pl.when(j == 2)
         def _():
             w_end(IN, 3)
-            w_top(OUT, 1, 2, 3)
 
         @pl.when(j == 3)
         def _():
-            w_mid(OUT, 1, 2, 3)
-            w_mid(FF, 1)
+            w_top(FF, 2)
 
         ph = dot(lhs[pl.ds(rows, 16), :], w_all[s_, pl.ds(o_in, d), ch:])
         for back in range(3):
@@ -518,9 +513,15 @@
                 q_ = a * q_
             return s, q_
 
-        s, q_ = lax.fori_loop(
-            0, steps // 4, step4, (jnp.zeros((SEGS, ch), F32), jnp.ones((SEGS, ch), F32))
+        half = lax.fori_loop(
+            0, steps // 8, step4, (jnp.zeros((SEGS, ch), F32), jnp.ones((SEGS, ch), F32))
         )
+
+        @pl.when(j == 0)
+        def _():
+            w_top(IN, 2)
+
+        s, q_ = lax.fori_loop(steps // 8, steps // 4, step4, half)
         ends[0, j] = s
         ends[1, j] = q_
         fsend[j] = jnp.broadcast_to(forward_chain(j, jnp.zeros((1, ch), F32)), (8, ch))
@@ -528,18 +529,21 @@
 
         @pl.when(j == 0)
         def _():
-            w_mid(IN, 2)
-            w_top(IN, 3)
-            w_end(IN, 1)
+            w_mid(IN, 1)
+            for i in range(3, 6):
+                loads[i].wait()
+            for kind in (OUT, FF):
+                for i in (2, 3, 1):
+                    for copy in w_sources(kind, i):
+                        copy.start()
+
+        @pl.when(j == 1)
+        def _():
+            w_top(OUT, 1, 2, 3)
 
         @pl.when(j == 2)
         def _():
-            w_top(FF, 1)
-
-        @pl.when(j == 3)
-        def _():
-            w_end(OUT, 1, 2, 3)
-            w_top(FF, 2)
+            w_mid(OUT, 1, 2, 3)
 
         return 0
 
@@ -555,9 +559,7 @@
         return remote(fsend.at[j], frecv.at[there], f_s.at[0], f_r.at[there], tensor=partner)
 
     lax.fori_loop(0, blocks, forward_block, 0)
-    w_mid(FF, 2)
     w_top(FF, 3)
-    w_end(FF, 1)
 
     def forward_fix(i, _):
         b = flip(i, 0)
@@ -577,9 +579,15 @@
             return s
 
         lax.fori_loop(0, steps // 8, step8, st[b, pl.ds(0, SEGS), :])
+
+        @pl.when(i == 0)
+        def _():
+            w_end(OUT, 1, 2, 3)
+
         return 0
 
     lax.fori_loop(0, blocks, forward_fix, 0)
+    w_mid(FF, 2)
     for j in range(1, blocks):
         w_wait(OUT, j, 0)
     shards = [zflip(j) for j in range(blocks)]
@@ -601,12 +609,17 @@
 
     lax.fori_loop(0, nchunk, second_rows, 0)
 
+    w_mid(FF, 3)
     act, din = dproj.at[1], dproj.at[2]
 
-    def ff_block(j, _):
+    def ff_place(i):
+        return lax.div(i + 3, 4) * (1 + lax.rem(i, 3))
+
+    def ff_block(i, _):
+        j, before, earlier = ff_place(i), ff_place(i - 1), ff_place(i - 2)
         s_ = zflip(j)
 
-        @pl.when(j > 0)
+        @pl.when(i > 0)
         def _():
             w_wait(FF, j, 0)
 
@@ -625,26 +638,33 @@
             bufa[pl.ds(at, CHUNK), :] += dot(av, wd)
             bufc[pl.ds(at, CHUNK), :] += dot_t(dv, wu)
 
-            @pl.when((r == 0) & (j == 0))
+            @pl.when((r == 1) & (i == 0))
             def _():
                 w_end(FF, 2)
-                w_mid(FF, 3)
-
-            @pl.when((r == 0) & (j == 1))
+
+            @pl.when((r == 2) & (i == 0))
+            def _():
+                w_top(FF, 1)
+
+            @pl.when((r == 3) & (i == 0))
             def _():
                 w_end(FF, 3)
 
-            @pl.when((r == 2) & (j > 0))
+            @pl.when((r == 0) & (i == 1))
             def _():
-                r_first(FF, j - 1)
-
-            @pl.when((r == 3) & (j > 1))
+                w_mid(FF, 1)
+
+            @pl.when((r == 1) & (i == 2))
             def _():
-                r_middle(FF, j - 2)
-
-            @pl.when((r == 3) & (j > 2))
+                w_end(FF, 1)
+
+            @pl.when((r == 3) & (i > 1))
             def _():
-                r_last(FF, j - 3)
+                r_middle(FF, earlier)
+
+            @pl.when((r == 3) & (i > 0))
+            def _():
+                r_first(FF, before)
 
             return 0
 
@@ -683,9 +703,7 @@
     gather(dproj.at[0])
     res_copy = pltpu.make_async_copy(dproj.at[0], res_hbm, lsem.at[6])
     res_copy.start()
-    r_middle(FF, 2)
-    r_first(FF, 3)
-    r_last(FF, 1)
+    r_first(FF, 1)
 
     def backward_block(i, _):
         j = blocks - 1 - i
@@ -703,6 +721,24 @@
                 second_t[half * rr : (half + 1) * rr, :], st[j, pl.ds(SEGS, rows), :].astype(BF16)
             ).astype(BF16)
         r_start(OUT, j, 0)
+
+        @pl.when(i == 0)
+        def _():
+            r_last(FF, 2)
+            r_middle(FF, 3)
+
+        @pl.when(i == 1)
+        def _():
+            r_last(FF, 0)
+
+        @pl.when(i == 2)
+        def _():
+            r_last(FF, 3)
+            r_middle(FF, 1)
+
+        @pl.when(i == 3)
+        def _():
+            r_middle(OUT, 3)
 
         def one(step, w, q_):
             at = pl.multiple_of(step * SEGS, SEGS)
@@ -735,25 +771,13 @@
             )
         pl.when(t == 3)(b_copy(j).start)
 
-        @pl.when(i == 1)
-        def _():
-            r_last(FF, 2)
-
-        @pl.when(i == 2)
-        def _():
-            r_middle(FF, 3)
-
         @pl.when(i > 0)
         def _():
             r_first(OUT, j + 1)
 
-        @pl.when(i > 1)
-        def _():
-            r_middle(OUT, j + 2)
-
-        @pl.when(i > 2)
-        def _():
-            r_last(OUT, j + 3)
+        @pl.when(i == 3)
+        def _():
+            r_middle(OUT, 2)
 
         return 0
 
@@ -770,7 +794,6 @@
 
     lax.fori_loop(0, blocks, backward_block, 0)
 
-    r_last(FF, 3)
     res_copy.wait()
 
     def backward_fix(i, _):
@@ -817,27 +840,39 @@
             return w, d1, d2, d3, c0, c1, c2, k0, k1, k2, k3, gb
 
         window = [cand[j, pl.ds((steps + 2 - n) * SEGS, SEGS), :] for n in range(3)]
-        out = lax.fori_loop(0, steps // 2, pair, (w, *after, *window, zero, zero, zero, zero, zero))
+        half = lax.fori_loop(0, steps // 4, pair, (w, *after, *window, zero, zero, zero, zero, zero))
+
+        @pl.when(i == 0)
+        def _():
+            r_last(FF, 1)
+            r_first(OUT, 0)
+            r_last(OUT, 3)
+
+        @pl.when(i == 1)
+        def _():
+            r_last(OUT, 2)
+            r_middle(OUT, 0)
+
+        @pl.when(i == 2)
+        def _():
+            r_last(OUT, 0)
+            a_first(FF)
+
+        @pl.when(i == 3)
+        def _():
+            r_middle(IN, 3)
+            a_first(OUT)
+
+        out = lax.fori_loop(steps // 4, steps // 2, pair, half)
         for n in range(5):
             at = 2 + 2 * n + bit_of(s_, 1)
             ssum[0, pl.ds(at, 1), pl.ds(pl.multiple_of(bit_of(s_, 0) * ch, LANES), ch)] = jnp.sum(
                 out[7 + n], axis=0, keepdims=True
             )
 
-        @pl.when(i == 0)
-        def _():
-            r_first(OUT, 0)
-            r_middle(OUT, 1)
-            r_last(OUT, 2)
-
-        @pl.when(i == 1)
-        def _():
-            r_middle(OUT, 0)
-            r_last(OUT, 1)
-
-        @pl.when(i == 2)
-        def _():
-            r_last(OUT, 0)
+        @pl.when(i > 1)
+        def _():
+            r_first(IN, j + 1)
 
         def first_grad(r, _):
             at = pl.multiple_of(r * CHUNK, CHUNK)
@@ -848,26 +883,18 @@
         r_start(IN, j, 0)
 
 
-        @pl.when(i > 0)
-        def _():
-            r_first(IN, j + 1)
-
-        @pl.when(i > 1)
-        def _():
-            r_middle(IN, j + 2)
-
-        @pl.when(i > 2)
-        def _():
-            r_last(IN, j + 3)
-
-        @pl.when(i == 2)
-        def _():
-            a_first(FF)
+        @pl.when(i == 0)
+        def _():
+            r_middle(OUT, 1)
+
+        @pl.when(i == 1)
+        def _():
+            r_first(IN, 3)
+            r_last(OUT, 1)
 
         @pl.when(i == 3)
         def _():
-            a_mid(FF)
-            a_first(OUT)
+            r_middle(IN, 2)
 
         return 0
 
@@ -881,16 +908,16 @@
         bufc[pl.ds(at, CHUNK), :] = v
 
     first_back(0)
-    r_last(IN, 2)
+    r_last(IN, 3)
     first_back(1)
     r_first(IN, 0)
+    first_back(2)
     r_middle(IN, 1)
-    a_end(FF)
-    first_back(2)
-    a_mid(OUT)
+    a_mid(FF)
     first_back(3)
     for r in range(4, nchunk):
         first_back(r)
+    r_last(IN, 2)
 
     def first_norm_back(r, gain):
         at = pl.multiple_of(r * CHUNK, CHUNK)
@@ -905,19 +932,21 @@
 
     ssum[0, pl.ds(0, 1), :] = lax.fori_loop(0, nchunk, first_norm_back, jnp.zeros((1, d), F32))
     s_start(0)
+    r_last(IN, 1)
     r_middle(IN, 0)
-    r_last(IN, 1)
+    a_mid(OUT)
     gather(mid)
     gx_copy = pltpu.make_async_copy(mid, gx_hbm, lsem.at[7])
     gx_copy.start()
-    a_end(OUT)
     s_next(0)
+    a_end(FF)
     r_last(IN, 0)
     a_first(IN)
     for g in range(1, len(groups) - 1):
         s_next(g)
     a_mid(IN)
     a_end(IN)
+    a_end(OUT)
     s_next(len(groups) - 1)
     gains_ref[...] = ssum[len(groups), pl.ds(0, 8), :]
     for n in range(5):
@@ -930,6 +959,7 @@
     a_wait(IN, 0)
 
     gx_copy.wait()
+    pl.when(t == 2)(hcopy.wait_send)
     wait_for(cb.at[pl.ds(0, blocks - 1)], c_s.at[0])
     pl.when(t == 2)(lambda: wait_for(fsend, f_s.at[0]))
     pl.when(t == 3)(lambda: wait_for(bsend, b_s.at[0]))

time: 120 us -> 112 us (0.933)
  Pallas kernels: 116 us -> 108 us
    pallas_call x1, Pallas kernels: 110 us -> 102 us  [per_device(): pl.pallas_call(functools.partial(block_kernel, (rows, d, blocks, ch, ff,...]
where the time goes in v4:
time: 112 us
  Pallas kernels  108 us (96%)
  local copies, waits for them, and re-layouts  1.92 us (2%)
  between operations  1.3 us (1%)
    pallas_call x1, Pallas kernels, per_device(): pl.pallas_call(functools.partial(block_kernel, (rows, d, blocks, ch, ff,...  102 us
    pallas_call x1, Pallas kernels, per_device(): pl.pallas_call(functools.partial(finish_kernel, (rows, d, ch, ff)), out_s...  6.04 us

profile of v4, /device:TPU:0, one launch (start us, length us, event | category | flops | bytes accessed | tf_op | source)
XLA Modules:
  0.0 111.5 jit_solution(690595671284324386)
XLA Ops:
  1.3 1.9 %copy.22 = bf16[64,8,2,256]{3,1,2,0:T(8,128)(2,1)} copy(bf16[64,8,2,256]{3,2,1,0:T(2,128)(2,1)} %bitcast.9) | data formatting | bytes 1048576
  3.2 102.3 %block.1 = (bf16[1024,512]{1,0:T(8,128)(2,1)}, f32[1024,512]{1,0:T(8,128)}, bf16[1792,512]{1,0:T(8,128)(2,1)}, f32[8,512]{1,0:T(8,128)}, f32[8,256]{1,0:T(8,128)}) custom-call(s32[2]{0:T(128)} %short_ref.1, s32[1]{0:T(128)S(6)} %copy.23.long_ref, bf16[1024,512]{1,0:T(8,128)(2,1)} %x_hbm.1, bf16[1024,512]{1,0:T(8,128)(2,1)} %cot_hbm.1, f32[1,512]{1,0:T(1,128)} %bitcast.10, ...), custom_call_target="tpu_custom_call" | custom-call | tf_op jit(solution)/shard_map/block/pallas_call | solution.py:1054
  105.5 6.0 %finish.1 = (bf16[1024,512]{1,0:T(8,128)(2,1)}, f32[1024,512]{1,0:T(8,128)}, f32[512,2,256]{2,1,0:T(2,128)}, f32[256,512]{1,0:T(8,128)}, f32[512,512]{1,0:T(8,12...) custom-call(f32[8,512]{1,0:T(8,128)} %get-tuple-element.25.gains, ...), custom_call_target="tpu_custom_call" | custom-call | tf_op jit(solution)/shard_map/finish/pallas_call | solution.py:1132

commit v5 on v4

--- a/solution.py
+++ b/solution.py
@@ -68,13 +68,14 @@
     wout_hbm,
     wup_hbm,
     wdown_hbm,
-    res_hbm,
-    gx_hbm,
+    res,
+    mid,
     fin,
     gains_ref,
     chan_ref,
     w_all,
     grad,
+    win,
     xp,
     cand,
     upd,
@@ -86,7 +87,6 @@
     dout,
     dout_t,
     bufa,
-    mid,
     bufc,
     dproj,
     perm,
@@ -353,7 +353,7 @@
         return pltpu.make_async_copy(src, dst_, lsem.at[i])
 
     loads = [
-        local(win_hbm, w_all.at[t, pl.ds(o_in, d), :], 0),
+        local(win_hbm, win, 0),
         local(x_hbm, dproj.at[0], 1),
         local(cot_hbm, dproj.at[1], 2),
         local(wout_hbm, w_all.at[t, pl.ds(o_out, ch), :], 3),
@@ -382,9 +382,24 @@
     for j in range(1, blocks):
         c_copy(j).start()
     loads[0].wait()
+
+    piece = span(IN, nb)
+
+    def part(c, start):
+        w_all[t, at_rows(IN, start, piece), lanes[c]] = win[pl.ds(start, piece), c, :]
+
+    for c in range(2):
+        part(c, low_of(IN, c, nb))
     for j in range(1, blocks):
         for copy in w_sources(IN, j):
             copy.start()
+
+    def other_part(i, _):
+        for c in range(2):
+            part(c, lax.rem(low_of(IN, c, nb) + (i + 1) * piece, d))
+        return 0
+
+    lax.fori_loop(0, d // piece - 1, other_part, 0)
     loads[1].wait()
 
     nlane = d // LANES
@@ -580,7 +595,7 @@
 
         lax.fori_loop(0, steps // 8, step8, st[b, pl.ds(0, SEGS), :])
 
-        @pl.when(i == 0)
+        @pl.when(i == 1)
         def _():
             w_end(OUT, 1, 2, 3)
 
@@ -646,11 +661,11 @@
             def _():
                 w_top(FF, 1)
 
-            @pl.when((r == 3) & (i == 0))
+            @pl.when((r == 0) & (i == 1))
             def _():
                 w_end(FF, 3)
 
-            @pl.when((r == 0) & (i == 1))
+            @pl.when((r == 1) & (i == 1))
             def _():
                 w_mid(FF, 1)
 
@@ -700,9 +715,7 @@
     gain2 = lax.fori_loop(0, nchunk, second_back, jnp.zeros((1, d), F32))
     ssum[0] = jnp.zeros((16, d), F32)
     ssum[0, pl.ds(1, 1), :] = gain2
-    gather(dproj.at[0])
-    res_copy = pltpu.make_async_copy(dproj.at[0], res_hbm, lsem.at[6])
-    res_copy.start()
+    gather(res)
     r_first(FF, 1)
 
     def backward_block(i, _):
@@ -775,10 +788,6 @@
         def _():
             r_first(OUT, j + 1)
 
-        @pl.when(i == 3)
-        def _():
-            r_middle(OUT, 2)
-
         return 0
 
     def backward_chain(j, start):
@@ -794,7 +803,6 @@
 
     lax.fori_loop(0, blocks, backward_block, 0)
 
-    res_copy.wait()
 
     def backward_fix(i, _):
         j = blocks - 1 - i
@@ -844,6 +852,7 @@
 
         @pl.when(i == 0)
         def _():
+            r_middle(OUT, 2)
             r_last(FF, 1)
             r_first(OUT, 0)
             r_last(OUT, 3)
@@ -913,7 +922,6 @@
     r_first(IN, 0)
     first_back(2)
     r_middle(IN, 1)
-    a_mid(FF)
     first_back(3)
     for r in range(4, nchunk):
         first_back(r)
@@ -934,14 +942,13 @@
     s_start(0)
     r_last(IN, 1)
     r_middle(IN, 0)
+    a_mid(FF)
     a_mid(OUT)
     gather(mid)
-    gx_copy = pltpu.make_async_copy(mid, gx_hbm, lsem.at[7])
-    gx_copy.start()
     s_next(0)
-    a_end(FF)
     r_last(IN, 0)
     a_first(IN)
+    a_end(FF)
     for g in range(1, len(groups) - 1):
         s_next(g)
     a_mid(IN)
@@ -958,7 +965,6 @@
     a_wait(OUT, 0)
     a_wait(IN, 0)
 
-    gx_copy.wait()
     pl.when(t == 2)(hcopy.wait_send)
     wait_for(cb.at[pl.ds(0, blocks - 1)], c_s.at[0])
     pl.when(t == 2)(lambda: wait_for(fsend, f_s.at[0]))
@@ -976,43 +982,34 @@
         wait_for(sgot.at[g, pl.ds(0, (1 << len(groups[g])) - 1)], s_s.at[g])
 
 
-def finish_kernel(dims, gains, chan, res, gx, fin, res_out, gx_out, gin_o, gout_o, gup_o, gdown_o, gnorm, gmlp, taps, gbias,
-                  rbuf, gbuf, fbuf, gin, gout, gup, gdown, sem):
+def finish_kernel(
+    dims, gains, chan, res, gx, fin, res_out, gx_out, gin_o, gout_o, gup_o, gdown_o, gnorm, gmlp, taps, gbias,
+    gin, gout, gup, gdown, sem,
+):
     rows, d, ch, ff = dims
-    cuts = ((d + ch, ff), (d + ch + ff, ff), (d, ch), (0, d))
-    parts = [pltpu.make_async_copy(fin.at[pl.ds(a, n)], fbuf.at[pl.ds(a, n)], sem.at[i]) for i, (a, n) in enumerate(cuts)]
-    ins = [pltpu.make_async_copy(gx, gbuf, sem.at[4]), pltpu.make_async_copy(res, rbuf, sem.at[5])]
-    for copy in parts + ins:
-        copy.start()
     outs = []
 
     def put(src, dst):
-        copy = pltpu.make_async_copy(src, dst, sem.at[6 + len(outs)])
+        copy = pltpu.make_async_copy(src, dst, sem.at[len(outs)])
         copy.start()
         outs.append(copy)
 
+    put(gx, gx_out)
+    put(res, res_out)
+    gup[...] = fin[pl.ds(d + ch, d), :].astype(F32)
+    put(gup, gup_o)
+    gin[:, 0, :] = fin[pl.ds(0, d), :ch].astype(F32)
+    gin[:, 1, :] = fin[pl.ds(0, d), ch:].astype(F32)
+    put(gin, gin_o)
+    gdown[...] = fin[pl.ds(d + ch + ff, d), :].astype(F32).T
+    put(gdown, gdown_o)
+    gout[:, : d // 2] = fin[pl.ds(d, ch), :ch].astype(F32).T
+    gout[:, d // 2 :] = fin[pl.ds(d, ch), ch:].astype(F32).T
+    put(gout, gout_o)
     gnorm[...] = gains[pl.ds(0, 1), :]
     gmlp[...] = gains[pl.ds(1, 1), :]
     taps[...] = chan[pl.ds(0, 4), :]
     gbias[...] = chan[pl.ds(4, 1), :]
-    parts[0].wait()
-    gup[...] = fbuf[pl.ds(d + ch, d), :].astype(F32)
-    put(gup, gup_o)
-    parts[1].wait()
-    gdown[...] = fbuf[pl.ds(d + ch + ff, d), :].astype(F32).T
-    put(gdown, gdown_o)
-    ins[0].wait()
-    put(gbuf, gx_out)
-    ins[1].wait()
-    put(rbuf, res_out)
-    parts[2].wait()
-    gout[:, : d // 2] = fbuf[pl.ds(d, ch), :ch].astype(F32).T
-    gout[:, d // 2 :] = fbuf[pl.ds(d, ch), ch:].astype(F32).T
-    put(gout, gout_o)
-    parts[3].wait()
-    gin[:, 0, :] = fbuf[pl.ds(0, d), :ch].astype(F32)
-    gin[:, 1, :] = fbuf[pl.ds(0, d), ch:].astype(F32)
-    put(gin, gin_o)
     for copy in outs:
         copy.wait()
 
@@ -1038,7 +1035,7 @@
     dp = lax.axis_size("dp")
     nb = log2(dp)
     assert dp == 1 << nb and blocks == 4 and rows == LSHORT and 2 * rows == LLONG
-    assert short_lengths.shape == (2,) and long_lengths.shape == (1,)
+    assert 2 * ch == d and short_lengths.shape == (2,) and long_lengths.shape == (1,)
     sizes = (d, ch, 2 * ff)
     total = sum(sizes)
     halves = tuple(min(nb, log2(r // TILE)) for r in sizes)
@@ -1054,17 +1051,18 @@
     res, gx, fin, gains, chan = pl.pallas_call(
         functools.partial(block_kernel, (rows, d, blocks, ch, ff, nb)),
         out_shape=(
-            jax.ShapeDtypeStruct((rows, d), BF16),
-            jax.ShapeDtypeStruct((rows, d), F32),
-            jax.ShapeDtypeStruct((total, d), BF16),
-            jax.ShapeDtypeStruct((8, d), F32),
-            jax.ShapeDtypeStruct((8, ch), F32),
+            pltpu.VMEM((rows, d), BF16),
+            pltpu.VMEM((rows, d), F32),
+            pltpu.VMEM((total, d), BF16),
+            pltpu.VMEM((8, d), F32),
+            pltpu.VMEM((8, ch), F32),
         ),
         in_specs=[sm, sm, hb, hb, vm, vm, vm, vm, hb, hb, hb, hb],
-        out_specs=(hb, hb) + (vm,) * 3,
+        out_specs=(vm,) * 5,
         scratch_shapes=[
             pltpu.VMEM((blocks, total, d), BF16),
             pltpu.VMEM((blocks, total, d), BF16),
+            pltpu.VMEM((d, 2, ch), BF16),
             pltpu.VMEM((rows, d), BF16),
             pltpu.VMEM((blocks, rows + 3 * SEGS, ch), F32),
             pltpu.VMEM((blocks, rows, ch), F32),
@@ -1075,7 +1073,6 @@
             pltpu.VMEM((d, rows), BF16),
             pltpu.VMEM((rows, d), BF16),
             pltpu.VMEM((d, rows), BF16),
-            pltpu.VMEM((rows, d), F32),
             pltpu.VMEM((rows, d), F32),
             pltpu.VMEM((rows, d), F32),
             pltpu.VMEM((blocks, rows, d), BF16),
@@ -1091,7 +1088,7 @@
             pltpu.VMEM((blocks, span_all(nb), d), BF16),
             pltpu.VMEM((ngroups + 1, 16, d), F32),
             pltpu.VMEM((ngroups, 3, 16, d), F32),
-            dma((8,)),
+            dma((6,)),
             dma((1,)),
             dma((blocks,)),
             dma((1,)),
@@ -1112,7 +1109,7 @@
         ]
         + [pltpu.VMEM((blocks, span_all(k + 1), d), BF16) for k in range(nb)],
         compiler_params=pltpu.CompilerParams(
-            collective_id=0, has_side_effects=True, vmem_limit_bytes=67043328
+            collective_id=0, has_side_effects=True, vmem_limit_bytes=58 << 20
         ),
         name="block",
     )(
@@ -1124,7 +1121,7 @@
         mlp_gain[None],
         conv_kernel,
         gate_bias[None],
-        in_weight.reshape(d, 2 * ch),
+        in_weight,
         out_weight,
         up_weight,
         down_weight,
@@ -1143,19 +1140,16 @@
             jax.ShapeDtypeStruct((4, ch), F32),
             jax.ShapeDtypeStruct((1, ch), F32),
         ),
-        in_specs=[vm, vm, hb, hb, hb],
+        in_specs=[vm] * 5,
         out_specs=(hb,) * 6 + (vm,) * 4,
         scratch_shapes=[
-            pltpu.VMEM((rows, d), BF16),
-            pltpu.VMEM((rows, d), F32),
-            pltpu.VMEM((total, d), BF16),
             pltpu.VMEM((d, 2, ch), F32),
             pltpu.VMEM((ch, d), F32),
             pltpu.VMEM((d, ff), F32),
             pltpu.VMEM((ff, d), F32),
-            dma((12,)),
+            dma((6,)),
         ],
-        compiler_params=pltpu.CompilerParams(vmem_limit_bytes=67043328),
+        compiler_params=pltpu.CompilerParams(vmem_limit_bytes=32 << 20),
         name="finish",
     )(gains, chan, res, gx, fin)
     return (result, grad_inputs, gnorm[0], gin, taps, gbias[0], gout, gmlp[0], gup, gdown)

time: 112 us -> 105 us (0.938)
  Pallas kernels: 108 us -> 104 us
  local copies, waits for them, and re-layouts: 1.92 us -> 0 us
    pallas_call x1, Pallas kernels: 6.04 us -> 3.47 us  [per_device(): pl.pallas_call(functools.partial(finish_kernel, (rows, d, ch, ff)), out_s...]
    unnamed x1 -> x0, local copies, waits for them, and re-layouts: 1.92 us -> none
    pallas_call x1, Pallas kernels: 102 us -> 100 us  [per_device(): pl.pallas_call(functools.partial(block_kernel, (rows, d, blocks, ch, ff,...]
where the time goes in v5:
time: 105 us
  Pallas kernels  104 us (99%)
  between operations  1.3 us (1%)
    pallas_call x1, Pallas kernels, per_device(): pl.pallas_call(functools.partial(block_kernel, (rows, d, blocks, ch, ff,...  100 us
    pallas_call x1, Pallas kernels, per_device(): pl.pallas_call(functools.partial(finish_kernel, (rows, d, ch, ff)), out_s...  3.47 us

profile of v5, /device:TPU:0, one launch (start us, length us, event | category | flops | bytes accessed | tf_op | source)
XLA Modules:
  0.0 105.2 jit_solution(13331302850529242144)
XLA Ops:
  1.3 100.4 %block.1 = (bf16[1024,512]{1,0:T(8,128)(2,1)S(1)}, f32[1024,512]{1,0:T(8,128)S(1)}, bf16[1792,512]{1,0:T(8,128)(2,1)S(1)}, f32[8,512]{1,0:T(8,128)S(1)}, f32[8,256]{1,0:T(8,128)S(1)}) custom-call(s32[2]{0:T(128)} %short_ref.1, s32[1]{0:T(128)S(6)} %copy.22.long_ref, bf16[1024,512]{1,0:T(8,128)(2,1)} %x_hbm.1, bf16[1024,512]{1,0:T(8,128)(2,1)} %cot_hbm.1, ...), custom_call_target="tpu_custom_call" | custom-call | tf_op jit(solution)/shard_map/block/pallas_call | solution.py:1051
  101.7 3.5 %finish.1 = (bf16[1024,512]{1,0:T(8,128)(2,1)}, f32[1024,512]{1,0:T(8,128)}, f32[512,2,256]{2,1,0:T(2,128)}, f32[256,512]{1,0:T(8,128)}, f32[512,512]{1,0:T(8,12...) custom-call(f32[8,512]{1,0:T(8,128)S(1)} %get-tuple-element.25.gains,, ...), custom_call_target="tpu_custom_call" | custom-call | tf_op jit(solution)/shard_map/finish/pallas_call | solution.py:1129

commit v6 on v5

--- a/solution.py
+++ b/solution.py
@@ -13,6 +13,7 @@
 SEGS = 8
 EPS = 1e-05
 CHUNK = 256
+WIDE = 1024
 TILE = 16
 LANES = 128
 F32 = jnp.float32
@@ -81,7 +82,7 @@
     upd,
     st,
     dst,
-    lhs,
+    edge_rows,
     first_t,
     second_t,
     dout,
@@ -134,7 +135,7 @@
     half_d = d // 2
     lanes = (pl.ds(0, half_d), pl.ds(half_d, half_d))
     orders = ((0,) + tuple(range(nb - 1, 0, -1)), tuple(range(nb)))
-    nstage = len(stage_bufs)
+    lhs = dproj.at[3]
 
     def zflip(j):
         b0, b1 = lax.rem(j, 2), lax.div(j, 2)
@@ -473,24 +474,24 @@
             w_wait(IN, j, 0)
 
         def project(r, _):
-            at = pl.multiple_of(r * CHUNK, CHUNK)
-            v = dot(lhs[pl.ds(at, CHUNK), :], w_all[s_, pl.ds(o_in, d), :])
-            bufa[pl.ds(at, CHUNK), :ch] = v[:, :ch]
-            cand[j, pl.ds(at + 3 * SEGS, CHUNK), :] = v[:, ch:]
-
-            @pl.when((j == 0) & (r == 1))
+            at = pl.multiple_of(r * WIDE, WIDE)
+            v = dot(lhs[pl.ds(at, WIDE), :], w_all[s_, pl.ds(o_in, d), :])
+            bufa[pl.ds(at, WIDE), :ch] = v[:, :ch]
+            cand[j, pl.ds(at + 3 * SEGS, WIDE), :] = v[:, ch:]
+
+            @pl.when((j == 0) & (r == 0))
             def _():
                 w_top(IN, 1)
 
             return 0
 
-        lax.fori_loop(0, nchunk, project, 0)
+        lax.fori_loop(0, rows // WIDE, project, 0)
 
         @pl.when(j == 0)
         def _():
             pl.when(t == 3)(hcopy.wait_recv)
             hv = halo[...].astype(F32)
-            lhs[pl.ds(rows, 16), :] = (hv * scale_of(hv) * g1_ref[...]).astype(BF16)
+            edge_rows[...] = (hv * scale_of(hv) * g1_ref[...]).astype(BF16)
 
         @pl.when(j == 1)
         def _():
@@ -504,7 +505,7 @@
         def _():
             w_top(FF, 2)
 
-        ph = dot(lhs[pl.ds(rows, 16), :], w_all[s_, pl.ds(o_in, d), ch:])
+        ph = dot(edge_rows[...], w_all[s_, pl.ds(o_in, d), ch:])
         for back in range(3):
             last = cand[j, pl.ds((steps + back) * SEGS, SEGS), :]
             rolled = pltpu.roll(last, 1, 0)
@@ -535,6 +536,10 @@
         @pl.when(j == 0)
         def _():
             w_top(IN, 2)
+            loads[3].wait()
+            for i in (2, 3, 1):
+                for copy in w_sources(OUT, i):
+                    copy.start()
 
         s, q_ = lax.fori_loop(steps // 8, steps // 4, step4, half)
         ends[0, j] = s
@@ -545,12 +550,11 @@
         @pl.when(j == 0)
         def _():
             w_mid(IN, 1)
-            for i in range(3, 6):
-                loads[i].wait()
-            for kind in (OUT, FF):
-                for i in (2, 3, 1):
-                    for copy in w_sources(kind, i):
-                        copy.start()
+            loads[4].wait()
+            loads[5].wait()
+            for i in (2, 3, 1):
+                for copy in w_sources(FF, i):
+                    copy.start()
 
         @pl.when(j == 1)
         def _():
@@ -608,21 +612,21 @@
     shards = [zflip(j) for j in range(blocks)]
 
     def second_rows(r, _):
-        at = pl.multiple_of(r * CHUNK, CHUNK)
-        m = xp[pl.ds(at, CHUNK), :].astype(F32)
+        at = pl.multiple_of(r * 512, 512)
+        m = xp[pl.ds(at, 512), :].astype(F32)
         for j in range(blocks):
             m = m + dot(
-                st[j, pl.ds(at + SEGS, CHUNK), :].astype(BF16), w_all[shards[j], pl.ds(o_out, ch), :]
+                st[j, pl.ds(at + SEGS, 512), :].astype(BF16), w_all[shards[j], pl.ds(o_out, ch), :]
             )
-        mid[pl.ds(at, CHUNK), :] = m
+        mid[pl.ds(at, 512), :] = m
         sv = m * scale_of(m) * g2_ref[...]
-        lhs[pl.ds(at, CHUNK), :] = sv.astype(BF16)
-        second_t[:, pl.ds(at, CHUNK)] = sv.T.astype(BF16)
-        bufa[pl.ds(at, CHUNK), :] = m
-        bufc[pl.ds(at, CHUNK), :] = jnp.zeros((CHUNK, d), F32)
+        lhs[pl.ds(at, 512), :] = sv.astype(BF16)
+        second_t[:, pl.ds(at, 512)] = sv.T.astype(BF16)
+        bufa[pl.ds(at, 512), :] = m
+        bufc[pl.ds(at, 512), :] = jnp.zeros((512, d), F32)
         return 0
 
-    lax.fori_loop(0, nchunk, second_rows, 0)
+    lax.fori_loop(0, rows // 512, second_rows, 0)
 
     w_mid(FF, 3)
     act, din = dproj.at[1], dproj.at[2]
@@ -639,25 +643,25 @@
             w_wait(FF, j, 0)
 
         def ff_rows(r, _):
-            at = pl.multiple_of(r * CHUNK, CHUNK)
+            at = pl.multiple_of(r * 512, 512)
             wu = w_all[s_, pl.ds(o_up, ff), :]
             wd = w_all[s_, pl.ds(o_down, ff), :]
-            inner = dot(lhs[pl.ds(at, CHUNK), :], wu)
-            da = dot_t(dout[pl.ds(at, CHUNK), :], wd)
+            inner = dot(lhs[pl.ds(at, 512), :], wu)
+            da = dot_t(dout[pl.ds(at, 512), :], wd)
             cdf = 0.5 + 0.5 * lax.erf(inner * np.float32(np.sqrt(0.5)))
             pdf = jnp.exp(inner * inner * -0.5) * np.float32(1.0 / np.sqrt(2.0 * np.pi))
             av = (inner * cdf).astype(BF16)
             dv = (da * (cdf + inner * pdf)).astype(BF16)
-            act[pl.ds(at, CHUNK), :] = av
-            din[pl.ds(at, CHUNK), :] = dv
-            bufa[pl.ds(at, CHUNK), :] += dot(av, wd)
-            bufc[pl.ds(at, CHUNK), :] += dot_t(dv, wu)
-
-            @pl.when((r == 1) & (i == 0))
+            act[pl.ds(at, 512), :] = av
+            din[pl.ds(at, 512), :] = dv
+            bufa[pl.ds(at, 512), :] += dot(av, wd)
+            bufc[pl.ds(at, 512), :] += dot_t(dv, wu)
+
+            @pl.when((r == 0) & (i == 0))
             def _():
                 w_end(FF, 2)
 
-            @pl.when((r == 2) & (i == 0))
+            @pl.when((r == 1) & (i == 0))
             def _():
                 w_top(FF, 1)
 
@@ -665,33 +669,33 @@
             def _():
                 w_end(FF, 3)
 
-            @pl.when((r == 1) & (i == 1))
+            @pl.when((r == 0) & (i == 1))
             def _():
                 w_mid(FF, 1)
 
-            @pl.when((r == 1) & (i == 2))
+            @pl.when((r == 0) & (i == 2))
             def _():
                 w_end(FF, 1)
 
-            @pl.when((r == 3) & (i > 1))
-            def _():
-                r_middle(FF, earlier)
-
-            @pl.when((r == 3) & (i > 0))
+            @pl.when((r == 1) & (i > 0))
             def _():
                 r_first(FF, before)
 
             return 0
 
-        lax.fori_loop(0, nchunk, ff_rows, 0)
+        lax.fori_loop(0, rows // 512, ff_rows, 0)
 
         def ff_grads(r, _):
-            at = pl.multiple_of(r * CHUNK, CHUNK)
-            grad[s_, pl.ds(o_up + at, CHUNK), :] = dot(second_t[pl.ds(at, CHUNK), :], din[...]).astype(BF16)
-            grad[s_, pl.ds(o_down + at, CHUNK), :] = dot(dout_t[pl.ds(at, CHUNK), :], act[...]).astype(BF16)
+            at = pl.multiple_of(r * 512, 512)
+            grad[s_, pl.ds(o_up + at, 512), :] = dot(second_t[pl.ds(at, 512), :], din[...]).astype(BF16)
+            grad[s_, pl.ds(o_down + at, 512), :] = dot(dout_t[pl.ds(at, 512), :], act[...]).astype(BF16)
             return 0
 
-        lax.fori_loop(0, d // CHUNK, ff_grads, 0)
+        lax.fori_loop(0, d // 512, ff_grads, 0)
+        @pl.when(i > 1)
+        def _():
+            r_middle(FF, earlier)
+
         r_start(FF, j, 0)
         return 0
 
@@ -723,15 +727,16 @@
         s_ = zflip(j)
 
         def project(r, _):
-            at = pl.multiple_of(r * CHUNK, CHUNK)
-            dst[j, pl.ds(at, CHUNK), :] = dot_t(lhs[pl.ds(at, CHUNK), :], w_all[s_, pl.ds(o_out, ch), :])
+            at = pl.multiple_of(r * 512, 512)
+            dst[j, pl.ds(at, 512), :] = dot_t(lhs[pl.ds(at, 512), :], w_all[s_, pl.ds(o_out, ch), :])
             return 0
 
-        lax.fori_loop(0, nchunk, project, 0)
+        lax.fori_loop(0, rows // 512, project, 0)
+        state = st[j, pl.ds(SEGS, rows), :].astype(BF16)
         for half in range(2):
             rr = d // 2
             grad[s_, pl.ds(o_out, ch), half * ch : (half + 1) * ch] = dot(
-                second_t[half * rr : (half + 1) * rr, :], st[j, pl.ds(SEGS, rows), :].astype(BF16)
+                second_t[half * rr : (half + 1) * rr, :], state
             ).astype(BF16)
         r_start(OUT, j, 0)
 
@@ -746,11 +751,11 @@
 
         @pl.when(i == 2)
         def _():
+            r_middle(FF, 1)
+
+        @pl.when(i == 3)
+        def _():
             r_last(FF, 3)
-            r_middle(FF, 1)
-
-        @pl.when(i == 3)
-        def _():
             r_middle(OUT, 3)
 
         def one(step, w, q_):
@@ -852,10 +857,9 @@
 
         @pl.when(i == 0)
         def _():
-            r_middle(OUT, 2)
             r_last(FF, 1)
             r_first(OUT, 0)
-            r_last(OUT, 3)
+            r_middle(OUT, 2)
 
         @pl.when(i == 1)
         def _():
@@ -884,16 +888,17 @@
             r_first(IN, j + 1)
 
         def first_grad(r, _):
-            at = pl.multiple_of(r * CHUNK, CHUNK)
-            grad[s_, pl.ds(o_in + at, CHUNK), :] = dot(first_t[pl.ds(at, CHUNK), :], dproj[j]).astype(BF16)
+            at = pl.multiple_of(r * 512, 512)
+            grad[s_, pl.ds(o_in + at, 512), :] = dot(first_t[pl.ds(at, 512), :], dproj[j]).astype(BF16)
             return 0
 
-        lax.fori_loop(0, d // CHUNK, first_grad, 0)
+        lax.fori_loop(0, d // 512, first_grad, 0)
         r_start(IN, j, 0)
 
 
         @pl.when(i == 0)
         def _():
+            r_last(OUT, 3)
             r_middle(OUT, 1)
 
         @pl.when(i == 1)
@@ -910,21 +915,18 @@
     lax.fori_loop(0, blocks, backward_fix, 0)
 
     def first_back(r):
-        at = r * CHUNK
-        v = dot_t(dproj[0, pl.ds(at, CHUNK), :], w_all[shards[0], pl.ds(o_in, d), :])
+        at = r * 512
+        v = dot_t(dproj[0, pl.ds(at, 512), :], w_all[shards[0], pl.ds(o_in, d), :])
         for j in range(1, blocks):
-            v = v + dot_t(dproj[j, pl.ds(at, CHUNK), :], w_all[shards[j], pl.ds(o_in, d), :])
-        bufc[pl.ds(at, CHUNK), :] = v
+            v = v + dot_t(dproj[j, pl.ds(at, 512), :], w_all[shards[j], pl.ds(o_in, d), :])
+        bufc[pl.ds(at, 512), :] = v
 
     first_back(0)
     r_last(IN, 3)
-    first_back(1)
     r_first(IN, 0)
-    first_back(2)
+    for r in range(1, rows // 512):
+        first_back(r)
     r_middle(IN, 1)
-    first_back(3)
-    for r in range(4, nchunk):
-        first_back(r)
     r_last(IN, 2)
 
     def first_norm_back(r, gain):
@@ -940,20 +942,20 @@
 
     ssum[0, pl.ds(0, 1), :] = lax.fori_loop(0, nchunk, first_norm_back, jnp.zeros((1, d), F32))
     s_start(0)
+    r_middle(IN, 0)
     r_last(IN, 1)
-    r_middle(IN, 0)
+    s_next(0)
     a_mid(FF)
     a_mid(OUT)
     gather(mid)
-    s_next(0)
     r_last(IN, 0)
     a_first(IN)
     a_end(FF)
     for g in range(1, len(groups) - 1):
         s_next(g)
     a_mid(IN)
+    a_end(OUT)
     a_end(IN)
-    a_end(OUT)
     s_next(len(groups) - 1)
     gains_ref[...] = ssum[len(groups), pl.ds(0, 8), :]
     for n in range(5):
@@ -1068,7 +1070,7 @@
             pltpu.VMEM((blocks, rows, ch), F32),
             pltpu.VMEM((blocks, rows + SEGS, ch), F32),
             pltpu.VMEM((blocks, rows, ch), F32),
-            pltpu.VMEM((rows + 16, d), BF16),
+            pltpu.VMEM((16, d), BF16),
             pltpu.VMEM((d, rows), BF16),
             pltpu.VMEM((d, rows), BF16),
             pltpu.VMEM((rows, d), BF16),
@@ -1109,7 +1111,7 @@
         ]
         + [pltpu.VMEM((blocks, span_all(k + 1), d), BF16) for k in range(nb)],
         compiler_params=pltpu.CompilerParams(
-            collective_id=0, has_side_effects=True, vmem_limit_bytes=58 << 20
+            collective_id=0, has_side_effects=True, vmem_limit_bytes=59 << 20
         ),
         name="block",
     )(

time: 105 us -> 99.4 us (0.947)
  Pallas kernels: 104 us -> 97.9 us
    pallas_call x1, Pallas kernels: 100 us -> 94.4 us  [per_device(): pl.pallas_call(functools.partial(block_kernel, (rows, d, blocks, ch, ff,...]
where the time goes in v6:
time: 99.4 us; the launch traced here: 99.2 us
  Pallas kernels  97.9 us (98%)
  between operations  1.3 us (1%)
    pallas_call x1, Pallas kernels, per_device(): pl.pallas_call(functools.partial(block_kernel, (rows, d, blocks, ch, ff,...  94.4 us
    pallas_call x1, Pallas kernels, per_device(): pl.pallas_call(functools.partial(finish_kernel, (rows, d, ch, ff)), out_s...  3.47 us

profile of v6, /device:TPU:0, one launch (start us, length us, event | category | flops | bytes accessed | tf_op | source)
XLA Modules:
  0.0 99.2 jit_solution(13100978350677032322)
XLA Ops:
  1.3 94.4 %block.1 = (bf16[1024,512]{1,0:T(8,128)(2,1)S(1)}, f32[1024,512]{1,0:T(8,128)S(1)}, bf16[1792,512]{1,0:T(8,128)(2,1)S(1)}, f32[8,512]{1,0:T(8,128)S(1)}, f32[8,256]{1,0:T(8,128)S(1)}) custom-call(s32[2]{0:T(128)} %short_ref.1, s32[1]{0:T(128)S(6)} %copy.22.long_ref, bf16[1024,512]{1,0:T(8,128)(2,1)} %x_hbm.1, bf16[1024,512]{1,0:T(8,128)(2,1)} %cot_hbm.1, ...), custom_call_target="tpu_custom_call" | custom-call | tf_op jit(solution)/shard_map/block/pallas_call | solution.py:1053
  95.7 3.5 %finish.1 = (bf16[1024,512]{1,0:T(8,128)(2,1)}, f32[1024,512]{1,0:T(8,128)}, f32[512,2,256]{2,1,0:T(2,128)}, f32[256,512]{1,0:T(8,128)}, f32[512,512]{1,0:T(8,12...) custom-call(f32[8,512]{1,0:T(8,128)S(1)} %get-tuple-element.25.gains,, ...), custom_call_target="tpu_custom_call" | custom-call | tf_op jit(solution)/shard_map/finish/pallas_call | solution.py:1131

commit v7 on v6

--- a/solution.py
+++ b/solution.py
@@ -61,10 +61,10 @@
     long_ref,
     x_hbm,
     cot_hbm,
-    g1_ref,
-    g2_ref,
-    conv_ref,
-    bias_ref,
+    g1_hbm,
+    g2_hbm,
+    conv_hbm,
+    bias_hbm,
     win_hbm,
     wout_hbm,
     wup_hbm,
@@ -74,6 +74,8 @@
     fin,
     gains_ref,
     chan_ref,
+    g1_ref,
+    g2_ref,
     w_all,
     grad,
     win,
@@ -242,9 +244,7 @@
             def add(i, _):
                 at = at_rows(kind, low + i * piece, piece)
                 here = pl.ds(pl.multiple_of(base + i * piece, TILE), piece)
-                grad[s, at, lanes[c]] = (
-                    grad[s, at, lanes[c]].astype(F32) + buf[j, here, lanes[c]].astype(F32)
-                ).astype(BF16)
+                grad[s, at, lanes[c]] += buf[j, here, lanes[c]]
                 return 0
 
             lax.fori_loop(0, n // piece, add, 0)
@@ -360,19 +360,30 @@
         local(wout_hbm, w_all.at[t, pl.ds(o_out, ch), :], 3),
         local(wup_hbm, w_all.at[t, pl.ds(o_up, ff), :], 4),
         local(wdown_hbm, w_all.at[t, pl.ds(o_down, ff), :], 5),
+        local(conv_hbm, cb.at[0, pl.ds(0, 4), :], 6),
+        local(bias_hbm, cb.at[0, pl.ds(4, 1), :], 7),
+        local(g1_hbm, g1_ref, 8),
+        local(g2_hbm, g2_ref, 9),
     ]
-    for copy in loads:
-        copy.start()
+    for i in (0, 1, 6, 7, 8, 9, 2, 3, 4, 5):
+        loads[i].start()
     frecv[...] = jnp.zeros_like(frecv)
     brecv[...] = jnp.zeros_like(brecv)
     halo[...] = jnp.zeros_like(halo)
-    cb[0, pl.ds(0, 4), :] = conv_ref[...]
-    cb[0, pl.ds(4, 1), :] = bias_ref[...]
     barrier = pltpu.get_barrier_semaphore()
     for b in range(nb):
         pl.semaphore_signal(barrier, inc=1, device_id={"dp": flip(p, b)}, device_id_type=MESH)
     for j in range(1, blocks):
         pl.semaphore_signal(barrier, inc=1, device_id={"tensor": zflip(j)}, device_id_type=MESH)
+    loads[0].wait()
+
+    piece = span(IN, nb)
+
+    def part(c, start):
+        w_all[t, at_rows(IN, start, piece), lanes[c]] = win[pl.ds(start, piece), c, :]
+
+    for c in range(2):
+        part(c, low_of(IN, c, nb))
     pl.semaphore_wait(barrier, nb + blocks - 1)
 
     def c_copy(j):
@@ -381,19 +392,12 @@
     hcopy = remote(x_hbm.at[pl.ds(rows - 16, 16), :], halo, h_s.at[0], h_r.at[0], tensor=partner)
     pl.when(t == 2)(hcopy.start)
     for j in range(1, blocks):
-        c_copy(j).start()
-    loads[0].wait()
-
-    piece = span(IN, nb)
-
-    def part(c, start):
-        w_all[t, at_rows(IN, start, piece), lanes[c]] = win[pl.ds(start, piece), c, :]
-
-    for c in range(2):
-        part(c, low_of(IN, c, nb))
-    for j in range(1, blocks):
         for copy in w_sources(IN, j):
             copy.start()
+    for i in range(6, 10):
+        loads[i].wait()
+    for j in range(1, blocks):
+        c_copy(j).start()
 
     def other_part(i, _):
         for c in range(2):
@@ -454,6 +458,7 @@
         return 0
 
     lax.fori_loop(0, nchunk, dout_rows, 0)
+    w_top(IN, 1)
     seg_id = lax.broadcasted_iota(jnp.int32, (SEGS, ch), 0)
     has_prev = jnp.where(t == 3, 1.0, 0.0).astype(F32)
     has_next = jnp.where(t == 2, 1.0, 0.0).astype(F32)
@@ -478,10 +483,6 @@
             v = dot(lhs[pl.ds(at, WIDE), :], w_all[s_, pl.ds(o_in, d), :])
             bufa[pl.ds(at, WIDE), :ch] = v[:, :ch]
             cand[j, pl.ds(at + 3 * SEGS, WIDE), :] = v[:, ch:]
-
-            @pl.when((j == 0) & (r == 0))
-            def _():
-                w_top(IN, 1)
 
             return 0
 
@@ -514,10 +515,10 @@
         k_ = [jnp.broadcast_to(cb[j, pl.ds(i, 1), :], (SEGS, ch)) for i in range(4)]
         bias = jnp.broadcast_to(cb[j, pl.ds(4, 1), :], (SEGS, ch))
 
-        def step4(i, carry):
+        def step8(i, carry):
             s, q_ = carry
-            for q in range(4):
-                at = pl.multiple_of((i * 4 + q) * SEGS, SEGS)
+            for q in range(8):
+                at = pl.multiple_of((i * 8 + q) * SEGS, SEGS)
                 u = sigmoid(bufa[pl.ds(at, SEGS), :ch] + bias)
                 f = k_[0] * cand[j, pl.ds(at + 3 * SEGS, SEGS), :]
                 for lag in range(1, 4):
@@ -530,7 +531,7 @@
             return s, q_
 
         half = lax.fori_loop(
-            0, steps // 8, step4, (jnp.zeros((SEGS, ch), F32), jnp.ones((SEGS, ch), F32))
+            0, steps // 16, step8, (jnp.zeros((SEGS, ch), F32), jnp.ones((SEGS, ch), F32))
         )
 
         @pl.when(j == 0)
@@ -541,7 +542,7 @@
                 for copy in w_sources(OUT, i):
                     copy.start()
 
-        s, q_ = lax.fori_loop(steps // 8, steps // 4, step4, half)
+        s, q_ = lax.fori_loop(steps // 16, steps // 8, step8, half)
         ends[0, j] = s
         ends[1, j] = q_
         fsend[j] = jnp.broadcast_to(forward_chain(j, jnp.zeros((1, ch), F32)), (8, ch))
@@ -703,7 +704,6 @@
 
     def second_back(r, gain):
         at = pl.multiple_of(r * CHUNK, CHUNK)
-        put_perm(at, bufa[pl.ds(at, CHUNK), :])
         m = mid[pl.ds(at, CHUNK), :]
         s = scale_of(m)
         dn = bufc[pl.ds(at, CHUNK), :]
@@ -719,7 +719,6 @@
     gain2 = lax.fori_loop(0, nchunk, second_back, jnp.zeros((1, d), F32))
     ssum[0] = jnp.zeros((16, d), F32)
     ssum[0, pl.ds(1, 1), :] = gain2
-    gather(res)
     r_first(FF, 1)
 
     def backward_block(i, _):
@@ -853,7 +852,10 @@
             return w, d1, d2, d3, c0, c1, c2, k0, k1, k2, k3, gb
 
         window = [cand[j, pl.ds((steps + 2 - n) * SEGS, SEGS), :] for n in range(3)]
-        half = lax.fori_loop(0, steps // 4, pair, (w, *after, *window, zero, zero, zero, zero, zero))
+        def quad(n, carry):
+            return pair(2 * n + 1, pair(2 * n, carry))
+
+        half = lax.fori_loop(0, steps // 8, quad, (w, *after, *window, zero, zero, zero, zero, zero))
 
         @pl.when(i == 0)
         def _():
@@ -869,14 +871,13 @@
         @pl.when(i == 2)
         def _():
             r_last(OUT, 0)
-            a_first(FF)
 
         @pl.when(i == 3)
         def _():
             r_middle(IN, 3)
             a_first(OUT)
 
-        out = lax.fori_loop(steps // 4, steps // 2, pair, half)
+        out = lax.fori_loop(steps // 8, steps // 4, quad, half)
         for n in range(5):
             at = 2 + 2 * n + bit_of(s_, 1)
             ssum[0, pl.ds(at, 1), pl.ds(pl.multiple_of(bit_of(s_, 0) * ch, LANES), ch)] = jnp.sum(
@@ -905,6 +906,10 @@
         def _():
             r_first(IN, 3)
             r_last(OUT, 1)
+
+        @pl.when(i == 2)
+        def _():
+            a_first(FF)
 
         @pl.when(i == 3)
         def _():
@@ -927,6 +932,7 @@
     for r in range(1, rows // 512):
         first_back(r)
     r_middle(IN, 1)
+    a_mid(FF)
     r_last(IN, 2)
 
     def first_norm_back(r, gain):
@@ -945,12 +951,14 @@
     r_middle(IN, 0)
     r_last(IN, 1)
     s_next(0)
-    a_mid(FF)
-    a_mid(OUT)
     gather(mid)
     r_last(IN, 0)
     a_first(IN)
+    a_mid(OUT)
     a_end(FF)
+    for r in range(nchunk):
+        put_perm(r * CHUNK, bufa[pl.ds(r * CHUNK, CHUNK), :])
+    gather(res)
     for g in range(1, len(groups) - 1):
         s_next(g)
     a_mid(IN)
@@ -1059,9 +1067,11 @@
             pltpu.VMEM((8, d), F32),
             pltpu.VMEM((8, ch), F32),
         ),
-        in_specs=[sm, sm, hb, hb, vm, vm, vm, vm, hb, hb, hb, hb],
+        in_specs=[sm, sm] + [hb] * 10,
         out_specs=(vm,) * 5,
         scratch_shapes=[
+            pltpu.VMEM((1, d), F32),
+            pltpu.VMEM((1, d), F32),
             pltpu.VMEM((blocks, total, d), BF16),
             pltpu.VMEM((blocks, total, d), BF16),
             pltpu.VMEM((d, 2, ch), BF16),
@@ -1090,7 +1100,7 @@
             pltpu.VMEM((blocks, span_all(nb), d), BF16),
             pltpu.VMEM((ngroups + 1, 16, d), F32),
             pltpu.VMEM((ngroups, 3, 16, d), F32),
-            dma((6,)),
+            dma((10,)),
             dma((1,)),
             dma((blocks,)),
             dma((1,)),

time: 99.4 us -> 98 us (0.986)
  Pallas kernels: 97.9 us -> 96.6 us
    pallas_call x1, Pallas kernels: 94.4 us -> 93.1 us  [per_device(): pl.pallas_call(functools.partial(block_kernel, (rows, d, blocks, ch, ff,...]
where the time goes in v7:
time: 98 us; the launch traced here: 97.9 us
  Pallas kernels  96.6 us (99%)
  between operations  1.3 us (1%)
    pallas_call x1, Pallas kernels, per_device(): pl.pallas_call(functools.partial(block_kernel, (rows, d, blocks, ch, ff,...  93.1 us
    pallas_call x1, Pallas kernels, per_device(): pl.pallas_call(functools.partial(finish_kernel, (rows, d, ch, ff)), out_s...  3.47 us

profile of v7, /device:TPU:0, one launch (start us, length us, event | category | flops | bytes accessed | tf_op | source)
XLA Modules:
  0.0 97.9 jit_solution(15424272117940662089)
XLA Ops:
  1.3 93.1 %block.1 = (bf16[1024,512]{1,0:T(8,128)(2,1)S(1)}, f32[1024,512]{1,0:T(8,128)S(1)}, bf16[1792,512]{1,0:T(8,128)(2,1)S(1)}, f32[8,512]{1,0:T(8,128)S(1)}, f32[8,256]{1,0:T(8,128)S(1)}) custom-call(s32[2]{0:T(128)} %short_ref.1, s32[1]{0:T(128)S(6)} %copy.22.long_ref, bf16[1024,512]{1,0:T(8,128)(2,1)} %x_hbm.1, bf16[1024,512]{1,0:T(8,128)(2,1)} %cot_hbm.1, ...), custom_call_target="tpu_custom_call" | custom-call | tf_op jit(solution)/shard_map/block/pallas_call | solution.py:1061
  94.4 3.5 %finish.1 = (bf16[1024,512]{1,0:T(8,128)(2,1)}, f32[1024,512]{1,0:T(8,128)}, f32[512,2,256]{2,1,0:T(2,128)}, f32[256,512]{1,0:T(8,128)}, f32[512,512]{1,0:T(8,12...) custom-call(f32[8,512]{1,0:T(8,128)S(1)} %get-tuple-element.25.gains,, ...), custom_call_target="tpu_custom_call" | custom-call | tf_op jit(solution)/shard_map/finish/pallas_call | solution.py:1141

commit v8 on v7

--- a/solution.py
+++ b/solution.py
@@ -327,6 +327,15 @@
         a_wait(kind, 1)
         a_start(kind, 0)
 
+    def a_part(kind, rest):
+        n = span(kind, 2)
+        for c in range(2):
+            low = low_of(kind, c, 2)
+            if rest:
+                low = low + (1 - 2 * bit_of(p, orders[c][1])) * n
+            ref = fin.at[at_rows(kind, low, n), lanes[c]]
+            remote(ref, ref, a_s.at[kind, 0], a_r.at[kind, 0], dp=flip(p, orders[c][0])).start()
+
     groups = bit_groups(nb)
 
     def s_start(g):
@@ -391,9 +400,12 @@
 
     hcopy = remote(x_hbm.at[pl.ds(rows - 16, 16), :], halo, h_s.at[0], h_r.at[0], tensor=partner)
     pl.when(t == 2)(hcopy.start)
+    def w_send(kind, j):
+        for copy in w_sources(kind, j):
+            copy.start()
+
     for j in range(1, blocks):
-        for copy in w_sources(IN, j):
-            copy.start()
+        w_send(IN, j)
     for i in range(6, 10):
         loads[i].wait()
     for j in range(1, blocks):
@@ -469,6 +481,9 @@
         @pl.when(j == 1)
         def _():
             w_top(IN, 3)
+            loads[4].wait()
+            loads[5].wait()
+            w_send(FF, 2)
             w_mid(IN, 2)
             w_end(IN, 1)
             w_mid(IN, 3)
@@ -497,6 +512,7 @@
         @pl.when(j == 1)
         def _():
             w_end(IN, 2)
+            w_send(FF, 3)
 
         @pl.when(j == 2)
         def _():
@@ -539,8 +555,7 @@
             w_top(IN, 2)
             loads[3].wait()
             for i in (2, 3, 1):
-                for copy in w_sources(OUT, i):
-                    copy.start()
+                w_send(OUT, i)
 
         s, q_ = lax.fori_loop(steps // 16, steps // 8, step8, half)
         ends[0, j] = s
@@ -551,15 +566,11 @@
         @pl.when(j == 0)
         def _():
             w_mid(IN, 1)
-            loads[4].wait()
-            loads[5].wait()
-            for i in (2, 3, 1):
-                for copy in w_sources(FF, i):
-                    copy.start()
 
         @pl.when(j == 1)
         def _():
             w_top(OUT, 1, 2, 3)
+            w_send(FF, 1)
 
         @pl.when(j == 2)
         def _():
@@ -962,8 +973,10 @@
     for g in range(1, len(groups) - 1):
         s_next(g)
     a_mid(IN)
+    a_part(IN, False)
     a_end(OUT)
-    a_end(IN)
+    a_wait(IN, 1)
+    a_part(IN, True)
     s_next(len(groups) - 1)
     gains_ref[...] = ssum[len(groups), pl.ds(0, 8), :]
     for n in range(5):

time: 98 us -> 97.7 us (level)
  no operation moved by 1% of the time
where the time goes in v8:
time: 97.7 us; the launch traced here: 97.5 us
  Pallas kernels  96.2 us (98%)
  between operations  1.3 us (1%)
    pallas_call x1, Pallas kernels, per_device(): pl.pallas_call(functools.partial(block_kernel, (rows, d, blocks, ch, ff,...  92.7 us
    pallas_call x1, Pallas kernels, per_device(): pl.pallas_call(functools.partial(finish_kernel, (rows, d, ch, ff)), out_s...  3.47 us

profile of v8, /device:TPU:0, one launch (start us, length us, event | category | flops | bytes accessed | tf_op | source)
XLA Modules:
  0.0 97.5 jit_solution(11114172958474643652)
XLA Ops:
  1.3 92.7 %block.1 = (bf16[1024,512]{1,0:T(8,128)(2,1)S(1)}, f32[1024,512]{1,0:T(8,128)S(1)}, bf16[1792,512]{1,0:T(8,128)(2,1)S(1)}, f32[8,512]{1,0:T(8,128)S(1)}, f32[8,256]{1,0:T(8,128)S(1)}) custom-call(s32[2]{0:T(128)} %short_ref.1, s32[1]{0:T(128)S(6)} %copy.22.long_ref, bf16[1024,512]{1,0:T(8,128)(2,1)} %x_hbm.1, bf16[1024,512]{1,0:T(8,128)(2,1)} %cot_hbm.1, ...), custom_call_target="tpu_custom_call" | custom-call | tf_op jit(solution)/shard_map/block/pallas_call | solution.py:1074
  94.0 3.5 %finish.1 = (bf16[1024,512]{1,0:T(8,128)(2,1)}, f32[1024,512]{1,0:T(8,128)}, f32[512,2,256]{2,1,0:T(2,128)}, f32[256,512]{1,0:T(8,128)}, f32[512,512]{1,0:T(8,12...) custom-call(f32[8,512]{1,0:T(8,128)S(1)} %get-tuple-element.25.gains,, ...), custom_call_target="tpu_custom_call" | custom-call | tf_op jit(solution)/shard_map/finish/pallas_call | solution.py:1154
